TPU v7x, 256 devices: a whole 4x4x8 slice. The times are simulated.
256 devices in a mesh: req: 32 (over x, z_hi, core), tp: 8 (over y, z_lo).
Axes of the slice: x: 4, y: 4, z: 8 (z_hi: 4, z_lo: 2; z = z_hi * 2 + z_lo), core: 2. Of those that a mesh axis runs over, the one named last changes fastest.
Arguments:
- queries: bfloat16 [8192, 5120], P('req', 'tp')
- suffix_keys: bfloat16 [8192, 5120], P('req', 'tp')
- suffix_values: bfloat16 [8192, 5120], P('req', 'tp'), may hold values from -6 to 6
- page_cache: bfloat16 [64, 128, 2, 5120], P('req', None, None, 'tp'), may hold values from -6 to 6
- page_table: int32 [2, 32], replicated, may hold values from 0 to 63, as said below
- suffix_lengths: int32 [32, 4], P('req'), may hold values from 1 to 128, 256 in all within a row
- request_group: int32 [32, 4], P('req'), may hold values from 0 to 1
- residual: bfloat16 [8192, 5120], P('req', 'tp'), may hold values from -6 to 6
- out_weight: bfloat16 [5120, 5120], P('tp'), may hold values from -0.3125 to 0.3125
- attn_gate: float32 [5120], P('tp'), may hold values from 0.5 to 2
- mod_shift: float32 [5120], P('tp'), may hold values from -3 to 3
- mod_scale: float32 [5120], P('tp'), may hold values from -0.5 to 1
Outputs:
- stream: bfloat16 [8192, 5120], P('req', 'tp')
- mlp_input: bfloat16 [8192, 5120], P('req', 'tp')
Inputs may be any that keep to these rules, and one draw needn't show every extreme that they name: `page_table`: every slot 0 to 63 appears exactly once; slot s lies on req index s // 2. `suffix_lengths`: the lengths of one req index's requests sum to 256.
All inputs are finite; a program needn't handle non-finite values.
Results may differ from a plain program's by a relative error of at most 0.015.
Values may be sent and summed in bfloat16 or wider, within the bound.
No kernel may reach another device: no remote copies, remote signals or barrier semaphores. Data moves between devices by JAX's collectives and lax.ppermute only.
A program may use at most 128 MiB of HBM per device.

v0:
```python
import functools
import math

import jax
import jax.numpy as jnp
from jax import lax
from jax.experimental import pallas as pl
from jax.experimental.pallas import tpu as pltpu
from jax.sharding import PartitionSpec as P


D = 5120
HS = 128
SPAN = 64
HEADS_DEV = 5
TOK = 256
BIG = -1e30
INV_SQRT = 1.0 / math.sqrt(HS)
EXP2_SCALE = INV_SQRT * math.log2(math.e)


NX, NZ, NC = 4, 4, 2


def rank(x, z, c):
    return ((x % NX) * NZ + z % NZ) * NC + c % NC


def shift(dx, dz, dc):
    return [
        (rank(x, z, c), rank(x + dx, z + dz, c + dc))
        for x in range(NX)
        for z in range(NZ)
        for c in range(NC)
    ]


def token_facts(facts, shape):
    lane = lax.broadcasted_iota(jnp.int32, facts.shape, 1)
    pick = lambda j: jnp.sum(jnp.where(lane == j, facts, 0.0), axis=1, keepdims=True)
    lens = [pick(j).astype(jnp.int32) for j in range(3)]
    groups = [pick(4 + j).astype(jnp.int32) for j in range(4)]
    pos = lax.broadcasted_iota(jnp.int32, shape, 0)
    e0 = lens[0]
    e1 = e0 + lens[1]
    e2 = e1 + lens[2]
    after0, after1, after2 = pos >= e0, pos >= e1, pos >= e2
    request = jnp.where(after2, 3, jnp.where(after1, 2, jnp.where(after0, 1, 0)))
    start = jnp.where(after2, e2, jnp.where(after1, e1, jnp.where(after0, e0, 0)))
    group = jnp.where(
        after2, groups[3], jnp.where(after1, groups[2], jnp.where(after0, groups[1], groups[0]))
    )
    block = jnp.where(pos - start >= SPAN, 1, 0)
    return request, block, group


def features(own, first, page_group_ref, q_ref, feat, kfeat, blocks):
    wide = (TOK, HS)
    facts = q_ref[TOK : TOK + 16, :].astype(jnp.float32)[0:1, :]
    request, block, group = token_facts(facts, wide)
    lane = lax.broadcasted_iota(jnp.int32, wide, 1)
    row = lax.broadcasted_iota(jnp.int32, wide, 0)
    feat[0] = jnp.where(lane == group, 1.0, 0.0).astype(jnp.bfloat16)
    for i in range(blocks):
        low, high = page_group_ref[first + 2 * i], page_group_ref[first + 2 * i + 1]
        hidden = (lane < 2) & (lane != jnp.where(row < 128, low, high))
        kfeat[i] = jnp.where(hidden, BIG, 0.0).astype(jnp.bfloat16)
    if own:
        feat[1] = jnp.where(lane == 2 * request + block, 1.0, 0.0).astype(jnp.bfloat16)
        seen = (request == lane // 2) & (block <= lane % 2)
        kfeat[blocks] = jnp.where((lane < 8) & ~seen, BIG, 0.0).astype(jnp.bfloat16)


def score_pass(query, keys, marks, feat, kfeat, scores, floor):
    best = floor
    for i, (key, mark) in enumerate(zip(keys, marks)):
        left = jnp.concatenate([query, feat[mark]], axis=1)
        right = jnp.concatenate([key, kfeat[i]], axis=1)
        score = lax.dot_general(
            left, right, (((1,), (1,)), ((), ())), preferred_element_type=jnp.float32
        )
        scores[:, i * TOK : (i + 1) * TOK] = score
        here = jnp.maximum(score[:, :HS], score[:, HS:])
        best = here if best is None else jnp.maximum(best, here)
    return jnp.broadcast_to(jnp.max(best, axis=1, keepdims=True), (TOK, HS))


def value_pass(values, scores, largest):
    both = jnp.concatenate([largest, largest], axis=1)
    ones = jnp.ones((TOK, HS), jnp.bfloat16)
    total = None
    for i, value in enumerate(values):
        weight = jnp.exp2((scores[:, i * TOK : (i + 1) * TOK] - both) * EXP2_SCALE)
        part = jnp.dot(
            weight.astype(jnp.bfloat16),
            jnp.concatenate([value, ones], axis=1),
            preferred_element_type=jnp.float32,
        )
        total = part if total is None else total + part
    return total[:, :HS], total[:, HS:]


def near_kernel(own, page_group_ref, q_ref, *refs):
    kv_refs, refs = refs[:6], refs[6:]
    suffix, refs = (refs[:2], refs[2:]) if own else ((), refs)
    num_ref, top_ref, sum_ref, feat, kfeat, scores = refs

    @pl.when(pl.program_id(0) == 0)
    def _():
        features(own, 0, page_group_ref, q_ref, feat, kfeat, 6)

    @pl.when(page_group_ref[0] >= 0)
    def _():
        keys = [jnp.concatenate([r[0:128, :], r[256:384, :]], axis=0) for r in kv_refs]
        keys = keys + [r[...] for r in suffix[:1]]
        marks = [0] * 6 + [1]
        top_ref[...] = score_pass(q_ref[0:TOK, :], keys, marks, feat, kfeat, scores, None)

    @pl.when(page_group_ref[1] >= 0)
    def _():
        values = [jnp.concatenate([r[128:256, :], r[384:512, :]], axis=0) for r in kv_refs]
        values = values + [r[...] for r in suffix[1:]]
        num_ref[...], sum_ref[...] = value_pass(values, scores, top_ref[...])


def near(own, page_group, query, blocks, suffix=()):
    count = 7 if own else 6
    q_spec = pl.BlockSpec((TOK + 16, HS), lambda h, *_: (0, h))
    s_spec = pl.BlockSpec((TOK, HS), lambda h, *_: (0, h))
    kv_spec = pl.BlockSpec((2 * TOK, HS), lambda h, *_: (0, h))
    out = jax.ShapeDtypeStruct((TOK, HEADS_DEV * HS), jnp.float32)
    return pl.pallas_call(
        functools.partial(near_kernel, own),
        name="near_own" if own else "near",
        out_shape=(out, out, out),
        grid_spec=pltpu.PrefetchScalarGridSpec(
            num_scalar_prefetch=1,
            grid=(HEADS_DEV,),
            in_specs=[q_spec]
            + [kv_spec] * 6
            + [s_spec] * len(suffix),
            out_specs=(s_spec, s_spec, s_spec),
            scratch_shapes=[
                pltpu.VMEM((2, TOK, HS), jnp.bfloat16),
                pltpu.VMEM((7, TOK, HS), jnp.bfloat16),
                pltpu.VMEM((TOK, count * TOK), jnp.float32),
            ],
        ),
        compiler_params=pltpu.CompilerParams(vmem_limit_bytes=24 << 20),
        cost_estimate=pl.CostEstimate(
            flops=2 * 2 * TOK * TOK * count * HS * HEADS_DEV,
            bytes_accessed=2 * TOK * HS * HEADS_DEV * (2 * count + 7),
            transcendentals=TOK * TOK * count * HEADS_DEV,
        ),
    )(page_group, query, *blocks, *suffix)


def far_kernel(own, page_group_ref, q_ref, u0, v0, u1, v1, num_in, top_in, sum_in, *refs):
    if own:
        num_ref, ml_ref, feat, kfeat, scores, top, ml = refs
    else:
        num_ref, feat, kfeat, scores, top, ml = refs
    head = pl.program_id(0)
    wide = (TOK, HS)

    @pl.when(head == 0)
    def _():
        features(False, 12, page_group_ref, q_ref, feat, kfeat, 2)
        ml[...] = jnp.zeros_like(ml)

    @pl.when(page_group_ref[0] >= 0)
    def _():
        keys = [jnp.concatenate([a[0:128, :], b[0:128, :]], axis=0) for a, b in ((u0, v0), (u1, v1))]
        top[...] = score_pass(q_ref[0:TOK, :], keys, [0, 0], feat, kfeat, scores, top_in[...])

    @pl.when(page_group_ref[1] >= 0)
    def _():
        largest = top[...]
        values = [
            jnp.concatenate([a[128:256, :], b[128:256, :]], axis=0) for a, b in ((u0, v0), (u1, v1))
        ]
        num, total = value_pass(values, scores, largest)
        keep = jnp.exp2((top_in[...] - largest) * EXP2_SCALE)
        num = num + keep * num_in[...]
        total = total + keep * sum_in[...]
        if own:
            num_ref[...] = num
        else:
            cols = pl.ds(pl.multiple_of(head * HS, HS), HS)
            num_ref[0:TOK, cols] = num.astype(jnp.bfloat16)
        lane = lax.broadcasted_iota(jnp.int32, wide, 1)
        ml[...] = jnp.where(lane == head, largest, jnp.where(lane == head + 8, total, ml[...]))

    @pl.when(head == HEADS_DEV - 1)
    def _():
        rows = ml[...].T[0:16, :]
        if own:
            ml_ref[...] = rows
        else:
            high = rows.astype(jnp.bfloat16)
            rest = rows - high.astype(jnp.float32)
            middle = rest.astype(jnp.bfloat16)
            low = (rest - middle.astype(jnp.float32))[0:8, :]
            low = jnp.concatenate([low[:, 0:HS], low[:, HS:]], axis=0).astype(jnp.bfloat16)
            num_ref[TOK : TOK + 16, :] = jnp.concatenate([high, middle, low], axis=1)


def far(own, page_group, query, blocks, state):
    width = HEADS_DEV * HS
    q_spec = pl.BlockSpec((TOK + 16, HS), lambda h, *_: (0, h))
    s_spec = pl.BlockSpec((TOK, HS), lambda h, *_: (0, h))
    if own:
        out_shape = (
            jax.ShapeDtypeStruct((TOK, width), jnp.float32),
            jax.ShapeDtypeStruct((16, TOK), jnp.float32),
        )
        out_specs = (s_spec, pl.BlockSpec((16, TOK), lambda h, *_: (0, 0)))
    else:
        out_shape = jax.ShapeDtypeStruct((TOK + 16, width), jnp.bfloat16)
        out_specs = pl.BlockSpec((TOK + 16, width), lambda h, *_: (0, 0))
    return pl.pallas_call(
        functools.partial(far_kernel, own),
        name="far_own" if own else "far",
        out_shape=out_shape,
        grid_spec=pltpu.PrefetchScalarGridSpec(
            num_scalar_prefetch=1,
            grid=(HEADS_DEV,),
            in_specs=[q_spec] + [s_spec] * 7,
            out_specs=out_specs,
            scratch_shapes=[
                pltpu.VMEM((2, TOK, HS), jnp.bfloat16),
                pltpu.VMEM((2, TOK, HS), jnp.bfloat16),
                pltpu.VMEM((TOK, 2 * TOK), jnp.float32),
                pltpu.VMEM((TOK, HS), jnp.float32),
                pltpu.VMEM((TOK, HS), jnp.float32),
            ],
        ),
        compiler_params=pltpu.CompilerParams(vmem_limit_bytes=24 << 20),
        cost_estimate=pl.CostEstimate(
            flops=2 * 2 * TOK * TOK * 2 * HS * HEADS_DEV,
            bytes_accessed=2 * TOK * HS * HEADS_DEV * 12,
            transcendentals=TOK * TOK * 2 * HEADS_DEV,
        ),
    )(page_group, query, *blocks, *state)


def project_kernel(n0, s0, n1, n2, n3, w_ref, out_ref, att):
    @pl.when(pl.program_id(0) == 0)
    def _():
        tops, sums = [s0[0:8, :]], [s0[8:16, :]]
        for n in (n1, n2, n3):
            piece = n[TOK : TOK + 16, :].astype(jnp.float32)
            low = jnp.concatenate([piece[0:8, 2 * TOK :], piece[8:16, 2 * TOK :]], axis=1)
            tops.append(piece[0:8, :TOK] + piece[0:8, TOK : 2 * TOK] + low)
            sums.append(piece[8:16, :TOK] + piece[8:16, TOK : 2 * TOK])
        best = jnp.maximum(jnp.maximum(tops[0], tops[1]), jnp.maximum(tops[2], tops[3]))
        parts = [jnp.exp2((t - best) * EXP2_SCALE) for t in tops]
        under = sum(p * s for p, s in zip(parts, sums))
        rows = [p / under for p in parts] + [jnp.zeros((96, TOK), jnp.float32)]
        share = jnp.concatenate(rows, axis=0).T
        for h in range(HEADS_DEV):
            cols = slice(h * HS, (h + 1) * HS)
            merged = sum(
                share[:, 8 * i + h : 8 * i + h + 1] * n[0:TOK, cols].astype(jnp.float32)
                for i, n in enumerate((n0, n1, n2, n3))
            )
            att[:, cols] = merged.astype(jnp.bfloat16)

    width = HEADS_DEV * HS
    done = jnp.dot(att[...], w_ref[...], preferred_element_type=jnp.float32)
    out_ref[0] = done[:, :width].astype(jnp.bfloat16)
    out_ref[1] = done[:, width:].astype(jnp.bfloat16)


def project(num, ml, others, weight):
    width = HEADS_DEV * HS
    whole = lambda shape: pl.BlockSpec(shape, lambda j: (0, 0))
    return pl.pallas_call(
        project_kernel,
        name="project",
        out_shape=jax.ShapeDtypeStruct((8, TOK, width), jnp.bfloat16),
        grid=(4,),
        in_specs=[whole((TOK, width)), whole((16, TOK))]
        + [whole((TOK + 16, width))] * 3
        + [pl.BlockSpec((width, 2 * width), lambda j: (0, j))],
        out_specs=pl.BlockSpec((2, TOK, width), lambda j: (j, 0, 0)),
        scratch_shapes=[pltpu.VMEM((TOK, width), jnp.bfloat16)],
        cost_estimate=pl.CostEstimate(
            flops=2 * TOK * width * D,
            bytes_accessed=2 * (width * D + TOK * D) + 3 * 2 * TOK * width,
            transcendentals=TOK * 20,
        ),
    )(num, ml, *others, weight)


def combine_kernel(parts_ref, residual_ref, gate_ref, combined_ref, sums_ref):
    acc = parts_ref[0].astype(jnp.float32)
    for i in range(1, 8):
        acc = acc + parts_ref[i].astype(jnp.float32)
    combined = residual_ref[...].astype(jnp.float32) + gate_ref[...] * acc
    combined_ref[...] = combined
    first = jnp.sum(combined, axis=1, keepdims=True)
    second = jnp.sum(combined * combined, axis=1, keepdims=True)
    lane = lax.broadcasted_iota(jnp.int32, (HS, HS), 1)
    both = jnp.where(lane == 0, first, jnp.where(lane == 1, second, 0.0))
    rows = both.T[0:8, :]
    for i in range(8):
        sums_ref[i] = rows


def combine(parts, residual, gate):
    width = residual.shape[1]
    return pl.pallas_call(
        combine_kernel,
        name="combine",
        grid=(TOK // HS,),
        in_specs=[
            pl.BlockSpec((8, HS, width), lambda i: (0, i, 0)),
            pl.BlockSpec((HS, width), lambda i: (i, 0)),
            pl.BlockSpec((1, width), lambda i: (0, 0)),
        ],
        out_specs=(
            pl.BlockSpec((HS, width), lambda i: (i, 0)),
            pl.BlockSpec((8, 8, HS), lambda i: (0, 0, i)),
        ),
        out_shape=(
            jax.ShapeDtypeStruct((TOK, width), jnp.float32),
            jax.ShapeDtypeStruct((8, 8, TOK), jnp.float32),
        ),
    )(parts, residual, gate)


def finish_kernel(combined_ref, sums_ref, shift_ref, scale_ref, stream_ref, mlp_ref):
    total = sums_ref[0]
    for i in range(1, 8):
        total = total + sums_ref[i]
    mean = total[0:1, :] / D
    variance = total[1:2, :] / D - mean * mean
    inverse = 1.0 / jnp.sqrt(variance + 1e-6)
    rows = lax.broadcasted_iota(jnp.int32, (HS, TOK), 0)
    both = jnp.where(rows == 0, mean, jnp.where(rows == 1, inverse, 0.0)).T
    combined = combined_ref[...]
    stream_ref[...] = combined.astype(jnp.bfloat16)
    normed = (combined - both[:, 0:1]) * both[:, 1:2]
    mlp_ref[...] = (normed * (1.0 + scale_ref[...]) + shift_ref[...]).astype(jnp.bfloat16)


def finish(combined, sums, mod_shift, mod_scale):
    shape = jax.ShapeDtypeStruct(combined.shape, jnp.bfloat16)
    return pl.pallas_call(finish_kernel, name="finish", out_shape=(shape, shape))(
        combined, sums, mod_shift, mod_scale
    )


def body(
    queries,
    suffix_keys,
    suffix_values,
    page_cache,
    page_table,
    suffix_lengths,
    request_group,
    residual,
    out_weight,
    attn_gate,
    mod_shift,
    mod_scale,
):
    width = queries.shape[1]
    send = lambda array, dx, dz, dc: lax.ppermute(array, "req", shift(dx, dz, dc))

    facts = jnp.concatenate([suffix_lengths, request_group], axis=1).astype(jnp.bfloat16)
    query = jnp.concatenate([queries, jnp.pad(facts, ((0, 15), (0, width - 8)))], axis=0)
    ways = [1, -1, 2]
    their_query = []
    for dz in ways:
        their_query.append(send(query, 0, dz, 0))

    pages = page_cache.transpose(0, 2, 1, 3).reshape(2 * TOK, width)
    left, right = send(pages, 1, 0, 0), send(pages, -1, 0, 0)
    over_left = send(left[:TOK], 1, 0, 0)
    over_right = send(right[TOK:], -1, 0, 0)
    near_blocks = [pages, left, right]
    near_blocks = near_blocks + [send(array, 0, 0, 1) for array in near_blocks]
    far_blocks = [over_left, over_right]
    far_blocks.append(send(over_left, 0, 0, 1))
    far_blocks.append(send(over_right, 0, 0, 1))

    me = lax.axis_index("req")
    x, z, c = me // (NZ * NC), (me // NC) % NZ, me % NC
    owners = jnp.stack(
        [rank(x - dx, z, c + dc) for dc in (0, 1) for dx in (0, 1, -1)]
        + [rank(x + 2, z, c), rank(x + 2, z, c + 1)]
    )
    slots = (2 * owners[:, None] + jnp.arange(2, dtype=jnp.int32)[None, :]).reshape(16)
    page_group = jnp.sum((page_table[1][None, :] == slots[:, None]).astype(jnp.int32), 1)

    suffix = (suffix_keys, suffix_values)
    states, others = [], []
    for q in their_query:
        states.append(near(False, page_group, q, near_blocks))
    for q, state, dz in zip(their_query, states, ways):
        num = far(False, page_group, q, far_blocks, state)
        others.append(send(num, 0, -dz, 0))
    state = near(True, page_group, query, near_blocks, suffix)
    num, ml = far(True, page_group, query, far_blocks, state)
    parts = project(num, ml, others, out_weight)
    parts = lax.all_to_all(parts, "tp", 0, 0, tiled=True)
    combined, sums = combine(parts, residual, attn_gate[None, :])
    sums = lax.all_to_all(sums, "tp", 0, 0, tiled=True)
    return finish(combined, sums, mod_shift[None, :], mod_scale[None, :])


def solution(mesh):
    in_specs = (
        P("req", "tp"),
        P("req", "tp"),
        P("req", "tp"),
        P("req", None, None, "tp"),
        P(),
        P("req", None),
        P("req", None),
        P("req", "tp"),
        P("tp", None),
        P("tp"),
        P("tp"),
        P("tp"),
    )
    out_specs = (P("req", "tp"), P("req", "tp"))

    return jax.shard_map(body, mesh=mesh, in_specs=in_specs, out_specs=out_specs, check_vma=False)
```

profile of v0, /device:TPU:2, one launch (start us, length us, event | category | flops | bytes accessed | tf_op | source)
XLA Modules:
  0.0 157.8 jit_solution(9504748585730844181)
XLA Ops:
  0.6 1.2 copy.16
  1.8 1.6 collective-permute-start
  3.4 0.8 collective-permute-start.2
  4.2 0.7 convert.6
  4.9 0.7 convert.7
  5.5 0.1 fusion.5
  5.6 1.8 %pad_maximum_fusion.q_ref = bf16[272,640]{1,0:T(8,128)(2,1)} fusion(bf16[16,640]{1,0:T(8,128)(2,1)S(1)} %fusion.5, bf16[256,640]{1,0:T(8,128)(2,1)} %param.12), kind=kLoop, calls=%fused_computation | loop fusion | flops 696320 | bytes 696320 | tf_op jit(solution)/shard_map/concatenate | solution.py:373
  7.4 6.9 %collective-permute-start.13 = (bf16[272,640]{1,0:T(8,128)(2,1)}, bf16[272,640]{1,0:T(8,128)(2,1)}, u32[]{:S(2)}, u32[]{:S(2)}) collective-permute-start(bf16[272,640]{1,0:T(8,128)(2,1)} %pad_maximum_fusion.q_ref), channel_id=1, source_target_pairs={{0,32},{8,40},{16,48},{24,56},{32,0},{40,8},{48,16},{56,24},{64,96... | collective-permute-start | bytes 1044488 | tf_op jit(solution)/shard_map/ppermute | solution.py:370
  14.3 0.0 collective-permute-start.6
  14.3 0.1 stack.35
  14.3 4.0 %collective-permute-done.refs_1_ = bf16[512,640]{1,0:T(8,128)(2,1)S(1)} collective-permute-done((bf16[512,640]{1,0:T(8,128)(2,1)S(1)}, bf16[512,640]{1,0:T(8,128)(2,1)S(1)}, u32[]{:S(2)}, u32[]{:S(2)}) %collective-permute-start) | collective-permute-done | bytes 655392 | tf_op jit(solution)/shard_map/ppermute | solution.py:370
  18.4 1.6 collective-permute-start.1
  20.0 0.0 collective-permute-done.2.refs_2_
  20.0 0.6 collective-permute-start.3
  20.6 0.0 collective-permute-start.7
  20.6 2.7 %collective-permute-done.13.q_ref = bf16[272,640]{1,0:T(8,128)(2,1)} collective-permute-done((bf16[272,640]{1,0:T(8,128)(2,1)}, bf16[272,640]{1,0:T(8,128)(2,1)}, u32[]{:S(2)}, u32[]{:S(2)}) %collective-permute-start.13) | collective-permute-done | bytes 348192 | tf_op jit(solution)/shard_map/ppermute | solution.py:370
  23.3 0.0 collective-permute-start.8
  23.3 0.1 iota_add_fusion
  23.4 0.0 collective-permute-done.6.refs_3_
  23.4 11.0 %collective-permute-start.11 = (bf16[272,640]{1,0:T(8,128)(2,1)}, bf16[272,640]{1,0:T(8,128)(2,1)}, u32[]{:S(2)}, u32[]{:S(2)}) collective-permute-start(bf16[272,640]{1,0:T(8,128)(2,1)} %pad_maximum_fusion.q_ref), channel_id=1, source_target_pairs={{0,48},{8,56},{16,0},{24,8},{32,16},{40,24},{48,32},{56,40},{64,11... | collective-permute-start | bytes 1044488 | tf_op jit(solution)/shard_map/ppermute | solution.py:370
  34.4 0.0 collective-permute-done.1.u0
  34.4 0.2 collective-permute-start.4
  34.6 0.3 collective-permute-start.5
  34.9 0.1 add.147
  35.0 0.0 collective-permute-done.7.refs_4_
  35.0 0.1 collective-permute-start.9
  35.1 0.2 convert_reduce_fusion.page_group_ref
  35.2 0.0 collective-permute-done.8.refs_5_
  35.2 6.8 %near.5 = (f32[256,640]{1,0:T(8,128)S(1)}, f32[256,640]{1,0:T(8,128)S(1)}, f32[256,640]{1,0:T(8,128)S(1)}) custom-call(s32[16]{0:T(128)S(1)} %convert_reduce_fusion.page_group_ref, bf16[272,640]{1,0:T(8,128)(2,1)} %collective-permute-done.13.q_ref, bf16[512,640]{1,0:T(8,128)(2,1)S(1)} %bitcast.15, bf16[512,640]{1,0:T(8,128)(2,1)S(1)} %collective-permute-done.refs_1_, ...), custom_call_target="tpu_custom_call" | custom-call | flops 1006632960 | bytes 6225920 | tf_op jit(solution)/shard_map/near/pallas_call | solution.py:132
  42.0 0.0 collective-permute-done.4.u1
  42.0 0.0 collective-permute-done.5.v1
  42.0 5.5 %far.5 = bf16[272,640]{1,0:T(8,128)(2,1)S(1)} custom-call(s32[16]{0:T(128)S(1)} %convert_reduce_fusion.page_group_ref, bf16[272,640]{1,0:T(8,128)(2,1)} %collective-permute-done.13.q_ref, bf16[256,640]{1,0:T(8,128)(2,1)} %collective-permute-done.1.u0, bf16[256,640]{1,0:T(8,128)(2,1)} %collective-permute-done.3.v0, ...), custom_call_target="tpu_custom_call" | custom-call | flops 335544320 | bytes 3932160 | tf_op jit(solution)/shard_map/far/pallas_call | solution.py:221
  47.6 3.4 %collective-permute-start.14 = (bf16[272,640]{1,0:T(8,128)(2,1)S(1)}, bf16[272,640]{1,0:T(8,128)(2,1)S(1)}, u32[]{:S(2)}, u32[]{:S(2)}) collective-permute-start(bf16[272,640]{1,0:T(8,128)(2,1)S(1)} %far.5), channel_id=1, source_target_pairs={{0,32},{8,40},{16,48},{24,56},{32,0},{40,8},{48,16},{56,24},{64,96... | collective-permute-start | bytes 1044488 | tf_op jit(solution)/shard_map/ppermute | solution.py:370
  51.0 0.0 collective-permute-done.11.q_ref
  51.0 6.8 %near.4 = (f32[256,640]{1,0:T(8,128)S(1)}, f32[256,640]{1,0:T(8,128)S(1)}, f32[256,640]{1,0:T(8,128)S(1)}) custom-call(s32[16]{0:T(128)S(1)} %convert_reduce_fusion.page_group_ref, bf16[272,640]{1,0:T(8,128)(2,1)} %collective-permute-done.11.q_ref, bf16[512,640]{1,0:T(8,128)(2,1)S(1)} %bitcast.16, bf16[512,640]{1,0:T(8,128)(2,1)S(1)} %collective-permute-done.refs_1_, ...), custom_call_target="tpu_custom_call" | custom-call | flops 1006632960 | bytes 6225920 | tf_op jit(solution)/shard_map/near/pallas_call | solution.py:132
  57.7 5.6 %far.4 = bf16[272,640]{1,0:T(8,128)(2,1)S(1)} custom-call(s32[16]{0:T(128)S(1)} %convert_reduce_fusion.page_group_ref, bf16[272,640]{1,0:T(8,128)(2,1)} %collective-permute-done.11.q_ref, bf16[256,640]{1,0:T(8,128)(2,1)} %collective-permute-done.1.u0, bf16[256,640]{1,0:T(8,128)(2,1)} %collective-permute-done.3.v0, ...), custom_call_target="tpu_custom_call" | custom-call | flops 335544320 | bytes 3932160 | tf_op jit(solution)/shard_map/far/pallas_call | solution.py:221
  63.3 3.5 %collective-permute-start.12 = (bf16[272,640]{1,0:T(8,128)(2,1)S(1)}, bf16[272,640]{1,0:T(8,128)(2,1)S(1)}, u32[]{:S(2)}, u32[]{:S(2)}) collective-permute-start(bf16[272,640]{1,0:T(8,128)(2,1)S(1)} %far.4), channel_id=1, source_target_pairs={{0,16},{8,24},{16,32},{24,40},{32,48},{40,56},{48,0},{56,8},{64,80... | collective-permute-start | bytes 1044488 | tf_op jit(solution)/shard_map/ppermute | solution.py:370
  66.8 0.0 collective-permute-done.9.q_ref
  66.8 6.8 %near.3 = (f32[256,640]{1,0:T(8,128)S(1)}, f32[256,640]{1,0:T(8,128)S(1)}, f32[256,640]{1,0:T(8,128)S(1)}) custom-call(s32[16]{0:T(128)S(1)} %convert_reduce_fusion.page_group_ref, bf16[272,640]{1,0:T(8,128)(2,1)S(1)} %collective-permute-done.9.q_ref, bf16[512,640]{1,0:T(8,128)(2,1)S(1)} %bitcast.17, bf16[512,640]{1,0:T(8,128)(2,1)S(1)} %collective-permute-done.refs_1_, ...), custom_call_target="tpu_custom_call" | custom-call | flops 1006632960 | bytes 6225920 | tf_op jit(solution)/shard_map/near/pallas_call | solution.py:132
  73.6 0.0 copy-start.1
  73.6 0.0 copy-start.2
  73.6 5.5 %far.3 = bf16[272,640]{1,0:T(8,128)(2,1)S(1)} custom-call(s32[16]{0:T(128)S(1)} %convert_reduce_fusion.page_group_ref, bf16[272,640]{1,0:T(8,128)(2,1)S(1)} %collective-permute-done.9.q_ref, bf16[256,640]{1,0:T(8,128)(2,1)} %collective-permute-done.1.u0, bf16[256,640]{1,0:T(8,128)(2,1)} %collective-permute-done.3.v0, ...), custom_call_target="tpu_custom_call" | custom-call | flops 335544320 | bytes 3932160 | tf_op jit(solution)/shard_map/far/pallas_call | solution.py:221
  79.1 1.0 collective-permute-start.10
  80.1 7.3 %near_own.1 = (f32[256,640]{1,0:T(8,128)S(1)}, f32[256,640]{1,0:T(8,128)S(1)}, f32[256,640]{1,0:T(8,128)S(1)}) custom-call(s32[16]{0:T(128)S(1)} %convert_reduce_fusion.page_group_ref, bf16[272,640]{1,0:T(8,128)(2,1)} %pad_maximum_fusion.q_ref, bf16[512,640]{1,0:T(8,128)(2,1)S(1)} %bitcast.18, bf16[512,640]{1,0:T(8,128)(2,1)S(1)} %collective-permute-done.refs_1_, ...), custom_call_target="tpu_custom_call" | custom-call | flops 1174405120 | bytes 6881280 | tf_op jit(solution)/shard_map/near_own/pallas_call | solution.py:132
  87.4 5.6 %far_own.1 = (f32[256,640]{1,0:T(8,128)S(1)}, f32[16,256]{1,0:T(8,128)S(1)}) custom-call(s32[16]{0:T(128)S(1)} %convert_reduce_fusion.page_group_ref, bf16[272,640]{1,0:T(8,128)(2,1)} %pad_maximum_fusion.q_ref, bf16[256,640]{1,0:T(8,128)(2,1)} %collective-permute-done.1.u0, bf16[256,640]{1,0:T(8,128)(2,1)} %collective-permute-done.3.v0, ...), custom_call_target="tpu_custom_call" | custom-call | flops 335544320 | bytes 3932160 | tf_op jit(solution)/shard_map/far_own/pallas_call | solution.py:221
  93.0 0.9 copy-done
  93.9 0.6 copy-done.3
  94.5 0.8 collective-permute-done.10.n1
  95.3 0.1 copy-done.6
  95.4 0.6 copy-done.7
  96.0 7.5 %project.1 = bf16[8,256,640]{2,1,0:T(8,128)(2,1)} custom-call(f32[256,640]{1,0:T(8,128)} %copy-done, f32[16,256]{1,0:T(8,128)} %copy-done.3, bf16[272,640]{1,0:T(8,128)(2,1)} %copy-done.7, bf16[272,640]{1,0:T(8,128)(2,1)} %copy-done.6, bf16[272,640]{1,0:T(8,128)(2,1)} %copy-done.5, bf16[640,5120]{1,0:T(8,128)(2,1)} %w_ref.1), custom_call_target="tpu_custom_call" | custom-call | flops 1677721600 | bytes 10158080 | tf_op jit(solution)/shard_map/project/pallas_call | solution.py:278
  103.6 5.6 %all-to-all-start = ((bf16[8,256,640]{2,1,0:T(8,128)(2,1)}), bf16[8,256,640]{2,1,0:T(8,128)(2,1)S(1)}, u32[]{:S(2)}, u32[]{:S(2)}) async-start(bf16[8,256,640]{2,1,0:T(8,128)(2,1)} %project.1), calls=%async_computation | async-start | bytes 5242880 | tf_op jit(solution)/shard_map/all_to_all | solution.py:408
  109.2 0.0 copy-start.10
  109.2 0.0 copy-start.11
  109.2 0.6 broadcast_in_dim.11.gate_ref
  109.8 31.3 %all-to-all-done.parts_ref = bf16[8,256,640]{2,1,0:T(8,128)(2,1)S(1)} async-done(((bf16[8,256,640]{2,1,0:T(8,128)(2,1)}), bf16[8,256,640]{2,1,0:T(8,128)(2,1)S(1)}, u32[]{:S(2)}, u32[]{:S(2)}) %all-to-all-start) | async-done | bytes 2621472 | tf_op jit(solution)/shard_map/all_to_all | solution.py:408
  141.1 1.5 copy-done.4
  142.6 2.7 %combine.1 = (f32[256,640]{1,0:T(8,128)}, f32[8,8,256]{2,1,0:T(8,128)}) custom-call(bf16[8,256,640]{2,1,0:T(8,128)(2,1)} %copy-done.4, bf16[256,640]{1,0:T(8,128)(2,1)} %residual_ref.1, f32[1,640]{1,0:T(1,128)} %broadcast_in_dim.11.gate_ref), custom_call_target="tpu_custom_call" | custom-call | tf_op jit(solution)/shard_map/combine/pallas_call | solution.py:313
  145.3 3.4 %all-to-all-start.1 = ((f32[8,8,256]{2,1,0:T(8,128)}), f32[8,8,256]{2,1,0:T(8,128)S(1)}, u32[]{:S(2)}, u32[]{:S(2)}) async-start(f32[8,8,256]{2,1,0:T(8,128)} %get-tuple-element.33), calls=%async_computation.1 | async-start | bytes 131072 | tf_op jit(solution)/shard_map/all_to_all | solution.py:410
  148.7 0.6 broadcast_in_dim.12.shift_ref
  149.3 0.6 broadcast_in_dim.13.scale_ref
  149.8 5.1 %all-to-all-done.1.sums_ref = f32[8,8,256]{2,1,0:T(8,128)S(1)} async-done(((f32[8,8,256]{2,1,0:T(8,128)}), f32[8,8,256]{2,1,0:T(8,128)S(1)}, u32[]{:S(2)}, u32[]{:S(2)}) %all-to-all-start.1) | async-done | bytes 65568 | tf_op jit(solution)/shard_map/all_to_all | solution.py:410
  154.9 0.6 copy-done.8
  155.6 2.2 %finish.1 = (bf16[256,640]{1,0:T(8,128)(2,1)}, bf16[256,640]{1,0:T(8,128)(2,1)}) custom-call(f32[256,640]{1,0:T(8,128)} %get-tuple-element.32.combined_ref, f32[8,8,256]{2,1,0:T(8,128)} %copy-done.8, f32[1,640]{1,0:T(1,128)} %broadcast_in_dim.12.shift_ref, f32[1,640]{1,0:T(1,128)} %broadcast_in_dim.13.scale_ref), custom_call_target="tpu_custom_call" | custom-call | tf_op jit(solution)/shard_map/finish/pallas_call | solution.py:350
  (23 shorter events, 0.1 us)
Async XLA Ops:
  0.6 34.3 %copy-start.12 = (s32[2,32]{1,0:T(2,128)S(1)}, s32[2,32]{1,0:T(2,128)}, u32[]{:S(2)}) copy-start(s32[2,32]{1,0:T(2,128)} %param.16) | copy-start | bytes 772
  1.8 16.6 %collective-permute-start = (bf16[512,640]{1,0:T(8,128)(2,1)S(1)}, bf16[512,640]{1,0:T(8,128)(2,1)S(1)}, u32[]{:S(2)}, u32[]{:S(2)}) collective-permute-start(bf16[512,640]{1,0:T(8,128)(2,1)S(1)} %bitcast.12), channel_id=1, source_target_pairs={{0,64},{8,72},{16,80},{24,88},{32,96},{40,104},{48,112},{56,120},{... | collective-permute-start | bytes 1966088 | tf_op jit(solution)/shard_map/ppermute | solution.py:370
  3.4 16.6 %collective-permute-start.2 = (bf16[512,640]{1,0:T(8,128)(2,1)S(1)}, bf16[512,640]{1,0:T(8,128)(2,1)S(1)}, u32[]{:S(2)}, u32[]{:S(2)}) collective-permute-start(bf16[512,640]{1,0:T(8,128)(2,1)S(1)} %bitcast.13), channel_id=1, source_target_pairs={{0,192},{8,200},{16,208},{24,216},{32,224},{40,232},{48,240},{56,2... | collective-permute-start | bytes 1966088 | tf_op jit(solution)/shard_map/ppermute | solution.py:370
  7.4 15.9 %collective-permute-start.13 = (bf16[272,640]{1,0:T(8,128)(2,1)}, bf16[272,640]{1,0:T(8,128)(2,1)}, u32[]{:S(2)}, u32[]{:S(2)}) collective-permute-start(bf16[272,640]{1,0:T(8,128)(2,1)} %pad_maximum_fusion.q_ref), channel_id=1, source_target_pairs={{0,32},{8,40},{16,48},{24,56},{32,0},{40,8},{48,16},{56,24},{64,96... | collective-permute-start | bytes 1044488 | tf_op jit(solution)/shard_map/ppermute | solution.py:370
  14.3 9.1 %collective-permute-start.6 = (bf16[512,640]{1,0:T(8,128)(2,1)S(1)}, bf16[512,640]{1,0:T(8,128)(2,1)S(1)}, u32[]{:S(2)}, u32[]{:S(2)}) collective-permute-start(bf16[512,640]{1,0:T(8,128)(2,1)S(1)} %bitcast.14), channel_id=1, source_target_pairs={{0,8},{8,0},{16,24},{24,16},{32,40},{40,32},{48,56},{56,48},{64,72... | collective-permute-start | bytes 1966088 | tf_op jit(solution)/shard_map/ppermute | solution.py:370
  18.4 16.0 %collective-permute-start.1 = (bf16[256,640]{1,0:T(8,128)(2,1)S(1)}, bf16[256,640]{1,0:T(8,128)(2,1)}, u32[]{:S(2)}, u32[]{:S(2)}) collective-permute-start(bf16[256,640]{1,0:T(8,128)(2,1)S(1)} %slice.12), channel_id=1, source_target_pairs={{0,64},{8,72},{16,80},{24,88},{32,96},{40,104},{48,112},{56,120},{... | collective-permute-start | bytes 983048 | tf_op jit(solution)/shard_map/ppermute | solution.py:370
  20.0 14.6 %collective-permute-start.3 = (bf16[256,640]{1,0:T(8,128)(2,1)S(1)}, bf16[256,640]{1,0:T(8,128)(2,1)}, u32[]{:S(2)}, u32[]{:S(2)}) collective-permute-start(bf16[256,640]{1,0:T(8,128)(2,1)S(1)} %slice.13), channel_id=1, source_target_pairs={{0,192},{8,200},{16,208},{24,216},{32,224},{40,232},{48,240},{56,2... | collective-permute-start | bytes 983048 | tf_op jit(solution)/shard_map/ppermute | solution.py:370
  20.6 14.4 %collective-permute-start.7 = (bf16[512,640]{1,0:T(8,128)(2,1)S(1)}, bf16[512,640]{1,0:T(8,128)(2,1)S(1)}, u32[]{:S(2)}, u32[]{:S(2)}) collective-permute-start(bf16[512,640]{1,0:T(8,128)(2,1)S(1)} %collective-permute-done.refs_1_), channel_id=1, source_target_pairs={{0,8},{8,0},{16,24},{24,16},{32,40},{40,32},{48,56},{56,48},{64,72... | collective-permute-start | bytes 1966088 | tf_op jit(solution)/shard_map/ppermute | solution.py:370
  23.3 12.0 %collective-permute-start.8 = (bf16[512,640]{1,0:T(8,128)(2,1)S(1)}, bf16[512,640]{1,0:T(8,128)(2,1)}, u32[]{:S(2)}, u32[]{:S(2)}) collective-permute-start(bf16[512,640]{1,0:T(8,128)(2,1)S(1)} %collective-permute-done.2.refs_2_), channel_id=1, source_target_pairs={{0,8},{8,0},{16,24},{24,16},{32,40},{40,32},{48,56},{56,48},{64,72... | collective-permute-start | bytes 1966088 | tf_op jit(solution)/shard_map/ppermute | solution.py:370
  23.4 27.6 %collective-permute-start.11 = (bf16[272,640]{1,0:T(8,128)(2,1)}, bf16[272,640]{1,0:T(8,128)(2,1)}, u32[]{:S(2)}, u32[]{:S(2)}) collective-permute-start(bf16[272,640]{1,0:T(8,128)(2,1)} %pad_maximum_fusion.q_ref), channel_id=1, source_target_pairs={{0,48},{8,56},{16,0},{24,8},{32,16},{40,24},{48,32},{56,40},{64,11... | collective-permute-start | bytes 1044488 | tf_op jit(solution)/shard_map/ppermute | solution.py:370
  34.4 7.7 %collective-permute-start.4 = (bf16[256,640]{1,0:T(8,128)(2,1)}, bf16[256,640]{1,0:T(8,128)(2,1)}, u32[]{:S(2)}, u32[]{:S(2)}) collective-permute-start(bf16[256,640]{1,0:T(8,128)(2,1)} %collective-permute-done.1.u0), channel_id=1, source_target_pairs={{0,8},{8,0},{16,24},{24,16},{32,40},{40,32},{48,56},{56,48},{64,72... | collective-permute-start | bytes 983048 | tf_op jit(solution)/shard_map/ppermute | solution.py:370
  34.6 7.4 %collective-permute-start.5 = (bf16[256,640]{1,0:T(8,128)(2,1)}, bf16[256,640]{1,0:T(8,128)(2,1)}, u32[]{:S(2)}, u32[]{:S(2)}) collective-permute-start(bf16[256,640]{1,0:T(8,128)(2,1)} %collective-permute-done.3.v0), channel_id=1, source_target_pairs={{0,8},{8,0},{16,24},{24,16},{32,40},{40,32},{48,56},{56,48},{64,72... | collective-permute-start | bytes 983048 | tf_op jit(solution)/shard_map/ppermute | solution.py:370
  35.0 31.8 %collective-permute-start.9 = (bf16[272,640]{1,0:T(8,128)(2,1)}, bf16[272,640]{1,0:T(8,128)(2,1)S(1)}, u32[]{:S(2)}, u32[]{:S(2)}) collective-permute-start(bf16[272,640]{1,0:T(8,128)(2,1)} %pad_maximum_fusion.q_ref), channel_id=1, source_target_pairs={{0,16},{8,24},{16,32},{24,40},{32,48},{40,56},{48,0},{56,8},{64,80... | collective-permute-start | bytes 1044488 | tf_op jit(solution)/shard_map/ppermute | solution.py:370
  47.6 46.9 %collective-permute-start.14 = (bf16[272,640]{1,0:T(8,128)(2,1)S(1)}, bf16[272,640]{1,0:T(8,128)(2,1)S(1)}, u32[]{:S(2)}, u32[]{:S(2)}) collective-permute-start(bf16[272,640]{1,0:T(8,128)(2,1)S(1)} %far.5), channel_id=1, source_target_pairs={{0,32},{8,40},{16,48},{24,56},{32,0},{40,8},{48,16},{56,24},{64,96... | collective-permute-start | bytes 1044488 | tf_op jit(solution)/shard_map/ppermute | solution.py:370
  63.3 31.2 %collective-permute-start.12 = (bf16[272,640]{1,0:T(8,128)(2,1)S(1)}, bf16[272,640]{1,0:T(8,128)(2,1)S(1)}, u32[]{:S(2)}, u32[]{:S(2)}) collective-permute-start(bf16[272,640]{1,0:T(8,128)(2,1)S(1)} %far.4), channel_id=1, source_target_pairs={{0,16},{8,24},{16,32},{24,40},{32,48},{40,56},{48,0},{56,8},{64,80... | collective-permute-start | bytes 1044488 | tf_op jit(solution)/shard_map/ppermute | solution.py:370
  73.6 6.5 %copy-start.1 = (bf16[256,640]{1,0:T(8,128)(2,1)S(1)}, bf16[256,640]{1,0:T(8,128)(2,1)}, u32[]{:S(2)}) copy-start(bf16[256,640]{1,0:T(8,128)(2,1)} %refs_6_.1) | copy-start | bytes 983044
  73.6 6.5 %copy-start.2 = (bf16[256,640]{1,0:T(8,128)(2,1)S(1)}, bf16[256,640]{1,0:T(8,128)(2,1)}, u32[]{:S(2)}) copy-start(bf16[256,640]{1,0:T(8,128)(2,1)} %refs_7_.1) | copy-start | bytes 983044
  79.1 16.2 %collective-permute-start.10 = (bf16[272,640]{1,0:T(8,128)(2,1)S(1)}, bf16[272,640]{1,0:T(8,128)(2,1)S(1)}, u32[]{:S(2)}, u32[]{:S(2)}) collective-permute-start(bf16[272,640]{1,0:T(8,128)(2,1)S(1)} %far.3), channel_id=1, source_target_pairs={{0,48},{8,56},{16,0},{24,8},{32,16},{40,24},{48,32},{56,40},{64,11... | collective-permute-start | bytes 1044488 | tf_op jit(solution)/shard_map/ppermute | solution.py:370
  93.0 0.9 copy-start
  93.9 0.6 copy-start.3
  94.5 0.8 copy-start.5
  94.5 0.9 copy-start.6
  95.3 0.7 copy-start.7
  103.6 5.6 %copy-start.9 = (f32[640]{0:T(1024)S(1)}, f32[640]{0:T(1024)}, u32[]{:S(2)}) copy-start(f32[640]{0:T(1024)} %param.21) | copy-start | bytes 7684
  103.6 37.5 %all-to-all-start = ((bf16[8,256,640]{2,1,0:T(8,128)(2,1)}), bf16[8,256,640]{2,1,0:T(8,128)(2,1)S(1)}, u32[]{:S(2)}, u32[]{:S(2)}) async-start(bf16[8,256,640]{2,1,0:T(8,128)(2,1)} %project.1), calls=%async_computation | async-start | bytes 5242880 | tf_op jit(solution)/shard_map/all_to_all | solution.py:408
  109.2 39.5 %copy-start.10 = (f32[640]{0:T(1024)S(1)}, f32[640]{0:T(1024)}, u32[]{:S(2)}) copy-start(f32[640]{0:T(1024)} %param.22) | copy-start | bytes 7684
  109.2 40.0 %copy-start.11 = (f32[640]{0:T(1024)S(1)}, f32[640]{0:T(1024)}, u32[]{:S(2)}) copy-start(f32[640]{0:T(1024)} %param.23) | copy-start | bytes 7684
  141.1 1.5 copy-start.4
  145.3 9.6 %all-to-all-start.1 = ((f32[8,8,256]{2,1,0:T(8,128)}), f32[8,8,256]{2,1,0:T(8,128)S(1)}, u32[]{:S(2)}, u32[]{:S(2)}) async-start(f32[8,8,256]{2,1,0:T(8,128)} %get-tuple-element.33), calls=%async_computation.1 | async-start | bytes 131072 | tf_op jit(solution)/shard_map/all_to_all | solution.py:410
  154.9 0.6 copy-start.8
where the time goes:
time: 159 us; the launch traced here: 158 us
  Pallas kernels  62.4 us (39%)
  waiting for transfers between devices  43.9 us (28%)
  starting transfers between devices  39.9 us (25%)
  local copies, waits for them, and re-layouts  7.48 us (5%)
  other arithmetic  3.41 us (2%)
    all_to_all x1, waiting for transfers between devices, body(): parts = lax.all_to_all(parts, 'tp', 0, 0, tiled=True)  31.3 us
    ppermute x15, starting transfers between devices, body(): lax.ppermute(array, 'req', shift(dx, dz, dc))  30.9 us
    pallas_call x4, Pallas kernels, near(): pl.pallas_call(functools.partial(near_kernel, own), name='near_own' if ow...  27.6 us
    pallas_call x4, Pallas kernels, far(): pl.pallas_call(functools.partial(far_kernel, own), name='far_own' if own...  22.2 us
    pallas_call x1, Pallas kernels, project(): pl.pallas_call(project_kernel, name='project', out_shape=jax.ShapeDtypeSt...  7.55 us
    ppermute x15, waiting for transfers between devices, body(): lax.ppermute(array, 'req', shift(dx, dz, dc))  7.48 us
    all_to_all x1, starting transfers between devices, body(): parts = lax.all_to_all(parts, 'tp', 0, 0, tiled=True)  5.63 us
    all_to_all x1, waiting for transfers between devices, body(): sums = lax.all_to_all(sums, 'tp', 0, 0, tiled=True)  5.1 us
  transfers between devices with their start and end apart: 17, of which 5 were waited for; matrix products, arithmetic and copies ran while one was open for 3% of the time, Pallas kernels for 32%

commit v1 on v0

--- a/solution.py
+++ b/solution.py
@@ -54,25 +54,47 @@
     return request, block, group
 
 
-def features(own, first, page_group_ref, q_ref, feat, kfeat, blocks):
+def pack_kernel(lens_ref, groups_ref, q_ref, out_ref):
+    width = q_ref.shape[1]
+    out_ref[0:TOK, :] = q_ref[...]
+    lane = lax.broadcasted_iota(jnp.int32, (16, width), 1)
+    facts = jnp.zeros((16, width), jnp.int32)
+    for i in range(4):
+        facts = jnp.where(lane == i, lens_ref[0, i], facts)
+        facts = jnp.where(lane == 4 + i, groups_ref[0, i], facts)
+    out_ref[TOK : TOK + 16, :] = facts.astype(jnp.float32).astype(jnp.bfloat16)
+
+
+def pack(lens, groups, queries):
+    smem = pl.BlockSpec(memory_space=pltpu.SMEM)
+    return pl.pallas_call(
+        pack_kernel,
+        name="pack",
+        in_specs=[smem, smem, pl.BlockSpec(memory_space=pltpu.VMEM)],
+        out_specs=pl.BlockSpec(memory_space=pltpu.VMEM),
+        out_shape=jax.ShapeDtypeStruct((TOK + 16, queries.shape[1]), queries.dtype),
+        compiler_params=pltpu.CompilerParams(vmem_limit_bytes=8 << 20),
+    )(lens, groups, queries)
+
+
+def features(own, facts, page_group_ref, feat, kfeat):
     wide = (TOK, HS)
-    facts = q_ref[TOK : TOK + 16, :].astype(jnp.float32)[0:1, :]
-    request, block, group = token_facts(facts, wide)
+    request, block, group = token_facts(facts.astype(jnp.float32)[0:1, :], wide)
     lane = lax.broadcasted_iota(jnp.int32, wide, 1)
     row = lax.broadcasted_iota(jnp.int32, wide, 0)
     feat[0] = jnp.where(lane == group, 1.0, 0.0).astype(jnp.bfloat16)
-    for i in range(blocks):
-        low, high = page_group_ref[first + 2 * i], page_group_ref[first + 2 * i + 1]
+    for i in range(8):
+        low, high = page_group_ref[2 * i], page_group_ref[2 * i + 1]
         hidden = (lane < 2) & (lane != jnp.where(row < 128, low, high))
         kfeat[i] = jnp.where(hidden, BIG, 0.0).astype(jnp.bfloat16)
     if own:
         feat[1] = jnp.where(lane == 2 * request + block, 1.0, 0.0).astype(jnp.bfloat16)
         seen = (request == lane // 2) & (block <= lane % 2)
-        kfeat[blocks] = jnp.where((lane < 8) & ~seen, BIG, 0.0).astype(jnp.bfloat16)
-
-
-def score_pass(query, keys, marks, feat, kfeat, scores, floor):
-    best = floor
+        kfeat[8] = jnp.where((lane < 8) & ~seen, BIG, 0.0).astype(jnp.bfloat16)
+
+
+def score_pass(query, keys, marks, feat, kfeat, scores):
+    best = None
     for i, (key, mark) in enumerate(zip(keys, marks)):
         left = jnp.concatenate([query, feat[mark]], axis=1)
         right = jnp.concatenate([key, kfeat[i]], axis=1)
@@ -100,62 +122,10 @@
     return total[:, :HS], total[:, HS:]
 
 
-def near_kernel(own, page_group_ref, q_ref, *refs):
-    kv_refs, refs = refs[:6], refs[6:]
+def attend_kernel(own, pieces, page_group_ref, *refs):
+    q_refs, refs = refs[:pieces], refs[pieces:]
+    kv_refs, refs = refs[:10], refs[10:]
     suffix, refs = (refs[:2], refs[2:]) if own else ((), refs)
-    num_ref, top_ref, sum_ref, feat, kfeat, scores = refs
-
-    @pl.when(pl.program_id(0) == 0)
-    def _():
-        features(own, 0, page_group_ref, q_ref, feat, kfeat, 6)
-
-    @pl.when(page_group_ref[0] >= 0)
-    def _():
-        keys = [jnp.concatenate([r[0:128, :], r[256:384, :]], axis=0) for r in kv_refs]
-        keys = keys + [r[...] for r in suffix[:1]]
-        marks = [0] * 6 + [1]
-        top_ref[...] = score_pass(q_ref[0:TOK, :], keys, marks, feat, kfeat, scores, None)
-
-    @pl.when(page_group_ref[1] >= 0)
-    def _():
-        values = [jnp.concatenate([r[128:256, :], r[384:512, :]], axis=0) for r in kv_refs]
-        values = values + [r[...] for r in suffix[1:]]
-        num_ref[...], sum_ref[...] = value_pass(values, scores, top_ref[...])
-
-
-def near(own, page_group, query, blocks, suffix=()):
-    count = 7 if own else 6
-    q_spec = pl.BlockSpec((TOK + 16, HS), lambda h, *_: (0, h))
-    s_spec = pl.BlockSpec((TOK, HS), lambda h, *_: (0, h))
-    kv_spec = pl.BlockSpec((2 * TOK, HS), lambda h, *_: (0, h))
-    out = jax.ShapeDtypeStruct((TOK, HEADS_DEV * HS), jnp.float32)
-    return pl.pallas_call(
-        functools.partial(near_kernel, own),
-        name="near_own" if own else "near",
-        out_shape=(out, out, out),
-        grid_spec=pltpu.PrefetchScalarGridSpec(
-            num_scalar_prefetch=1,
-            grid=(HEADS_DEV,),
-            in_specs=[q_spec]
-            + [kv_spec] * 6
-            + [s_spec] * len(suffix),
-            out_specs=(s_spec, s_spec, s_spec),
-            scratch_shapes=[
-                pltpu.VMEM((2, TOK, HS), jnp.bfloat16),
-                pltpu.VMEM((7, TOK, HS), jnp.bfloat16),
-                pltpu.VMEM((TOK, count * TOK), jnp.float32),
-            ],
-        ),
-        compiler_params=pltpu.CompilerParams(vmem_limit_bytes=24 << 20),
-        cost_estimate=pl.CostEstimate(
-            flops=2 * 2 * TOK * TOK * count * HS * HEADS_DEV,
-            bytes_accessed=2 * TOK * HS * HEADS_DEV * (2 * count + 7),
-            transcendentals=TOK * TOK * count * HEADS_DEV,
-        ),
-    )(page_group, query, *blocks, *suffix)
-
-
-def far_kernel(own, page_group_ref, q_ref, u0, v0, u1, v1, num_in, top_in, sum_in, *refs):
     if own:
         num_ref, ml_ref, feat, kfeat, scores, top, ml = refs
     else:
@@ -165,24 +135,32 @@
 
     @pl.when(head == 0)
     def _():
-        features(False, 12, page_group_ref, q_ref, feat, kfeat, 2)
+        facts = q_refs[-1][TOK // pieces : TOK // pieces + 16, :]
+        features(own, facts, page_group_ref, feat, kfeat)
         ml[...] = jnp.zeros_like(ml)
+
+    def rows(start):
+        pick = slice(start, start + 128)
+        later = slice(start + 256, start + 384)
+        out = [jnp.concatenate([r[pick, :], r[later, :]], axis=0) for r in kv_refs[:6]]
+        for a, b in (kv_refs[6:8], kv_refs[8:10]):
+            out.append(jnp.concatenate([a[pick, :], b[pick, :]], axis=0))
+        return out
 
     @pl.when(page_group_ref[0] >= 0)
     def _():
-        keys = [jnp.concatenate([a[0:128, :], b[0:128, :]], axis=0) for a, b in ((u0, v0), (u1, v1))]
-        top[...] = score_pass(q_ref[0:TOK, :], keys, [0, 0], feat, kfeat, scores, top_in[...])
+        if pieces == 1:
+            query = q_refs[0][0:TOK, :]
+        else:
+            query = jnp.concatenate([q_refs[0][...], q_refs[1][0:128, :]], axis=0)
+        keys = rows(0) + [r[...] for r in suffix[:1]]
+        top[...] = score_pass(query, keys, [0] * 8 + [1], feat, kfeat, scores)
 
     @pl.when(page_group_ref[1] >= 0)
     def _():
         largest = top[...]
-        values = [
-            jnp.concatenate([a[128:256, :], b[128:256, :]], axis=0) for a, b in ((u0, v0), (u1, v1))
-        ]
+        values = rows(128) + [r[...] for r in suffix[1:]]
         num, total = value_pass(values, scores, largest)
-        keep = jnp.exp2((top_in[...] - largest) * EXP2_SCALE)
-        num = num + keep * num_in[...]
-        total = total + keep * sum_in[...]
         if own:
             num_ref[...] = num
         else:
@@ -205,43 +183,48 @@
             num_ref[TOK : TOK + 16, :] = jnp.concatenate([high, middle, low], axis=1)
 
 
-def far(own, page_group, query, blocks, state):
+def attend(page_group, query, blocks, suffix=()):
+    own = bool(suffix)
+    count = 9 if own else 8
     width = HEADS_DEV * HS
-    q_spec = pl.BlockSpec((TOK + 16, HS), lambda h, *_: (0, h))
-    s_spec = pl.BlockSpec((TOK, HS), lambda h, *_: (0, h))
+    tall = lambda array: pl.BlockSpec((array.shape[0], HS), lambda h, *_: (0, h))
     if own:
         out_shape = (
             jax.ShapeDtypeStruct((TOK, width), jnp.float32),
             jax.ShapeDtypeStruct((16, TOK), jnp.float32),
         )
-        out_specs = (s_spec, pl.BlockSpec((16, TOK), lambda h, *_: (0, 0)))
+        out_specs = (
+            pl.BlockSpec((TOK, HS), lambda h, *_: (0, h)),
+            pl.BlockSpec((16, TOK), lambda h, *_: (0, 0)),
+        )
     else:
         out_shape = jax.ShapeDtypeStruct((TOK + 16, width), jnp.bfloat16)
         out_specs = pl.BlockSpec((TOK + 16, width), lambda h, *_: (0, 0))
+    operands = (*query, *blocks, *suffix)
     return pl.pallas_call(
-        functools.partial(far_kernel, own),
-        name="far_own" if own else "far",
+        functools.partial(attend_kernel, own, len(query)),
+        name="attend_own" if own else "attend",
         out_shape=out_shape,
         grid_spec=pltpu.PrefetchScalarGridSpec(
             num_scalar_prefetch=1,
             grid=(HEADS_DEV,),
-            in_specs=[q_spec] + [s_spec] * 7,
+            in_specs=[tall(array) for array in operands],
             out_specs=out_specs,
             scratch_shapes=[
                 pltpu.VMEM((2, TOK, HS), jnp.bfloat16),
-                pltpu.VMEM((2, TOK, HS), jnp.bfloat16),
-                pltpu.VMEM((TOK, 2 * TOK), jnp.float32),
+                pltpu.VMEM((9, TOK, HS), jnp.bfloat16),
+                pltpu.VMEM((TOK, count * TOK), jnp.float32),
                 pltpu.VMEM((TOK, HS), jnp.float32),
                 pltpu.VMEM((TOK, HS), jnp.float32),
             ],
         ),
         compiler_params=pltpu.CompilerParams(vmem_limit_bytes=24 << 20),
         cost_estimate=pl.CostEstimate(
-            flops=2 * 2 * TOK * TOK * 2 * HS * HEADS_DEV,
-            bytes_accessed=2 * TOK * HS * HEADS_DEV * 12,
-            transcendentals=TOK * TOK * 2 * HEADS_DEV,
+            flops=2 * 2 * TOK * TOK * count * HS * HEADS_DEV,
+            bytes_accessed=2 * TOK * HS * HEADS_DEV * (2 * count + 3),
+            transcendentals=TOK * TOK * count * HEADS_DEV,
         ),
-    )(page_group, query, *blocks, *state)
+    )(page_group, *operands)
 
 
 def project_kernel(n0, s0, n1, n2, n3, w_ref, out_ref, att):
@@ -369,22 +352,17 @@
     width = queries.shape[1]
     send = lambda array, dx, dz, dc: lax.ppermute(array, "req", shift(dx, dz, dc))
 
-    facts = jnp.concatenate([suffix_lengths, request_group], axis=1).astype(jnp.bfloat16)
-    query = jnp.concatenate([queries, jnp.pad(facts, ((0, 15), (0, width - 8)))], axis=0)
-    ways = [1, -1, 2]
-    their_query = []
-    for dz in ways:
-        their_query.append(send(query, 0, dz, 0))
+    query = pack(suffix_lengths, request_group, queries)
+    below = send(query, 0, 1, 0)
+    above = send(query, 0, -1, 0)
+    opposite = (send(below[:128], 0, 1, 0), send(above[128:], 0, -1, 0))
 
     pages = page_cache.transpose(0, 2, 1, 3).reshape(2 * TOK, width)
     left, right = send(pages, 1, 0, 0), send(pages, -1, 0, 0)
     over_left = send(left[:TOK], 1, 0, 0)
     over_right = send(right[TOK:], -1, 0, 0)
-    near_blocks = [pages, left, right]
-    near_blocks = near_blocks + [send(array, 0, 0, 1) for array in near_blocks]
-    far_blocks = [over_left, over_right]
-    far_blocks.append(send(over_left, 0, 0, 1))
-    far_blocks.append(send(over_right, 0, 0, 1))
+    across = lambda arrays: arrays + [send(array, 0, 0, 1) for array in arrays]
+    blocks = across([pages, left, right]) + across([over_left, over_right])
 
     me = lax.axis_index("req")
     x, z, c = me // (NZ * NC), (me // NC) % NZ, me % NC
@@ -396,14 +374,11 @@
     page_group = jnp.sum((page_table[1][None, :] == slots[:, None]).astype(jnp.int32), 1)
 
     suffix = (suffix_keys, suffix_values)
-    states, others = [], []
-    for q in their_query:
-        states.append(near(False, page_group, q, near_blocks))
-    for q, state, dz in zip(their_query, states, ways):
-        num = far(False, page_group, q, far_blocks, state)
+    others = []
+    for block, dz in ((opposite, 2), ((below,), 1), ((above,), -1)):
+        num = attend(page_group, block, blocks)
         others.append(send(num, 0, -dz, 0))
-    state = near(True, page_group, query, near_blocks, suffix)
-    num, ml = far(True, page_group, query, far_blocks, state)
+    num, ml = attend(page_group, (query,), blocks, suffix)
     parts = project(num, ml, others, out_weight)
     parts = lax.all_to_all(parts, "tp", 0, 0, tiled=True)
     combined, sums = combine(parts, residual, attn_gate[None, :])

time: 159 us -> 162 us (1.019)
  waiting for transfers between devices: 43.9 us -> 69.9 us
  Pallas kernels: 62.4 us -> 44 us
  starting transfers between devices: 39.9 us -> 30.5 us
  local copies, waits for them, and re-layouts: 7.48 us -> 15 us
  other arithmetic: 3.41 us -> 0.26 us
    ppermute x15 -> x16, waiting for transfers between devices: 7.48 us -> 33 us  [body(): lax.ppermute(array, 'req', shift(dx, dz, dc))]
    pallas_call x8 -> x5, Pallas kernels: 49.8 us -> 31.5 us  [the longest x4 30.9 us: attend(): pl.pallas_call(functools.partial(attend_kernel, own, len(query)), name='a...]
    ppermute x15 -> x16, starting transfers between devices: 30.9 us -> 22.5 us  [body(): lax.ppermute(array, 'req', shift(dx, dz, dc))]
    unnamed x26 -> x48, local copies, waits for them, and re-layouts: 4.35 us -> 9.68 us
    concatenate x2 -> x0, other arithmetic: 1.83 us -> none  [the longest x1 1.75 us: body(): jnp.concatenate([queries, jnp.pad(facts, ((0, 15), (0, width - 8)))], axi...]
  transfers between devices with their start and end apart: 17 -> 18, of which waited for: 5 -> 9; matrix products, arithmetic and copies ran while one was open for 3% -> 3% of each run, Pallas kernels for 32% -> 15%
where the time goes in v1:
time: 162 us; the launch traced here: 161 us
  waiting for transfers between devices  69.9 us (43%)
  Pallas kernels  44 us (27%)
  starting transfers between devices  30.5 us (19%)
  local copies, waits for them, and re-layouts  15 us (9%)
    ppermute x16, waiting for transfers between devices, body(): lax.ppermute(array, 'req', shift(dx, dz, dc))  33 us
    all_to_all x1, waiting for transfers between devices, body(): parts = lax.all_to_all(parts, 'tp', 0, 0, tiled=True)  31.9 us
    pallas_call x4, Pallas kernels, attend(): pl.pallas_call(functools.partial(attend_kernel, own, len(query)), name='a...  30.9 us
    ppermute x16, starting transfers between devices, body(): lax.ppermute(array, 'req', shift(dx, dz, dc))  22.5 us
    unnamed x48, local copies, waits for them, and re-layouts  9.68 us
    pallas_call x1, Pallas kernels, project(): pl.pallas_call(project_kernel, name='project', out_shape=jax.ShapeDtypeSt...  7.54 us
    all_to_all x1, waiting for transfers between devices, body(): sums = lax.all_to_all(sums, 'tp', 0, 0, tiled=True)  5.07 us
    all_to_all x1, starting transfers between devices, body(): parts = lax.all_to_all(parts, 'tp', 0, 0, tiled=True)  4.61 us
  transfers between devices with their start and end apart: 18, of which 9 were waited for; matrix products, arithmetic and copies ran while one was open for 3% of the time, Pallas kernels for 15%

profile of v1, /device:TPU:2, one launch (start us, length us, event | category | flops | bytes accessed | tf_op | source)
XLA Modules:
  0.0 160.5 jit_solution(12735491303385077918)
XLA Ops:
  0.6 1.2 copy.16
  1.8 2.3 %collective-permute-start.1 = (bf16[512,640]{1,0:T(8,128)(2,1)S(1)}, bf16[512,640]{1,0:T(8,128)(2,1)S(1)}, u32[]{:S(2)}, u32[]{:S(2)}) collective-permute-start(bf16[512,640]{1,0:T(8,128)(2,1)S(1)} %bitcast.12), channel_id=1, source_target_pairs={{0,192},{8,200},{16,208},{24,216},{32,224},{40,232},{48,240},{56,2... | collective-permute-start | bytes 1966088 | tf_op jit(solution)/shard_map/ppermute | solution.py:353
  4.1 0.0 collective-permute-start
  4.1 1.0 copy-done.9
  5.1 0.7 copy-done.13
  5.8 0.7 copy-done.14
  6.4 0.6 pack.1.refs_0_
  7.0 6.2 %collective-permute-start.11 = (bf16[272,640]{1,0:T(8,128)(2,1)S(1)}, bf16[272,640]{1,0:T(8,128)(2,1)S(1)}, u32[]{:S(2)}, u32[]{:S(2)}) collective-permute-start(bf16[272,640]{1,0:T(8,128)(2,1)S(1)} %pack.1.refs_0_), channel_id=1, source_target_pairs={{0,48},{8,56},{16,0},{24,8},{32,16},{40,24},{48,32},{56,40},{64,11... | collective-permute-start | bytes 1044488 | tf_op jit(solution)/shard_map/ppermute | solution.py:353
  13.2 0.0 collective-permute-start.9
  13.2 14.3 %collective-permute-done.11.refs_0_ = bf16[272,640]{1,0:T(8,128)(2,1)S(1)} collective-permute-done((bf16[272,640]{1,0:T(8,128)(2,1)S(1)}, bf16[272,640]{1,0:T(8,128)(2,1)S(1)}, u32[]{:S(2)}, u32[]{:S(2)}) %collective-permute-start.11) | collective-permute-done | bytes 348192 | tf_op jit(solution)/shard_map/ppermute | solution.py:353
  27.5 0.7 slice.23
  28.2 0.7 copy-done.2
  28.9 4.6 %collective-permute-start.12 = (bf16[144,640]{1,0:T(8,128)(2,1)}, bf16[144,640]{1,0:T(8,128)(2,1)S(1)}, u32[]{:S(2)}, u32[]{:S(2)}) collective-permute-start(bf16[144,640]{1,0:T(8,128)(2,1)} %slice.23), channel_id=1, source_target_pairs={{0,48},{8,56},{16,0},{24,8},{32,16},{40,24},{48,32},{56,40},{64,11... | collective-permute-start | bytes 552968 | tf_op jit(solution)/shard_map/ppermute | solution.py:353
  33.5 0.0 collective-permute-done.9.refs_0_
  33.5 0.8 copy-done.4
  34.3 0.0 collective-permute-start.10
  34.3 0.0 collective-permute-start.2
  34.3 0.1 stack.35
  34.4 0.0 collective-permute-done.1.refs_3_.refs_4_
  34.4 0.8 slice.21
  35.1 1.6 collective-permute-start.6
  36.7 0.0 collective-permute-done.refs_2_.refs_3_
  36.7 0.8 slice.20
  37.5 0.5 collective-permute-start.5
  37.9 3.8 %collective-permute-done.10.refs_0_ = bf16[128,640]{1,0:T(8,128)(2,1)S(1)} collective-permute-done((bf16[128,640]{1,0:T(8,128)(2,1)S(1)}, bf16[128,640]{1,0:T(8,128)(2,1)S(1)}, u32[]{:S(2)}, u32[]{:S(2)}) %collective-permute-start.10) | collective-permute-done | bytes 163872 | tf_op jit(solution)/shard_map/ppermute | solution.py:353
  41.7 0.7 copy-done.10
  42.4 0.5 collective-permute-start.3
  42.9 0.1 iota_add_fusion
  43.0 0.1 add.145
  43.1 2.5 %collective-permute-done.6.refs_8_.refs_9_ = bf16[256,640]{1,0:T(8,128)(2,1)} collective-permute-done((bf16[256,640]{1,0:T(8,128)(2,1)}, bf16[256,640]{1,0:T(8,128)(2,1)}, u32[]{:S(2)}, u32[]{:S(2)}) %collective-permute-start.6) | collective-permute-done | bytes 327712 | tf_op jit(solution)/shard_map/ppermute | solution.py:353
  45.6 3.2 %collective-permute-done.5.refs_7_.refs_8_ = bf16[256,640]{1,0:T(8,128)(2,1)} collective-permute-done((bf16[256,640]{1,0:T(8,128)(2,1)}, bf16[256,640]{1,0:T(8,128)(2,1)}, u32[]{:S(2)}, u32[]{:S(2)}) %collective-permute-start.5) | collective-permute-done | bytes 327712 | tf_op jit(solution)/shard_map/ppermute | solution.py:353
  48.8 0.0 collective-permute-start.7
  48.8 0.2 convert_reduce_fusion.page_group_ref
  49.0 0.0 collective-permute-done.2.refs_4_.refs_5_
  49.1 1.6 %collective-permute-done.7.refs_9_.refs_10_ = bf16[256,640]{1,0:T(8,128)(2,1)S(1)} collective-permute-done((bf16[256,640]{1,0:T(8,128)(2,1)}, bf16[256,640]{1,0:T(8,128)(2,1)S(1)}, u32[]{:S(2)}, u32[]{:S(2)}) %collective-permute-start.7) | collective-permute-done | bytes 327712 | tf_op jit(solution)/shard_map/ppermute | solution.py:353
  50.7 0.9 copy-done.11
  51.6 7.6 %attend.3 = bf16[272,640]{1,0:T(8,128)(2,1)S(1)} custom-call(s32[16]{0:T(128)S(1)} %convert_reduce_fusion.page_group_ref, bf16[128,640]{1,0:T(8,128)(2,1)S(1)} %copy-done.11, bf16[144,640]{1,0:T(8,128)(2,1)S(1)} %collective-permute-done.12.refs_1_, bf16[512,640]{1,0:T(8,128)(2,1)S(1)} %bitcast.15, bf16[512,640]{1,0:T(8,128)(2,1)S(1)} %collective-permute-done.refs_2_.refs_3_, ...), custom_call_target="tpu_custom_call" | custom-call | flops 1342177280 | bytes 6225920 | tf_op jit(solution)/shard_map/attend/pallas_call | solution.py:204
  59.2 3.0 %collective-permute-start.13 = (bf16[272,640]{1,0:T(8,128)(2,1)S(1)}, bf16[272,640]{1,0:T(8,128)(2,1)S(1)}, u32[]{:S(2)}, u32[]{:S(2)}) collective-permute-start(bf16[272,640]{1,0:T(8,128)(2,1)S(1)} %attend.3), channel_id=1, source_target_pairs={{0,32},{8,40},{16,48},{24,56},{32,0},{40,8},{48,16},{56,24},{64,96... | collective-permute-start | bytes 1044488 | tf_op jit(solution)/shard_map/ppermute | solution.py:353
  62.2 7.6 %attend.4 = bf16[272,640]{1,0:T(8,128)(2,1)S(1)} custom-call(s32[16]{0:T(128)S(1)} %convert_reduce_fusion.page_group_ref, bf16[272,640]{1,0:T(8,128)(2,1)S(1)} %copy-done.5, bf16[512,640]{1,0:T(8,128)(2,1)S(1)} %bitcast.16, bf16[512,640]{1,0:T(8,128)(2,1)S(1)} %collective-permute-done.refs_2_.refs_3_, ...), custom_call_target="tpu_custom_call" | custom-call | flops 1342177280 | bytes 6225920 | tf_op jit(solution)/shard_map/attend/pallas_call | solution.py:204
  69.7 0.0 copy-start.7
  69.8 0.0 copy-start.8
  69.8 2.7 %collective-permute-start.14 = (bf16[272,640]{1,0:T(8,128)(2,1)S(1)}, bf16[272,640]{1,0:T(8,128)(2,1)S(1)}, u32[]{:S(2)}, u32[]{:S(2)}) collective-permute-start(bf16[272,640]{1,0:T(8,128)(2,1)S(1)} %attend.4), channel_id=1, source_target_pairs={{0,48},{8,56},{16,0},{24,8},{32,16},{40,24},{48,32},{56,40},{64,11... | collective-permute-start | bytes 1044488 | tf_op jit(solution)/shard_map/ppermute | solution.py:353
  72.5 7.6 %attend.5 = bf16[272,640]{1,0:T(8,128)(2,1)S(1)} custom-call(s32[16]{0:T(128)S(1)} %convert_reduce_fusion.page_group_ref, bf16[272,640]{1,0:T(8,128)(2,1)S(1)} %copy-done.3, bf16[512,640]{1,0:T(8,128)(2,1)S(1)} %bitcast.17, bf16[512,640]{1,0:T(8,128)(2,1)S(1)} %collective-permute-done.refs_2_.refs_3_, ...), custom_call_target="tpu_custom_call" | custom-call | flops 1342177280 | bytes 6225920 | tf_op jit(solution)/shard_map/attend/pallas_call | solution.py:204
  80.0 1.3 collective-permute-start.15
  81.4 8.2 %attend_own.1 = (f32[256,640]{1,0:T(8,128)S(1)}, f32[16,256]{1,0:T(8,128)S(1)}) custom-call(s32[16]{0:T(128)S(1)} %convert_reduce_fusion.page_group_ref, bf16[272,640]{1,0:T(8,128)(2,1)S(1)} %copy-done.1, bf16[512,640]{1,0:T(8,128)(2,1)S(1)} %bitcast.18, bf16[512,640]{1,0:T(8,128)(2,1)S(1)} %collective-permute-done.refs_2_.refs_3_, ...), custom_call_target="tpu_custom_call" | custom-call | flops 1509949440 | bytes 6881280 | tf_op jit(solution)/shard_map/attend_own/pallas_call | solution.py:204
  89.6 0.8 copy-done.6
  90.4 0.6 copy-done.12
  91.0 4.1 %collective-permute-done.14.n2 = bf16[272,640]{1,0:T(8,128)(2,1)S(1)} collective-permute-done((bf16[272,640]{1,0:T(8,128)(2,1)S(1)}, bf16[272,640]{1,0:T(8,128)(2,1)S(1)}, u32[]{:S(2)}, u32[]{:S(2)}) %collective-permute-start.14) | collective-permute-done | bytes 348192 | tf_op jit(solution)/shard_map/ppermute | solution.py:353
  95.1 3.3 %collective-permute-done.15.n3 = bf16[272,640]{1,0:T(8,128)(2,1)S(1)} collective-permute-done((bf16[272,640]{1,0:T(8,128)(2,1)S(1)}, bf16[272,640]{1,0:T(8,128)(2,1)S(1)}, u32[]{:S(2)}, u32[]{:S(2)}) %collective-permute-start.15) | collective-permute-done | bytes 348192 | tf_op jit(solution)/shard_map/ppermute | solution.py:353
  98.5 0.7 copy-done.18
  99.2 7.5 %project.1 = bf16[8,256,640]{2,1,0:T(8,128)(2,1)} custom-call(f32[256,640]{1,0:T(8,128)} %copy-done.6, f32[16,256]{1,0:T(8,128)} %copy-done.12, bf16[272,640]{1,0:T(8,128)(2,1)} %copy-done.16, bf16[272,640]{1,0:T(8,128)(2,1)} %copy-done.17, bf16[272,640]{1,0:T(8,128)(2,1)} %copy-done.18, bf16[640,5120]{1,0:T(8,128)(2,1)} %w_ref.1), custom_call_target="tpu_custom_call" | custom-call | flops 1677721600 | bytes 10158080 | tf_op jit(solution)/shard_map/project/pallas_call | solution.py:261
  106.8 4.6 %all-to-all-start = ((bf16[8,256,640]{2,1,0:T(8,128)(2,1)}), bf16[8,256,640]{2,1,0:T(8,128)(2,1)S(1)}, u32[]{:S(2)}, u32[]{:S(2)}) async-start(bf16[8,256,640]{2,1,0:T(8,128)(2,1)} %project.1), calls=%async_computation | async-start | bytes 5242880 | tf_op jit(solution)/shard_map/all_to_all | solution.py:383
  111.4 0.0 copy-start.21
  111.4 0.0 copy-start.22
  111.4 0.6 broadcast_in_dim.11.gate_ref
  112.0 31.9 %all-to-all-done.parts_ref = bf16[8,256,640]{2,1,0:T(8,128)(2,1)S(1)} async-done(((bf16[8,256,640]{2,1,0:T(8,128)(2,1)}), bf16[8,256,640]{2,1,0:T(8,128)(2,1)S(1)}, u32[]{:S(2)}, u32[]{:S(2)}) %all-to-all-start) | async-done | bytes 2621472 | tf_op jit(solution)/shard_map/all_to_all | solution.py:383
  143.8 1.5 copy-done.15
  145.3 2.7 %combine.1 = (f32[256,640]{1,0:T(8,128)}, f32[8,8,256]{2,1,0:T(8,128)}) custom-call(bf16[8,256,640]{2,1,0:T(8,128)(2,1)} %copy-done.15, bf16[256,640]{1,0:T(8,128)(2,1)} %residual_ref.1, f32[1,640]{1,0:T(1,128)} %broadcast_in_dim.11.gate_ref), custom_call_target="tpu_custom_call" | custom-call | tf_op jit(solution)/shard_map/combine/pallas_call | solution.py:296
  148.1 3.4 %all-to-all-start.1 = ((f32[8,8,256]{2,1,0:T(8,128)}), f32[8,8,256]{2,1,0:T(8,128)S(1)}, u32[]{:S(2)}, u32[]{:S(2)}) async-start(f32[8,8,256]{2,1,0:T(8,128)} %get-tuple-element.9), calls=%async_computation.1 | async-start | bytes 131072 | tf_op jit(solution)/shard_map/all_to_all | solution.py:385
  151.4 0.6 broadcast_in_dim.12.shift_ref
  152.0 0.6 broadcast_in_dim.13.scale_ref
  152.6 5.1 %all-to-all-done.1.sums_ref = f32[8,8,256]{2,1,0:T(8,128)S(1)} async-done(((f32[8,8,256]{2,1,0:T(8,128)}), f32[8,8,256]{2,1,0:T(8,128)S(1)}, u32[]{:S(2)}, u32[]{:S(2)}) %all-to-all-start.1) | async-done | bytes 65568 | tf_op jit(solution)/shard_map/all_to_all | solution.py:385
  157.7 0.6 copy-done.19
  158.3 2.2 %finish.1 = (bf16[256,640]{1,0:T(8,128)(2,1)}, bf16[256,640]{1,0:T(8,128)(2,1)}) custom-call(f32[256,640]{1,0:T(8,128)} %get-tuple-element.8.combined_ref, f32[8,8,256]{2,1,0:T(8,128)} %copy-done.19, f32[1,640]{1,0:T(1,128)} %broadcast_in_dim.12.shift_ref, f32[1,640]{1,0:T(1,128)} %broadcast_in_dim.13.scale_ref), custom_call_target="tpu_custom_call" | custom-call | tf_op jit(solution)/shard_map/finish/pallas_call | solution.py:333
  (42 shorter events, 0.1 us)
Async XLA Ops:
  0.6 48.2 %copy-start.23 = (s32[2,32]{1,0:T(2,128)S(1)}, s32[2,32]{1,0:T(2,128)}, u32[]{:S(2)}) copy-start(s32[2,32]{1,0:T(2,128)} %param.16) | copy-start | bytes 772
  1.8 32.6 %collective-permute-start.1 = (bf16[512,640]{1,0:T(8,128)(2,1)S(1)}, bf16[512,640]{1,0:T(8,128)(2,1)S(1)}, u32[]{:S(2)}, u32[]{:S(2)}) collective-permute-start(bf16[512,640]{1,0:T(8,128)(2,1)S(1)} %bitcast.12), channel_id=1, source_target_pairs={{0,192},{8,200},{16,208},{24,216},{32,224},{40,232},{48,240},{56,2... | collective-permute-start | bytes 1966088 | tf_op jit(solution)/shard_map/ppermute | solution.py:353
  4.1 32.6 %collective-permute-start = (bf16[512,640]{1,0:T(8,128)(2,1)S(1)}, bf16[512,640]{1,0:T(8,128)(2,1)S(1)}, u32[]{:S(2)}, u32[]{:S(2)}) collective-permute-start(bf16[512,640]{1,0:T(8,128)(2,1)S(1)} %bitcast.13), channel_id=1, source_target_pairs={{0,64},{8,72},{16,80},{24,88},{32,96},{40,104},{48,112},{56,120},{... | collective-permute-start | bytes 1966088 | tf_op jit(solution)/shard_map/ppermute | solution.py:353
  4.1 1.0 copy-start.9
  5.1 0.7 copy-start.13
  5.8 0.7 copy-start.14
  7.0 26.5 %copy-start = (bf16[272,640]{1,0:T(8,128)(2,1)}, bf16[272,640]{1,0:T(8,128)(2,1)S(1)}, u32[]{:S(2)}) copy-start(bf16[272,640]{1,0:T(8,128)(2,1)S(1)} %pack.1.refs_0_) | copy-start | bytes 1044484
  7.0 20.5 %collective-permute-start.11 = (bf16[272,640]{1,0:T(8,128)(2,1)S(1)}, bf16[272,640]{1,0:T(8,128)(2,1)S(1)}, u32[]{:S(2)}, u32[]{:S(2)}) collective-permute-start(bf16[272,640]{1,0:T(8,128)(2,1)S(1)} %pack.1.refs_0_), channel_id=1, source_target_pairs={{0,48},{8,56},{16,0},{24,8},{32,16},{40,24},{48,32},{56,40},{64,11... | collective-permute-start | bytes 1044488 | tf_op jit(solution)/shard_map/ppermute | solution.py:353
  13.2 20.3 %collective-permute-start.9 = (bf16[272,640]{1,0:T(8,128)(2,1)S(1)}, bf16[272,640]{1,0:T(8,128)(2,1)S(1)}, u32[]{:S(2)}, u32[]{:S(2)}) collective-permute-start(bf16[272,640]{1,0:T(8,128)(2,1)S(1)} %pack.1.refs_0_), channel_id=1, source_target_pairs={{0,16},{8,24},{16,32},{24,40},{32,48},{40,56},{48,0},{56,8},{64,80... | collective-permute-start | bytes 1044488 | tf_op jit(solution)/shard_map/ppermute | solution.py:353
  28.2 0.7 copy-start.2
  28.9 13.5 %collective-permute-start.12 = (bf16[144,640]{1,0:T(8,128)(2,1)}, bf16[144,640]{1,0:T(8,128)(2,1)S(1)}, u32[]{:S(2)}, u32[]{:S(2)}) collective-permute-start(bf16[144,640]{1,0:T(8,128)(2,1)} %slice.23), channel_id=1, source_target_pairs={{0,48},{8,56},{16,0},{24,8},{32,16},{40,24},{48,32},{56,40},{64,11... | collective-permute-start | bytes 552968 | tf_op jit(solution)/shard_map/ppermute | solution.py:353
  33.5 0.8 copy-start.4
  34.3 7.4 %collective-permute-start.10 = (bf16[128,640]{1,0:T(8,128)(2,1)S(1)}, bf16[128,640]{1,0:T(8,128)(2,1)S(1)}, u32[]{:S(2)}, u32[]{:S(2)}) collective-permute-start(bf16[128,640]{1,0:T(8,128)(2,1)S(1)} %slice.22), channel_id=1, source_target_pairs={{0,16},{8,24},{16,32},{24,40},{32,48},{40,56},{48,0},{56,8},{64,80... | collective-permute-start | bytes 491528 | tf_op jit(solution)/shard_map/ppermute | solution.py:353
  34.3 14.7 %collective-permute-start.2 = (bf16[512,640]{1,0:T(8,128)(2,1)S(1)}, bf16[512,640]{1,0:T(8,128)(2,1)S(1)}, u32[]{:S(2)}, u32[]{:S(2)}) collective-permute-start(bf16[512,640]{1,0:T(8,128)(2,1)S(1)} %bitcast.14), channel_id=1, source_target_pairs={{0,8},{8,0},{16,24},{24,16},{32,40},{40,32},{48,56},{56,48},{64,72... | collective-permute-start | bytes 1966088 | tf_op jit(solution)/shard_map/ppermute | solution.py:353
  35.1 10.4 %collective-permute-start.6 = (bf16[256,640]{1,0:T(8,128)(2,1)}, bf16[256,640]{1,0:T(8,128)(2,1)}, u32[]{:S(2)}, u32[]{:S(2)}) collective-permute-start(bf16[256,640]{1,0:T(8,128)(2,1)} %slice.21), channel_id=1, source_target_pairs={{0,192},{8,200},{16,208},{24,216},{32,224},{40,232},{48,240},{56,2... | collective-permute-start | bytes 983048 | tf_op jit(solution)/shard_map/ppermute | solution.py:353
  37.5 11.4 %collective-permute-start.5 = (bf16[256,640]{1,0:T(8,128)(2,1)}, bf16[256,640]{1,0:T(8,128)(2,1)}, u32[]{:S(2)}, u32[]{:S(2)}) collective-permute-start(bf16[256,640]{1,0:T(8,128)(2,1)} %slice.20), channel_id=1, source_target_pairs={{0,64},{8,72},{16,80},{24,88},{32,96},{40,104},{48,112},{56,120},{... | collective-permute-start | bytes 983048 | tf_op jit(solution)/shard_map/ppermute | solution.py:353
  41.7 0.7 copy-start.10
  42.4 6.7 %collective-permute-start.4 = (bf16[512,640]{1,0:T(8,128)(2,1)S(1)}, bf16[512,640]{1,0:T(8,128)(2,1)S(1)}, u32[]{:S(2)}, u32[]{:S(2)}) collective-permute-start(bf16[512,640]{1,0:T(8,128)(2,1)S(1)} %collective-permute-done.1.refs_3_.refs_4_), channel_id=1, source_target_pairs={{0,8},{8,0},{16,24},{24,16},{32,40},{40,32},{48,56},{56,48},{64,72... | collective-permute-start | bytes 1966088 | tf_op jit(solution)/shard_map/ppermute | solution.py:353
  42.4 8.3 %collective-permute-start.3 = (bf16[512,640]{1,0:T(8,128)(2,1)S(1)}, bf16[512,640]{1,0:T(8,128)(2,1)}, u32[]{:S(2)}, u32[]{:S(2)}) collective-permute-start(bf16[512,640]{1,0:T(8,128)(2,1)S(1)} %collective-permute-done.refs_2_.refs_3_), channel_id=1, source_target_pairs={{0,8},{8,0},{16,24},{24,16},{32,40},{40,32},{48,56},{56,48},{64,72... | collective-permute-start | bytes 1966088 | tf_op jit(solution)/shard_map/ppermute | solution.py:353
  45.6 3.4 %collective-permute-start.8 = (bf16[256,640]{1,0:T(8,128)(2,1)}, bf16[256,640]{1,0:T(8,128)(2,1)S(1)}, u32[]{:S(2)}, u32[]{:S(2)}) collective-permute-start(bf16[256,640]{1,0:T(8,128)(2,1)} %collective-permute-done.6.refs_8_.refs_9_), channel_id=1, source_target_pairs={{0,8},{8,0},{16,24},{24,16},{32,40},{40,32},{48,56},{56,48},{64,72... | collective-permute-start | bytes 983048 | tf_op jit(solution)/shard_map/ppermute | solution.py:353
  48.8 1.8 %collective-permute-start.7 = (bf16[256,640]{1,0:T(8,128)(2,1)}, bf16[256,640]{1,0:T(8,128)(2,1)S(1)}, u32[]{:S(2)}, u32[]{:S(2)}) collective-permute-start(bf16[256,640]{1,0:T(8,128)(2,1)} %collective-permute-done.5.refs_7_.refs_8_), channel_id=1, source_target_pairs={{0,8},{8,0},{16,24},{24,16},{32,40},{40,32},{48,56},{56,48},{64,72... | collective-permute-start | bytes 983048 | tf_op jit(solution)/shard_map/ppermute | solution.py:353
  49.0 13.1 %copy-start.5 = (bf16[272,640]{1,0:T(8,128)(2,1)S(1)}, bf16[272,640]{1,0:T(8,128)(2,1)}, u32[]{:S(2)}) copy-start(bf16[272,640]{1,0:T(8,128)(2,1)} %copy-done.4) | copy-start | bytes 1044484
  50.7 0.9 copy-start.11
  59.2 13.3 %copy-start.3 = (bf16[272,640]{1,0:T(8,128)(2,1)S(1)}, bf16[272,640]{1,0:T(8,128)(2,1)}, u32[]{:S(2)}) copy-start(bf16[272,640]{1,0:T(8,128)(2,1)} %copy-done.2) | copy-start | bytes 1044484
  59.2 31.8 %collective-permute-start.13 = (bf16[272,640]{1,0:T(8,128)(2,1)S(1)}, bf16[272,640]{1,0:T(8,128)(2,1)S(1)}, u32[]{:S(2)}, u32[]{:S(2)}) collective-permute-start(bf16[272,640]{1,0:T(8,128)(2,1)S(1)} %attend.3), channel_id=1, source_target_pairs={{0,32},{8,40},{16,48},{24,56},{32,0},{40,8},{48,16},{56,24},{64,96... | collective-permute-start | bytes 1044488 | tf_op jit(solution)/shard_map/ppermute | solution.py:353
  69.7 11.6 %copy-start.1 = (bf16[272,640]{1,0:T(8,128)(2,1)S(1)}, bf16[272,640]{1,0:T(8,128)(2,1)}, u32[]{:S(2)}) copy-start(bf16[272,640]{1,0:T(8,128)(2,1)} %copy-done) | copy-start | bytes 1044484
  69.7 11.6 %copy-start.7 = (bf16[256,640]{1,0:T(8,128)(2,1)S(1)}, bf16[256,640]{1,0:T(8,128)(2,1)}, u32[]{:S(2)}) copy-start(bf16[256,640]{1,0:T(8,128)(2,1)} %refs_11_.1) | copy-start | bytes 983044
  69.8 11.6 %copy-start.8 = (bf16[256,640]{1,0:T(8,128)(2,1)S(1)}, bf16[256,640]{1,0:T(8,128)(2,1)}, u32[]{:S(2)}) copy-start(bf16[256,640]{1,0:T(8,128)(2,1)} %refs_12_.1) | copy-start | bytes 983044
  69.8 25.4 %collective-permute-start.14 = (bf16[272,640]{1,0:T(8,128)(2,1)S(1)}, bf16[272,640]{1,0:T(8,128)(2,1)S(1)}, u32[]{:S(2)}, u32[]{:S(2)}) collective-permute-start(bf16[272,640]{1,0:T(8,128)(2,1)S(1)} %attend.4), channel_id=1, source_target_pairs={{0,48},{8,56},{16,0},{24,8},{32,16},{40,24},{48,32},{56,40},{64,11... | collective-permute-start | bytes 1044488 | tf_op jit(solution)/shard_map/ppermute | solution.py:353
  80.0 18.4 %collective-permute-start.15 = (bf16[272,640]{1,0:T(8,128)(2,1)S(1)}, bf16[272,640]{1,0:T(8,128)(2,1)S(1)}, u32[]{:S(2)}, u32[]{:S(2)}) collective-permute-start(bf16[272,640]{1,0:T(8,128)(2,1)S(1)} %attend.5), channel_id=1, source_target_pairs={{0,16},{8,24},{16,32},{24,40},{32,48},{40,56},{48,0},{56,8},{64,80... | collective-permute-start | bytes 1044488 | tf_op jit(solution)/shard_map/ppermute | solution.py:353
  89.5 0.8 copy-start.6
  90.4 0.6 copy-start.12
  91.0 7.5 %copy-start.16 = (bf16[272,640]{1,0:T(8,128)(2,1)}, bf16[272,640]{1,0:T(8,128)(2,1)S(1)}, u32[]{:S(2)}) copy-start(bf16[272,640]{1,0:T(8,128)(2,1)S(1)} %collective-permute-done.13.n1) | copy-start | bytes 1044484
  95.1 3.3 %copy-start.17 = (bf16[272,640]{1,0:T(8,128)(2,1)}, bf16[272,640]{1,0:T(8,128)(2,1)S(1)}, u32[]{:S(2)}) copy-start(bf16[272,640]{1,0:T(8,128)(2,1)S(1)} %collective-permute-done.14.n2) | copy-start | bytes 1044484
  98.5 0.7 copy-start.18
  106.8 4.6 %copy-start.20 = (f32[640]{0:T(1024)S(1)}, f32[640]{0:T(1024)}, u32[]{:S(2)}) copy-start(f32[640]{0:T(1024)} %param.21) | copy-start | bytes 7684
  106.8 37.1 %all-to-all-start = ((bf16[8,256,640]{2,1,0:T(8,128)(2,1)}), bf16[8,256,640]{2,1,0:T(8,128)(2,1)S(1)}, u32[]{:S(2)}, u32[]{:S(2)}) async-start(bf16[8,256,640]{2,1,0:T(8,128)(2,1)} %project.1), calls=%async_computation | async-start | bytes 5242880 | tf_op jit(solution)/shard_map/all_to_all | solution.py:383
  111.4 40.0 %copy-start.21 = (f32[640]{0:T(1024)S(1)}, f32[640]{0:T(1024)}, u32[]{:S(2)}) copy-start(f32[640]{0:T(1024)} %param.22) | copy-start | bytes 7684
  111.4 40.6 %copy-start.22 = (f32[640]{0:T(1024)S(1)}, f32[640]{0:T(1024)}, u32[]{:S(2)}) copy-start(f32[640]{0:T(1024)} %param.23) | copy-start | bytes 7684
  143.8 1.5 copy-start.15
  148.1 9.6 %all-to-all-start.1 = ((f32[8,8,256]{2,1,0:T(8,128)}), f32[8,8,256]{2,1,0:T(8,128)S(1)}, u32[]{:S(2)}, u32[]{:S(2)}) async-start(f32[8,8,256]{2,1,0:T(8,128)} %get-tuple-element.9), calls=%async_computation.1 | async-start | bytes 131072 | tf_op jit(solution)/shard_map/all_to_all | solution.py:385
  157.7 0.6 copy-start.19

commit v2 on v1

--- a/solution.py
+++ b/solution.py
@@ -73,7 +73,6 @@
         in_specs=[smem, smem, pl.BlockSpec(memory_space=pltpu.VMEM)],
         out_specs=pl.BlockSpec(memory_space=pltpu.VMEM),
         out_shape=jax.ShapeDtypeStruct((TOK + 16, queries.shape[1]), queries.dtype),
-        compiler_params=pltpu.CompilerParams(vmem_limit_bytes=8 << 20),
     )(lens, groups, queries)
 
 
@@ -261,13 +260,14 @@
     return pl.pallas_call(
         project_kernel,
         name="project",
-        out_shape=jax.ShapeDtypeStruct((8, TOK, width), jnp.bfloat16),
+        out_shape=pltpu.HBM((8, TOK, width), jnp.bfloat16),
         grid=(4,),
         in_specs=[whole((TOK, width)), whole((16, TOK))]
         + [whole((TOK + 16, width))] * 3
         + [pl.BlockSpec((width, 2 * width), lambda j: (0, j))],
         out_specs=pl.BlockSpec((2, TOK, width), lambda j: (j, 0, 0)),
         scratch_shapes=[pltpu.VMEM((TOK, width), jnp.bfloat16)],
+        compiler_params=pltpu.CompilerParams(vmem_limit_bytes=24 << 20),
         cost_estimate=pl.CostEstimate(
             flops=2 * TOK * width * D,
             bytes_accessed=2 * (width * D + TOK * D) + 3 * 2 * TOK * width,
@@ -310,6 +310,7 @@
             jax.ShapeDtypeStruct((TOK, width), jnp.float32),
             jax.ShapeDtypeStruct((8, 8, TOK), jnp.float32),
         ),
+        compiler_params=pltpu.CompilerParams(vmem_limit_bytes=16 << 20),
     )(parts, residual, gate)
 
 
@@ -330,9 +331,12 @@
 
 def finish(combined, sums, mod_shift, mod_scale):
     shape = jax.ShapeDtypeStruct(combined.shape, jnp.bfloat16)
-    return pl.pallas_call(finish_kernel, name="finish", out_shape=(shape, shape))(
-        combined, sums, mod_shift, mod_scale
-    )
+    return pl.pallas_call(
+        finish_kernel,
+        name="finish",
+        out_shape=(shape, shape),
+        compiler_params=pltpu.CompilerParams(vmem_limit_bytes=16 << 20),
+    )(combined, sums, mod_shift, mod_scale)
 
 
 def body(
@@ -355,7 +359,7 @@
     query = pack(suffix_lengths, request_group, queries)
     below = send(query, 0, 1, 0)
     above = send(query, 0, -1, 0)
-    opposite = (send(below[:128], 0, 1, 0), send(above[128:], 0, -1, 0))
+    opposite = send(query, 0, 2, 0)
 
     pages = page_cache.transpose(0, 2, 1, 3).reshape(2 * TOK, width)
     left, right = send(pages, 1, 0, 0), send(pages, -1, 0, 0)
@@ -375,8 +379,8 @@
 
     suffix = (suffix_keys, suffix_values)
     others = []
-    for block, dz in ((opposite, 2), ((below,), 1), ((above,), -1)):
-        num = attend(page_group, block, blocks)
+    for block, dz in ((below, 1), (opposite, 2), (above, -1)):
+        num = attend(page_group, (block,), blocks)
         others.append(send(num, 0, -dz, 0))
     num, ml = attend(page_group, (query,), blocks, suffix)
     parts = project(num, ml, others, out_weight)

time: 162 us -> 163 us (level); the launches traced: 161 us -> 160 us
  starting transfers between devices: 30.5 us -> 53.3 us
  local copies, waits for them, and re-layouts: 15 us -> 3.14 us
  waiting for transfers between devices: 69.9 us -> 61.5 us
  Pallas kernels: 44 us -> 40.7 us
    all_to_all x1, starting transfers between devices: 4.61 us -> 21.2 us  [body(): parts = lax.all_to_all(parts, 'tp', 0, 0, tiled=True)]
    ppermute x16 -> x15, waiting for transfers between devices: 33 us -> 23.5 us  [body(): lax.ppermute(array, 'req', shift(dx, dz, dc))]
    unnamed x48 -> x20, local copies, waits for them, and re-layouts: 9.68 us -> 1.02 us
    ppermute x16 -> x15, starting transfers between devices: 22.5 us -> 28.7 us  [body(): lax.ppermute(array, 'req', shift(dx, dz, dc))]
    pallas_call x2, Pallas kernels: 9.78 us -> 6.2 us  [the longest x1 5.08 us: project(): pl.pallas_call(project_kernel, name='project', out_shape=pltpu.HBM((8, TO...]
  transfers between devices with their start and end apart: 18 -> 17, of which waited for: 9 -> 7; matrix products, arithmetic and copies ran while one was open for 3% -> 1% of each run, Pallas kernels for 15% -> 21%
where the time goes in v2:
time: 163 us; the launch traced here: 160 us
  waiting for transfers between devices  61.5 us (38%)
  starting transfers between devices  53.3 us (33%)
  Pallas kernels  40.7 us (25%)
  local copies, waits for them, and re-layouts  3.14 us (2%)
    all_to_all x1, waiting for transfers between devices, body(): parts = lax.all_to_all(parts, 'tp', 0, 0, tiled=True)  31.8 us
    pallas_call x4, Pallas kernels, attend(): pl.pallas_call(functools.partial(attend_kernel, own, len(query)), name='a...  31.2 us
    ppermute x15, starting transfers between devices, body(): lax.ppermute(array, 'req', shift(dx, dz, dc))  28.7 us
    ppermute x15, waiting for transfers between devices, body(): lax.ppermute(array, 'req', shift(dx, dz, dc))  23.5 us
    all_to_all x1, starting transfers between devices, body(): parts = lax.all_to_all(parts, 'tp', 0, 0, tiled=True)  21.2 us
    all_to_all x1, waiting for transfers between devices, body(): sums = lax.all_to_all(sums, 'tp', 0, 0, tiled=True)  6.23 us
    pallas_call x1, Pallas kernels, project(): pl.pallas_call(project_kernel, name='project', out_shape=pltpu.HBM((8, TO...  5.08 us
    all_to_all x1, starting transfers between devices, body(): sums = lax.all_to_all(sums, 'tp', 0, 0, tiled=True)  3.35 us
  transfers between devices with their start and end apart: 17, of which 7 were waited for; matrix products, arithmetic and copies ran while one was open for 1% of the time, Pallas kernels for 21%

profile of v2, /device:TPU:2, one launch (start us, length us, event | category | flops | bytes accessed | tf_op | source)
XLA Modules:
  0.0 159.7 jit_solution(17288284677961612871)
XLA Ops:
  0.6 0.0 copy-start.7
  0.6 1.2 copy.16
  1.8 1.6 collective-permute-start
  3.4 0.8 collective-permute-start.1
  4.2 1.7 %pack.1.refs_0_ = bf16[272,640]{1,0:T(8,128)(2,1)} custom-call(s32[1,4]{1,0:T(1,128)} %lens_ref.1, s32[1,4]{1,0:T(1,128)} %groups_ref.1, bf16[256,640]{1,0:T(8,128)(2,1)} %q_ref.1), custom_call_target="tpu_custom_call" | custom-call | tf_op jit(solution)/shard_map/pack/pallas_call | solution.py:70
  6.0 6.0 %collective-permute-start.13 = (bf16[272,640]{1,0:T(8,128)(2,1)}, bf16[272,640]{1,0:T(8,128)(2,1)}, u32[]{:S(2)}, u32[]{:S(2)}) collective-permute-start(bf16[272,640]{1,0:T(8,128)(2,1)} %pack.1.refs_0_), channel_id=1, source_target_pairs={{0,48},{8,56},{16,0},{24,8},{32,16},{40,24},{48,32},{56,40},{64,11... | collective-permute-start | bytes 1044488 | tf_op jit(solution)/shard_map/ppermute | solution.py:357
  12.0 0.0 collective-permute-start.2
  12.0 6.4 %collective-permute-done.refs_2_ = bf16[512,640]{1,0:T(8,128)(2,1)S(1)} collective-permute-done((bf16[512,640]{1,0:T(8,128)(2,1)S(1)}, bf16[512,640]{1,0:T(8,128)(2,1)S(1)}, u32[]{:S(2)}, u32[]{:S(2)}) %collective-permute-start) | collective-permute-done | bytes 655392 | tf_op jit(solution)/shard_map/ppermute | solution.py:357
  18.4 0.8 slice.12
  19.1 1.5 collective-permute-start.5
  20.6 0.1 stack.35
  20.7 0.0 collective-permute-done.1.refs_3_
  20.7 0.6 collective-permute-start.6
  21.3 0.0 collective-permute-start.3
  21.3 5.3 %collective-permute-done.13.refs_0_ = bf16[272,640]{1,0:T(8,128)(2,1)} collective-permute-done((bf16[272,640]{1,0:T(8,128)(2,1)}, bf16[272,640]{1,0:T(8,128)(2,1)}, u32[]{:S(2)}, u32[]{:S(2)}) %collective-permute-start.13) | collective-permute-done | bytes 348192 | tf_op jit(solution)/shard_map/ppermute | solution.py:357
  26.6 0.0 collective-permute-start.4
  26.6 1.3 collective-permute-done.5.refs_7_
  27.9 0.0 collective-permute-start.7
  27.9 0.1 iota_add_fusion
  28.0 0.0 collective-permute-done.2.refs_4_
  28.0 7.4 %collective-permute-start.11 = (bf16[272,640]{1,0:T(8,128)(2,1)}, bf16[272,640]{1,0:T(8,128)(2,1)}, u32[]{:S(2)}, u32[]{:S(2)}) collective-permute-start(bf16[272,640]{1,0:T(8,128)(2,1)} %pack.1.refs_0_), channel_id=1, source_target_pairs={{0,32},{8,40},{16,48},{24,56},{32,0},{40,8},{48,16},{56,24},{64,96... | collective-permute-start | bytes 1044488 | tf_op jit(solution)/shard_map/ppermute | solution.py:357
  35.4 0.0 collective-permute-done.6.refs_8_
  35.4 0.2 collective-permute-start.8
  35.6 0.0 copy-done.7
  35.6 0.1 add.145
  35.7 0.0 collective-permute-done.7.refs_9_
  35.7 1.6 collective-permute-start.9
  37.3 0.2 convert_reduce_fusion.page_group_ref
  37.5 0.0 collective-permute-done.8.refs_10_
  37.5 0.0 collective-permute-done.3.refs_5_
  37.5 0.0 collective-permute-done.4.refs_6_
  37.5 7.6 %attend.5 = bf16[272,640]{1,0:T(8,128)(2,1)S(1)} custom-call(s32[16]{0:T(128)S(1)} %convert_reduce_fusion.page_group_ref, bf16[272,640]{1,0:T(8,128)(2,1)} %collective-permute-done.13.refs_0_, bf16[512,640]{1,0:T(8,128)(2,1)S(1)} %bitcast.15, bf16[512,640]{1,0:T(8,128)(2,1)S(1)} %collective-permute-done.refs_2_, ...), custom_call_target="tpu_custom_call" | custom-call | flops 1342177280 | bytes 6225920 | tf_op jit(solution)/shard_map/attend/pallas_call | solution.py:203
  45.1 1.5 collective-permute-start.14
  46.5 4.4 %collective-permute-done.11.refs_0_ = bf16[272,640]{1,0:T(8,128)(2,1)} collective-permute-done((bf16[272,640]{1,0:T(8,128)(2,1)}, bf16[272,640]{1,0:T(8,128)(2,1)}, u32[]{:S(2)}, u32[]{:S(2)}) %collective-permute-start.11) | collective-permute-done | bytes 348192 | tf_op jit(solution)/shard_map/ppermute | solution.py:357
  50.9 7.7 %attend.4 = bf16[272,640]{1,0:T(8,128)(2,1)S(1)} custom-call(s32[16]{0:T(128)S(1)} %convert_reduce_fusion.page_group_ref, bf16[272,640]{1,0:T(8,128)(2,1)} %collective-permute-done.11.refs_0_, bf16[512,640]{1,0:T(8,128)(2,1)S(1)} %bitcast.16, bf16[512,640]{1,0:T(8,128)(2,1)S(1)} %collective-permute-done.refs_2_, ...), custom_call_target="tpu_custom_call" | custom-call | flops 1342177280 | bytes 6225920 | tf_op jit(solution)/shard_map/attend/pallas_call | solution.py:203
  58.6 0.0 copy-start
  58.7 0.0 copy-start.1
  58.7 0.0 copy-start.2
  58.7 0.0 slice-start.1
  58.7 7.0 %collective-permute-start.12 = (bf16[272,640]{1,0:T(8,128)(2,1)S(1)}, bf16[272,640]{1,0:T(8,128)(2,1)S(1)}, u32[]{:S(2)}, u32[]{:S(2)}) collective-permute-start(bf16[272,640]{1,0:T(8,128)(2,1)S(1)} %attend.4), channel_id=1, source_target_pairs={{0,32},{8,40},{16,48},{24,56},{32,0},{40,8},{48,16},{56,24},{64,96... | collective-permute-start | bytes 1044488 | tf_op jit(solution)/shard_map/ppermute | solution.py:357
  65.7 0.0 collective-permute-done.9.refs_0_
  65.7 7.6 %attend.3 = bf16[272,640]{1,0:T(8,128)(2,1)S(1)} custom-call(s32[16]{0:T(128)S(1)} %convert_reduce_fusion.page_group_ref, bf16[272,640]{1,0:T(8,128)(2,1)S(1)} %collective-permute-done.9.refs_0_, bf16[512,640]{1,0:T(8,128)(2,1)S(1)} %bitcast.17, bf16[512,640]{1,0:T(8,128)(2,1)S(1)} %collective-permute-done.refs_2_, ...), custom_call_target="tpu_custom_call" | custom-call | flops 1342177280 | bytes 6225920 | tf_op jit(solution)/shard_map/attend/pallas_call | solution.py:203
  73.4 0.5 collective-permute-start.10
  73.9 0.0 copy-done
  73.9 0.0 copy-done.1
  73.9 0.0 copy-done.2
  73.9 8.3 %attend_own.1 = (f32[256,640]{1,0:T(8,128)S(1)}, f32[16,256]{1,0:T(8,128)S(1)}) custom-call(s32[16]{0:T(128)S(1)} %convert_reduce_fusion.page_group_ref, bf16[272,640]{1,0:T(8,128)(2,1)S(1)} %copy-done, bf16[512,640]{1,0:T(8,128)(2,1)S(1)} %bitcast.18, bf16[512,640]{1,0:T(8,128)(2,1)S(1)} %collective-permute-done.refs_2_, ...), custom_call_target="tpu_custom_call" | custom-call | flops 1509949440 | bytes 6881280 | tf_op jit(solution)/shard_map/attend_own/pallas_call | solution.py:203
  82.1 0.0 collective-permute-done.14.n3
  82.2 0.0 collective-permute-done.12.n2
  82.2 6.2 %collective-permute-done.10.n1 = bf16[272,640]{1,0:T(8,128)(2,1)S(1)} collective-permute-done((bf16[272,640]{1,0:T(8,128)(2,1)S(1)}, bf16[272,640]{1,0:T(8,128)(2,1)S(1)}, u32[]{:S(2)}, u32[]{:S(2)}) %collective-permute-start.10) | collective-permute-done | bytes 348192 | tf_op jit(solution)/shard_map/ppermute | solution.py:357
  88.3 0.0 slice-done
  88.3 0.0 slice-done.1
  88.3 5.1 %project.1 = bf16[8,256,640]{2,1,0:T(8,128)(2,1)} custom-call(f32[256,640]{1,0:T(8,128)S(1)} %get-tuple-element.6.n0, f32[16,256]{1,0:T(8,128)S(1)} %get-tuple-element.7.s0, bf16[272,640]{1,0:T(8,128)(2,1)S(1)} %collective-permute-done.10.n1, bf16[272,640]{1,0:T(8,128)(2,1)S(1)} %collective-permute-done.12.n2, ...), custom_call_target="tpu_custom_call" | custom-call | flops 1677721600 | bytes 10158080 | tf_op jit(solution)/shard_map/project/pallas_call | solution.py:260
  93.4 21.2 %all-to-all-start = ((bf16[8,256,640]{2,1,0:T(8,128)(2,1)}), bf16[8,256,640]{2,1,0:T(8,128)(2,1)S(1)}, u32[]{:S(2)}, u32[]{:S(2)}) async-start(bf16[8,256,640]{2,1,0:T(8,128)(2,1)} %project.1), calls=%async_computation | async-start | bytes 5242880 | tf_op jit(solution)/shard_map/all_to_all | solution.py:387
  114.6 0.0 copy-done.4
  114.6 0.0 copy-start.5
  114.6 31.8 %all-to-all-done.parts_ref = bf16[8,256,640]{2,1,0:T(8,128)(2,1)S(1)} async-done(((bf16[8,256,640]{2,1,0:T(8,128)(2,1)}), bf16[8,256,640]{2,1,0:T(8,128)(2,1)S(1)}, u32[]{:S(2)}, u32[]{:S(2)}) %all-to-all-start) | async-done | bytes 2621472 | tf_op jit(solution)/shard_map/all_to_all | solution.py:387
  146.4 1.0 copy-done.3
  147.4 1.5 combine.1
  148.9 3.4 %all-to-all-start.1 = ((f32[8,8,256]{2,1,0:T(8,128)}), f32[8,8,256]{2,1,0:T(8,128)S(1)}, u32[]{:S(2)}, u32[]{:S(2)}) async-start(f32[8,8,256]{2,1,0:T(8,128)} %get-tuple-element.9), calls=%async_computation.1 | async-start | bytes 131072 | tf_op jit(solution)/shard_map/all_to_all | solution.py:389
  152.3 0.0 copy-done.5
  152.3 0.0 copy-done.6
  152.3 6.2 %all-to-all-done.1.sums_ref = f32[8,8,256]{2,1,0:T(8,128)S(1)} async-done(((f32[8,8,256]{2,1,0:T(8,128)}), f32[8,8,256]{2,1,0:T(8,128)S(1)}, u32[]{:S(2)}, u32[]{:S(2)}) %all-to-all-start.1) | async-done | bytes 65568 | tf_op jit(solution)/shard_map/all_to_all | solution.py:389
  158.6 1.1 finish.1
  (11 shorter events, 0.1 us)
Async XLA Ops:
  0.6 35.0 %copy-start.7 = (s32[2,32]{1,0:T(2,128)S(1)}, s32[2,32]{1,0:T(2,128)}, u32[]{:S(2)}) copy-start(s32[2,32]{1,0:T(2,128)} %param.16) | copy-start | bytes 772
  1.8 16.6 %collective-permute-start = (bf16[512,640]{1,0:T(8,128)(2,1)S(1)}, bf16[512,640]{1,0:T(8,128)(2,1)S(1)}, u32[]{:S(2)}, u32[]{:S(2)}) collective-permute-start(bf16[512,640]{1,0:T(8,128)(2,1)S(1)} %bitcast.12), channel_id=1, source_target_pairs={{0,64},{8,72},{16,80},{24,88},{32,96},{40,104},{48,112},{56,120},{... | collective-permute-start | bytes 1966088 | tf_op jit(solution)/shard_map/ppermute | solution.py:357
  3.4 17.3 %collective-permute-start.1 = (bf16[512,640]{1,0:T(8,128)(2,1)S(1)}, bf16[512,640]{1,0:T(8,128)(2,1)S(1)}, u32[]{:S(2)}, u32[]{:S(2)}) collective-permute-start(bf16[512,640]{1,0:T(8,128)(2,1)S(1)} %bitcast.13), channel_id=1, source_target_pairs={{0,192},{8,200},{16,208},{24,216},{32,224},{40,232},{48,240},{56,2... | collective-permute-start | bytes 1966088 | tf_op jit(solution)/shard_map/ppermute | solution.py:357
  6.0 20.7 %collective-permute-start.13 = (bf16[272,640]{1,0:T(8,128)(2,1)}, bf16[272,640]{1,0:T(8,128)(2,1)}, u32[]{:S(2)}, u32[]{:S(2)}) collective-permute-start(bf16[272,640]{1,0:T(8,128)(2,1)} %pack.1.refs_0_), channel_id=1, source_target_pairs={{0,48},{8,56},{16,0},{24,8},{32,16},{40,24},{48,32},{56,40},{64,11... | collective-permute-start | bytes 1044488 | tf_op jit(solution)/shard_map/ppermute | solution.py:357
  12.0 16.0 %collective-permute-start.2 = (bf16[512,640]{1,0:T(8,128)(2,1)S(1)}, bf16[512,640]{1,0:T(8,128)(2,1)S(1)}, u32[]{:S(2)}, u32[]{:S(2)}) collective-permute-start(bf16[512,640]{1,0:T(8,128)(2,1)S(1)} %bitcast.14), channel_id=1, source_target_pairs={{0,8},{8,0},{16,24},{24,16},{32,40},{40,32},{48,56},{56,48},{64,72... | collective-permute-start | bytes 1966088 | tf_op jit(solution)/shard_map/ppermute | solution.py:357
  19.1 8.8 %collective-permute-start.5 = (bf16[256,640]{1,0:T(8,128)(2,1)}, bf16[256,640]{1,0:T(8,128)(2,1)}, u32[]{:S(2)}, u32[]{:S(2)}) collective-permute-start(bf16[256,640]{1,0:T(8,128)(2,1)} %slice.12), channel_id=1, source_target_pairs={{0,64},{8,72},{16,80},{24,88},{32,96},{40,104},{48,112},{56,120},{... | collective-permute-start | bytes 983048 | tf_op jit(solution)/shard_map/ppermute | solution.py:357
  20.7 14.7 %collective-permute-start.6 = (bf16[256,640]{1,0:T(8,128)(2,1)S(1)}, bf16[256,640]{1,0:T(8,128)(2,1)}, u32[]{:S(2)}, u32[]{:S(2)}) collective-permute-start(bf16[256,640]{1,0:T(8,128)(2,1)S(1)} %slice.13), channel_id=1, source_target_pairs={{0,192},{8,200},{16,208},{24,216},{32,224},{40,232},{48,240},{56,2... | collective-permute-start | bytes 983048 | tf_op jit(solution)/shard_map/ppermute | solution.py:357
  21.3 16.1 %collective-permute-start.3 = (bf16[512,640]{1,0:T(8,128)(2,1)S(1)}, bf16[512,640]{1,0:T(8,128)(2,1)S(1)}, u32[]{:S(2)}, u32[]{:S(2)}) collective-permute-start(bf16[512,640]{1,0:T(8,128)(2,1)S(1)} %collective-permute-done.refs_2_), channel_id=1, source_target_pairs={{0,8},{8,0},{16,24},{24,16},{32,40},{40,32},{48,56},{56,48},{64,72... | collective-permute-start | bytes 1966088 | tf_op jit(solution)/shard_map/ppermute | solution.py:357
  26.6 10.8 %collective-permute-start.4 = (bf16[512,640]{1,0:T(8,128)(2,1)S(1)}, bf16[512,640]{1,0:T(8,128)(2,1)}, u32[]{:S(2)}, u32[]{:S(2)}) collective-permute-start(bf16[512,640]{1,0:T(8,128)(2,1)S(1)} %collective-permute-done.1.refs_3_), channel_id=1, source_target_pairs={{0,8},{8,0},{16,24},{24,16},{32,40},{40,32},{48,56},{56,48},{64,72... | collective-permute-start | bytes 1966088 | tf_op jit(solution)/shard_map/ppermute | solution.py:357
  27.9 7.8 %collective-permute-start.7 = (bf16[256,640]{1,0:T(8,128)(2,1)}, bf16[256,640]{1,0:T(8,128)(2,1)}, u32[]{:S(2)}, u32[]{:S(2)}) collective-permute-start(bf16[256,640]{1,0:T(8,128)(2,1)} %collective-permute-done.5.refs_7_), channel_id=1, source_target_pairs={{0,8},{8,0},{16,24},{24,16},{32,40},{40,32},{48,56},{56,48},{64,72... | collective-permute-start | bytes 983048 | tf_op jit(solution)/shard_map/ppermute | solution.py:357
  28.0 22.9 %collective-permute-start.11 = (bf16[272,640]{1,0:T(8,128)(2,1)}, bf16[272,640]{1,0:T(8,128)(2,1)}, u32[]{:S(2)}, u32[]{:S(2)}) collective-permute-start(bf16[272,640]{1,0:T(8,128)(2,1)} %pack.1.refs_0_), channel_id=1, source_target_pairs={{0,32},{8,40},{16,48},{24,56},{32,0},{40,8},{48,16},{56,24},{64,96... | collective-permute-start | bytes 1044488 | tf_op jit(solution)/shard_map/ppermute | solution.py:357
  35.4 2.0 %collective-permute-start.8 = (bf16[256,640]{1,0:T(8,128)(2,1)}, bf16[256,640]{1,0:T(8,128)(2,1)}, u32[]{:S(2)}, u32[]{:S(2)}) collective-permute-start(bf16[256,640]{1,0:T(8,128)(2,1)} %collective-permute-done.6.refs_8_), channel_id=1, source_target_pairs={{0,8},{8,0},{16,24},{24,16},{32,40},{40,32},{48,56},{56,48},{64,72... | collective-permute-start | bytes 983048 | tf_op jit(solution)/shard_map/ppermute | solution.py:357
  35.7 30.0 %collective-permute-start.9 = (bf16[272,640]{1,0:T(8,128)(2,1)}, bf16[272,640]{1,0:T(8,128)(2,1)S(1)}, u32[]{:S(2)}, u32[]{:S(2)}) collective-permute-start(bf16[272,640]{1,0:T(8,128)(2,1)} %pack.1.refs_0_), channel_id=1, source_target_pairs={{0,16},{8,24},{16,32},{24,40},{32,48},{40,56},{48,0},{56,8},{64,80... | collective-permute-start | bytes 1044488 | tf_op jit(solution)/shard_map/ppermute | solution.py:357
  45.1 37.1 %collective-permute-start.14 = (bf16[272,640]{1,0:T(8,128)(2,1)S(1)}, bf16[272,640]{1,0:T(8,128)(2,1)S(1)}, u32[]{:S(2)}, u32[]{:S(2)}) collective-permute-start(bf16[272,640]{1,0:T(8,128)(2,1)S(1)} %attend.5), channel_id=1, source_target_pairs={{0,16},{8,24},{16,32},{24,40},{32,48},{40,56},{48,0},{56,8},{64,80... | collective-permute-start | bytes 1044488 | tf_op jit(solution)/shard_map/ppermute | solution.py:357
  50.9 37.4 %slice-start = ((s8[6553600]{0:T(1024)(128)(4,1)}), s8[4194304]{0:T(1024)(128)(4,1)S(1)}, s32[]{:S(2)}) async-start(s8[6553600]{0:T(1024)(128)(4,1)} %bitcast.19), calls=%async_computation.2 | async-start | bytes 8388608
  58.6 15.2 %copy-start = (bf16[272,640]{1,0:T(8,128)(2,1)S(1)}, bf16[272,640]{1,0:T(8,128)(2,1)}, u32[]{:S(2)}) copy-start(bf16[272,640]{1,0:T(8,128)(2,1)} %pack.1.refs_0_) | copy-start | bytes 1044484
  58.7 15.2 %copy-start.1 = (bf16[256,640]{1,0:T(8,128)(2,1)S(1)}, bf16[256,640]{1,0:T(8,128)(2,1)}, u32[]{:S(2)}) copy-start(bf16[256,640]{1,0:T(8,128)(2,1)} %refs_11_.1) | copy-start | bytes 983044
  58.7 15.2 %copy-start.2 = (bf16[256,640]{1,0:T(8,128)(2,1)S(1)}, bf16[256,640]{1,0:T(8,128)(2,1)}, u32[]{:S(2)}) copy-start(bf16[256,640]{1,0:T(8,128)(2,1)} %refs_12_.1) | copy-start | bytes 983044
  58.7 29.6 %slice-start.1 = ((s8[6553600]{0:T(1024)(128)(4,1)}), s8[2359296]{0:T(1024)(128)(4,1)S(1)}, s32[]{:S(2)}) async-start(s8[6553600]{0:T(1024)(128)(4,1)} %bitcast.19), calls=%async_computation.3 | async-start | bytes 4718592
  58.7 23.5 %collective-permute-start.12 = (bf16[272,640]{1,0:T(8,128)(2,1)S(1)}, bf16[272,640]{1,0:T(8,128)(2,1)S(1)}, u32[]{:S(2)}, u32[]{:S(2)}) collective-permute-start(bf16[272,640]{1,0:T(8,128)(2,1)S(1)} %attend.4), channel_id=1, source_target_pairs={{0,32},{8,40},{16,48},{24,56},{32,0},{40,8},{48,16},{56,24},{64,96... | collective-permute-start | bytes 1044488 | tf_op jit(solution)/shard_map/ppermute | solution.py:357
  73.4 14.9 %collective-permute-start.10 = (bf16[272,640]{1,0:T(8,128)(2,1)S(1)}, bf16[272,640]{1,0:T(8,128)(2,1)S(1)}, u32[]{:S(2)}, u32[]{:S(2)}) collective-permute-start(bf16[272,640]{1,0:T(8,128)(2,1)S(1)} %attend.3), channel_id=1, source_target_pairs={{0,48},{8,56},{16,0},{24,8},{32,16},{40,24},{48,32},{56,40},{64,11... | collective-permute-start | bytes 1044488 | tf_op jit(solution)/shard_map/ppermute | solution.py:357
  93.4 21.2 %copy-start.4 = (f32[640]{0:T(1024)S(1)}, f32[640]{0:T(1024)}, u32[]{:S(2)}) copy-start(f32[640]{0:T(1024)} %param.21) | copy-start | bytes 7684
  93.4 58.9 %copy-start.6 = (f32[640]{0:T(1024)S(1)}, f32[640]{0:T(1024)}, u32[]{:S(2)}) copy-start(f32[640]{0:T(1024)} %param.23) | copy-start | bytes 7684
  93.4 53.0 %all-to-all-start = ((bf16[8,256,640]{2,1,0:T(8,128)(2,1)}), bf16[8,256,640]{2,1,0:T(8,128)(2,1)S(1)}, u32[]{:S(2)}, u32[]{:S(2)}) async-start(bf16[8,256,640]{2,1,0:T(8,128)(2,1)} %project.1), calls=%async_computation | async-start | bytes 5242880 | tf_op jit(solution)/shard_map/all_to_all | solution.py:387
  114.6 37.7 %copy-start.5 = (f32[640]{0:T(1024)S(1)}, f32[640]{0:T(1024)}, u32[]{:S(2)}) copy-start(f32[640]{0:T(1024)} %param.22) | copy-start | bytes 7684
  146.4 1.0 copy-start.3
  148.9 9.6 %all-to-all-start.1 = ((f32[8,8,256]{2,1,0:T(8,128)}), f32[8,8,256]{2,1,0:T(8,128)S(1)}, u32[]{:S(2)}, u32[]{:S(2)}) async-start(f32[8,8,256]{2,1,0:T(8,128)} %get-tuple-element.9), calls=%async_computation.1 | async-start | bytes 131072 | tf_op jit(solution)/shard_map/all_to_all | solution.py:389

commit v3 on v2

--- a/solution.py
+++ b/solution.py
@@ -54,31 +54,9 @@
     return request, block, group
 
 
-def pack_kernel(lens_ref, groups_ref, q_ref, out_ref):
-    width = q_ref.shape[1]
-    out_ref[0:TOK, :] = q_ref[...]
-    lane = lax.broadcasted_iota(jnp.int32, (16, width), 1)
-    facts = jnp.zeros((16, width), jnp.int32)
-    for i in range(4):
-        facts = jnp.where(lane == i, lens_ref[0, i], facts)
-        facts = jnp.where(lane == 4 + i, groups_ref[0, i], facts)
-    out_ref[TOK : TOK + 16, :] = facts.astype(jnp.float32).astype(jnp.bfloat16)
-
-
-def pack(lens, groups, queries):
-    smem = pl.BlockSpec(memory_space=pltpu.SMEM)
-    return pl.pallas_call(
-        pack_kernel,
-        name="pack",
-        in_specs=[smem, smem, pl.BlockSpec(memory_space=pltpu.VMEM)],
-        out_specs=pl.BlockSpec(memory_space=pltpu.VMEM),
-        out_shape=jax.ShapeDtypeStruct((TOK + 16, queries.shape[1]), queries.dtype),
-    )(lens, groups, queries)
-
-
 def features(own, facts, page_group_ref, feat, kfeat):
     wide = (TOK, HS)
-    request, block, group = token_facts(facts.astype(jnp.float32)[0:1, :], wide)
+    request, block, group = token_facts(facts, wide)
     lane = lax.broadcasted_iota(jnp.int32, wide, 1)
     row = lax.broadcasted_iota(jnp.int32, wide, 0)
     feat[0] = jnp.where(lane == group, 1.0, 0.0).astype(jnp.bfloat16)
@@ -121,8 +99,7 @@
     return total[:, :HS], total[:, HS:]
 
 
-def attend_kernel(own, pieces, page_group_ref, *refs):
-    q_refs, refs = refs[:pieces], refs[pieces:]
+def attend_kernel(own, page_group_ref, facts_ref, q_ref, *refs):
     kv_refs, refs = refs[:10], refs[10:]
     suffix, refs = (refs[:2], refs[2:]) if own else ((), refs)
     if own:
@@ -134,8 +111,7 @@
 
     @pl.when(head == 0)
     def _():
-        facts = q_refs[-1][TOK // pieces : TOK // pieces + 16, :]
-        features(own, facts, page_group_ref, feat, kfeat)
+        features(own, facts_ref[...].astype(jnp.float32), page_group_ref, feat, kfeat)
         ml[...] = jnp.zeros_like(ml)
 
     def rows(start):
@@ -148,10 +124,7 @@
 
     @pl.when(page_group_ref[0] >= 0)
     def _():
-        if pieces == 1:
-            query = q_refs[0][0:TOK, :]
-        else:
-            query = jnp.concatenate([q_refs[0][...], q_refs[1][0:128, :]], axis=0)
+        query = q_ref[...]
         keys = rows(0) + [r[...] for r in suffix[:1]]
         top[...] = score_pass(query, keys, [0] * 8 + [1], feat, kfeat, scores)
 
@@ -182,7 +155,7 @@
             num_ref[TOK : TOK + 16, :] = jnp.concatenate([high, middle, low], axis=1)
 
 
-def attend(page_group, query, blocks, suffix=()):
+def attend(page_group, facts, query, blocks, suffix=()):
     own = bool(suffix)
     count = 9 if own else 8
     width = HEADS_DEV * HS
@@ -199,15 +172,16 @@
     else:
         out_shape = jax.ShapeDtypeStruct((TOK + 16, width), jnp.bfloat16)
         out_specs = pl.BlockSpec((TOK + 16, width), lambda h, *_: (0, 0))
-    operands = (*query, *blocks, *suffix)
+    operands = (query, *blocks, *suffix)
     return pl.pallas_call(
-        functools.partial(attend_kernel, own, len(query)),
+        functools.partial(attend_kernel, own),
         name="attend_own" if own else "attend",
         out_shape=out_shape,
         grid_spec=pltpu.PrefetchScalarGridSpec(
             num_scalar_prefetch=1,
             grid=(HEADS_DEV,),
-            in_specs=[tall(array) for array in operands],
+            in_specs=[pl.BlockSpec((1, 8), lambda h, *_: (0, 0))]
+            + [tall(array) for array in operands],
             out_specs=out_specs,
             scratch_shapes=[
                 pltpu.VMEM((2, TOK, HS), jnp.bfloat16),
@@ -223,7 +197,7 @@
             bytes_accessed=2 * TOK * HS * HEADS_DEV * (2 * count + 3),
             transcendentals=TOK * TOK * count * HEADS_DEV,
         ),
-    )(page_group, *operands)
+    )(page_group, facts, *operands)
 
 
 def project_kernel(n0, s0, n1, n2, n3, w_ref, out_ref, att):
@@ -356,10 +330,10 @@
     width = queries.shape[1]
     send = lambda array, dx, dz, dc: lax.ppermute(array, "req", shift(dx, dz, dc))
 
-    query = pack(suffix_lengths, request_group, queries)
-    below = send(query, 0, 1, 0)
-    above = send(query, 0, -1, 0)
-    opposite = send(query, 0, 2, 0)
+    ways = (1, -1, 2)
+    facts = jnp.concatenate([suffix_lengths, request_group], axis=1)
+    their_query = [send(queries, 0, dz, 0) for dz in ways]
+    their_facts = [send(facts, 0, dz, 0) for dz in ways]
 
     pages = page_cache.transpose(0, 2, 1, 3).reshape(2 * TOK, width)
     left, right = send(pages, 1, 0, 0), send(pages, -1, 0, 0)
@@ -379,10 +353,10 @@
 
     suffix = (suffix_keys, suffix_values)
     others = []
-    for block, dz in ((below, 1), (opposite, 2), (above, -1)):
-        num = attend(page_group, (block,), blocks)
+    for i, dz in enumerate(ways):
+        num = attend(page_group, their_facts[i], their_query[i], blocks)
         others.append(send(num, 0, -dz, 0))
-    num, ml = attend(page_group, (query,), blocks, suffix)
+    num, ml = attend(page_group, facts, queries, blocks, suffix)
     parts = project(num, ml, others, out_weight)
     parts = lax.all_to_all(parts, "tp", 0, 0, tiled=True)
     combined, sums = combine(parts, residual, attn_gate[None, :])

time: 163 us -> 146 us (0.90)
  starting transfers between devices: 53.3 us -> 43.7 us
  waiting for transfers between devices: 61.5 us -> 56.2 us
  Pallas kernels: 40.7 us -> 39 us
    all_to_all x1, starting transfers between devices: 21.2 us -> 4.6 us  [body(): parts = lax.all_to_all(parts, 'tp', 0, 0, tiled=True)]
    ppermute x15 -> x18, starting transfers between devices: 28.7 us -> 35.7 us  [body(): lax.ppermute(array, 'req', shift(dx, dz, dc))]
    ppermute x15 -> x18, waiting for transfers between devices: 23.5 us -> 18.2 us  [body(): lax.ppermute(array, 'req', shift(dx, dz, dc))]
    pallas_call x5 -> x4, Pallas kernels: 33 us -> 31.2 us  [attend(): pl.pallas_call(functools.partial(attend_kernel, own), name='attend_own' i...]
  transfers between devices with their start and end apart: 17 -> 20, of which waited for: 7 -> 7; matrix products, arithmetic and copies ran while one was open for 1% -> 1% of each run, Pallas kernels for 21% -> 22%
where the time goes in v3:
time: 146 us; the launch traced here: 144 us
  waiting for transfers between devices  56.2 us (38%)
  starting transfers between devices  43.7 us (30%)
  Pallas kernels  39 us (27%)
  local copies, waits for them, and re-layouts  3.15 us (2%)
    ppermute x18, starting transfers between devices, body(): lax.ppermute(array, 'req', shift(dx, dz, dc))  35.7 us
    all_to_all x1, waiting for transfers between devices, body(): parts = lax.all_to_all(parts, 'tp', 0, 0, tiled=True)  31.7 us
    pallas_call x4, Pallas kernels, attend(): pl.pallas_call(functools.partial(attend_kernel, own), name='attend_own' i...  31.2 us
    ppermute x18, waiting for transfers between devices, body(): lax.ppermute(array, 'req', shift(dx, dz, dc))  18.2 us
    all_to_all x1, waiting for transfers between devices, body(): sums = lax.all_to_all(sums, 'tp', 0, 0, tiled=True)  6.23 us
    pallas_call x1, Pallas kernels, project(): pl.pallas_call(project_kernel, name='project', out_shape=pltpu.HBM((8, TO...  5.06 us
    all_to_all x1, starting transfers between devices, body(): parts = lax.all_to_all(parts, 'tp', 0, 0, tiled=True)  4.6 us
    all_to_all x1, starting transfers between devices, body(): sums = lax.all_to_all(sums, 'tp', 0, 0, tiled=True)  3.35 us
  transfers between devices with their start and end apart: 20, of which 7 were waited for; matrix products, arithmetic and copies ran while one was open for 1% of the time, Pallas kernels for 22%

profile of v3, /device:TPU:2, one launch (start us, length us, event | category | flops | bytes accessed | tf_op | source)
XLA Modules:
  0.0 143.8 jit_solution(687152850841553950)
XLA Ops:
  0.6 1.2 copy.16
  1.8 1.6 %collective-permute-start = (bf16[512,640]{1,0:T(8,128)(2,1)S(1)}, bf16[512,640]{1,0:T(8,128)(2,1)S(1)}, u32[]{:S(2)}, u32[]{:S(2)}) collective-permute-start(bf16[512,640]{1,0:T(8,128)(2,1)S(1)} %bitcast.12), channel_id=1, source_target_pairs={{0,64},{8,72},{16,80},{24,88},{32,96},{40,104},{48,112},{56,120},{... | collective-permute-start | bytes 1966088 | tf_op jit(solution)/shard_map/ppermute | solution.py:331
  3.4 0.8 collective-permute-start.1
  4.2 6.9 %collective-permute-start.16 = (bf16[256,640]{1,0:T(8,128)(2,1)}, bf16[256,640]{1,0:T(8,128)(2,1)}, u32[]{:S(2)}, u32[]{:S(2)}) collective-permute-start(bf16[256,640]{1,0:T(8,128)(2,1)} %q_ref.1), channel_id=1, source_target_pairs={{0,32},{8,40},{16,48},{24,56},{32,0},{40,8},{48,16},{56,24},{64,96... | collective-permute-start | bytes 983048 | tf_op jit(solution)/shard_map/ppermute | solution.py:331
  11.1 0.0 collective-permute-start.2
  11.1 7.3 %collective-permute-done.refs_1_ = bf16[512,640]{1,0:T(8,128)(2,1)S(1)} collective-permute-done((bf16[512,640]{1,0:T(8,128)(2,1)S(1)}, bf16[512,640]{1,0:T(8,128)(2,1)S(1)}, u32[]{:S(2)}, u32[]{:S(2)}) %collective-permute-start) | collective-permute-done | bytes 655392 | tf_op jit(solution)/shard_map/ppermute | solution.py:331
  18.4 0.8 slice.12
  19.1 1.5 %collective-permute-start.5 = (bf16[256,640]{1,0:T(8,128)(2,1)}, bf16[256,640]{1,0:T(8,128)(2,1)}, u32[]{:S(2)}, u32[]{:S(2)}) collective-permute-start(bf16[256,640]{1,0:T(8,128)(2,1)} %slice.12), channel_id=1, source_target_pairs={{0,64},{8,72},{16,80},{24,88},{32,96},{40,104},{48,112},{56,120},{... | collective-permute-start | bytes 983048 | tf_op jit(solution)/shard_map/ppermute | solution.py:331
  20.6 0.7 pad_add_fusion.facts_ref
  21.4 7.2 %collective-permute-start.15 = (s32[1,8]{1,0:T(1,128)S(1)}, s32[1,8]{1,0:T(1,128)S(1)}, u32[]{:S(2)}, u32[]{:S(2)}) collective-permute-start(s32[1,8]{1,0:T(1,128)S(1)} %pad_add_fusion.facts_ref), channel_id=1, source_target_pairs={{0,32},{8,40},{16,48},{24,56},{32,0},{40,8},{48,16},{56,24},{64,96... | collective-permute-start | bytes 104 | tf_op jit(solution)/shard_map/ppermute | solution.py:331
  28.5 0.1 stack.35
  28.6 0.0 collective-permute-done.1.refs_2_
  28.7 0.6 collective-permute-start.6
  29.3 0.8 collective-permute-done.15.facts_ref
  30.1 0.0 collective-permute-start.3
  30.1 0.0 collective-permute-done.16.q_ref
  30.1 0.5 collective-permute-start.4
  30.6 0.0 collective-permute-done.5.refs_6_
  30.6 0.1 collective-permute-start.7
  30.7 0.1 iota_add_fusion
  30.8 0.0 collective-permute-done.2.refs_3_
  30.8 5.0 %collective-permute-start.13 = (bf16[256,640]{1,0:T(8,128)(2,1)}, bf16[256,640]{1,0:T(8,128)(2,1)}, u32[]{:S(2)}, u32[]{:S(2)}) collective-permute-start(bf16[256,640]{1,0:T(8,128)(2,1)} %q_ref.1), channel_id=1, source_target_pairs={{0,48},{8,56},{16,0},{24,8},{32,16},{40,24},{48,32},{56,40},{64,11... | collective-permute-start | bytes 983048 | tf_op jit(solution)/shard_map/ppermute | solution.py:331
  35.8 1.2 collective-permute-done.6.refs_7_
  37.0 0.0 collective-permute-start.8
  37.0 0.0 copy-done.7
  37.0 0.1 add.145
  37.1 0.0 collective-permute-done.7.refs_8_
  37.1 1.5 %collective-permute-start.10 = (bf16[256,640]{1,0:T(8,128)(2,1)}, bf16[256,640]{1,0:T(8,128)(2,1)S(1)}, u32[]{:S(2)}, u32[]{:S(2)}) collective-permute-start(bf16[256,640]{1,0:T(8,128)(2,1)} %q_ref.1), channel_id=1, source_target_pairs={{0,16},{8,24},{16,32},{24,40},{32,48},{40,56},{48,0},{56,8},{64,80... | collective-permute-start | bytes 983048 | tf_op jit(solution)/shard_map/ppermute | solution.py:331
  38.6 0.2 convert_reduce_fusion.page_group_ref
  38.8 0.1 collective-permute-done.8.refs_9_
  39.0 2.6 %collective-permute-start.12 = (s32[1,8]{1,0:T(1,128)S(1)}, s32[1,8]{1,0:T(1,128)S(1)}, u32[]{:S(2)}, u32[]{:S(2)}) collective-permute-start(s32[1,8]{1,0:T(1,128)S(1)} %pad_add_fusion.facts_ref), channel_id=1, source_target_pairs={{0,48},{8,56},{16,0},{24,8},{32,16},{40,24},{48,32},{56,40},{64,11... | collective-permute-start | bytes 104 | tf_op jit(solution)/shard_map/ppermute | solution.py:331
  41.6 0.0 collective-permute-done.3.refs_4_
  41.6 0.3 collective-permute-start.9
  41.9 0.0 collective-permute-done.4.refs_5_
  41.9 7.6 %attend.5 = bf16[272,640]{1,0:T(8,128)(2,1)S(1)} custom-call(s32[16]{0:T(128)S(1)} %convert_reduce_fusion.page_group_ref, s32[1,8]{1,0:T(1,128)S(1)} %collective-permute-done.15.facts_ref, bf16[256,640]{1,0:T(8,128)(2,1)} %collective-permute-done.16.q_ref, bf16[512,640]{1,0:T(8,128)(2,1)S(1)} %bitcast.15, bf16[512,640]{1,0:T(8,128)(2,1)S(1)} %collective-permute-done.refs_1_, ...), custom_call_target="tpu_custom_call" | custom-call | flops 1342177280 | bytes 6225920 | tf_op jit(solution)/shard_map/attend/pallas_call | solution.py:176
  49.5 2.7 %collective-permute-start.17 = (bf16[272,640]{1,0:T(8,128)(2,1)S(1)}, bf16[272,640]{1,0:T(8,128)(2,1)S(1)}, u32[]{:S(2)}, u32[]{:S(2)}) collective-permute-start(bf16[272,640]{1,0:T(8,128)(2,1)S(1)} %attend.5), channel_id=1, source_target_pairs={{0,32},{8,40},{16,48},{24,56},{32,0},{40,8},{48,16},{56,24},{64,96... | collective-permute-start | bytes 1044488 | tf_op jit(solution)/shard_map/ppermute | solution.py:331
  52.2 0.0 collective-permute-done.12.facts_ref
  52.2 0.0 collective-permute-done.13.q_ref
  52.2 7.8 %attend.4 = bf16[272,640]{1,0:T(8,128)(2,1)S(1)} custom-call(s32[16]{0:T(128)S(1)} %convert_reduce_fusion.page_group_ref, s32[1,8]{1,0:T(1,128)S(1)} %collective-permute-done.12.facts_ref, bf16[256,640]{1,0:T(8,128)(2,1)} %collective-permute-done.13.q_ref, bf16[512,640]{1,0:T(8,128)(2,1)S(1)} %bitcast.16, bf16[512,640]{1,0:T(8,128)(2,1)S(1)} %collective-permute-done.refs_1_, ...), custom_call_target="tpu_custom_call" | custom-call | flops 1342177280 | bytes 6225920 | tf_op jit(solution)/shard_map/attend/pallas_call | solution.py:176
  59.9 0.0 copy-start
  60.0 0.0 copy-start.1
  60.0 0.0 copy-start.2
  60.0 0.0 slice-start.1
  60.0 3.8 %collective-permute-start.14 = (bf16[272,640]{1,0:T(8,128)(2,1)S(1)}, bf16[272,640]{1,0:T(8,128)(2,1)S(1)}, u32[]{:S(2)}, u32[]{:S(2)}) collective-permute-start(bf16[272,640]{1,0:T(8,128)(2,1)S(1)} %attend.4), channel_id=1, source_target_pairs={{0,16},{8,24},{16,32},{24,40},{32,48},{40,56},{48,0},{56,8},{64,80... | collective-permute-start | bytes 1044488 | tf_op jit(solution)/shard_map/ppermute | solution.py:331
  63.8 0.0 collective-permute-done.9.facts_ref
  63.8 0.0 collective-permute-done.10.q_ref
  63.8 7.6 %attend.3 = bf16[272,640]{1,0:T(8,128)(2,1)S(1)} custom-call(s32[16]{0:T(128)S(1)} %convert_reduce_fusion.page_group_ref, s32[1,8]{1,0:T(1,128)S(1)} %collective-permute-done.9.facts_ref, bf16[256,640]{1,0:T(8,128)(2,1)S(1)} %collective-permute-done.10.q_ref, bf16[512,640]{1,0:T(8,128)(2,1)S(1)} %bitcast.17, ...), custom_call_target="tpu_custom_call" | custom-call | flops 1342177280 | bytes 6225920 | tf_op jit(solution)/shard_map/attend/pallas_call | solution.py:176
  71.5 0.5 collective-permute-start.11
  72.0 8.3 %attend_own.1 = (f32[256,640]{1,0:T(8,128)S(1)}, f32[16,256]{1,0:T(8,128)S(1)}) custom-call(s32[16]{0:T(128)S(1)} %convert_reduce_fusion.page_group_ref, s32[1,8]{1,0:T(1,128)S(1)} %pad_add_fusion.facts_ref, bf16[256,640]{1,0:T(8,128)(2,1)S(1)} %copy-done, bf16[512,640]{1,0:T(8,128)(2,1)S(1)} %bitcast.18, bf16[512,640]{1,0:T(8,128)(2,1)S(1)} %collective-permute-done.refs_1_, ...), custom_call_target="tpu_custom_call" | custom-call | flops 1509949440 | bytes 6881280 | tf_op jit(solution)/shard_map/attend_own/pallas_call | solution.py:176
  80.2 0.0 collective-permute-done.17.n3
  80.2 0.0 collective-permute-done.14.n2
  80.3 8.8 %collective-permute-done.11.n1 = bf16[272,640]{1,0:T(8,128)(2,1)S(1)} collective-permute-done((bf16[272,640]{1,0:T(8,128)(2,1)S(1)}, bf16[272,640]{1,0:T(8,128)(2,1)S(1)}, u32[]{:S(2)}, u32[]{:S(2)}) %collective-permute-start.11) | collective-permute-done | bytes 348192 | tf_op jit(solution)/shard_map/ppermute | solution.py:331
  89.1 0.0 slice-done.1
  89.1 5.1 %project.1 = bf16[8,256,640]{2,1,0:T(8,128)(2,1)} custom-call(f32[256,640]{1,0:T(8,128)S(1)} %get-tuple-element.6.n0, f32[16,256]{1,0:T(8,128)S(1)} %get-tuple-element.7.s0, bf16[272,640]{1,0:T(8,128)(2,1)S(1)} %collective-permute-done.11.n1, bf16[272,640]{1,0:T(8,128)(2,1)S(1)} %collective-permute-done.14.n2, ...), custom_call_target="tpu_custom_call" | custom-call | flops 1677721600 | bytes 10158080 | tf_op jit(solution)/shard_map/project/pallas_call | solution.py:234
  94.2 4.6 %all-to-all-start = ((bf16[8,256,640]{2,1,0:T(8,128)(2,1)}), bf16[8,256,640]{2,1,0:T(8,128)(2,1)S(1)}, u32[]{:S(2)}, u32[]{:S(2)}) async-start(bf16[8,256,640]{2,1,0:T(8,128)(2,1)} %project.1), calls=%async_computation | async-start | bytes 5242880 | tf_op jit(solution)/shard_map/all_to_all | solution.py:361
  98.8 0.0 copy-start.5
  98.8 31.7 %all-to-all-done.parts_ref = bf16[8,256,640]{2,1,0:T(8,128)(2,1)S(1)} async-done(((bf16[8,256,640]{2,1,0:T(8,128)(2,1)}), bf16[8,256,640]{2,1,0:T(8,128)(2,1)S(1)}, u32[]{:S(2)}, u32[]{:S(2)}) %all-to-all-start) | async-done | bytes 2621472 | tf_op jit(solution)/shard_map/all_to_all | solution.py:361
  130.5 1.0 copy-done.3
  131.5 1.5 %combine.1 = (f32[256,640]{1,0:T(8,128)S(1)}, f32[8,8,256]{2,1,0:T(8,128)}) custom-call(bf16[8,256,640]{2,1,0:T(8,128)(2,1)S(1)} %all-to-all-done.parts_ref, bf16[256,640]{1,0:T(8,128)(2,1)S(1)} %copy-done.3, f32[1,640]{1,0:T(1,128)S(1)} %broadcast_in_dim.11.gate_ref), custom_call_target="tpu_custom_call" | custom-call | tf_op jit(solution)/shard_map/combine/pallas_call | solution.py:270
  133.0 3.4 %all-to-all-start.1 = ((f32[8,8,256]{2,1,0:T(8,128)}), f32[8,8,256]{2,1,0:T(8,128)S(1)}, u32[]{:S(2)}, u32[]{:S(2)}) async-start(f32[8,8,256]{2,1,0:T(8,128)} %get-tuple-element.9), calls=%async_computation.1 | async-start | bytes 131072 | tf_op jit(solution)/shard_map/all_to_all | solution.py:363
  136.4 0.0 copy-done.5
  136.4 0.0 copy-done.6
  136.4 6.2 %all-to-all-done.1.sums_ref = f32[8,8,256]{2,1,0:T(8,128)S(1)} async-done(((f32[8,8,256]{2,1,0:T(8,128)}), f32[8,8,256]{2,1,0:T(8,128)S(1)}, u32[]{:S(2)}, u32[]{:S(2)}) %all-to-all-start.1) | async-done | bytes 65568 | tf_op jit(solution)/shard_map/all_to_all | solution.py:363
  142.7 1.1 finish.1
  (17 shorter events, 0.1 us)
Async XLA Ops:
  0.6 36.4 %copy-start.7 = (s32[2,32]{1,0:T(2,128)S(1)}, s32[2,32]{1,0:T(2,128)}, u32[]{:S(2)}) copy-start(s32[2,32]{1,0:T(2,128)} %param.16) | copy-start | bytes 772
  1.8 16.6 %collective-permute-start = (bf16[512,640]{1,0:T(8,128)(2,1)S(1)}, bf16[512,640]{1,0:T(8,128)(2,1)S(1)}, u32[]{:S(2)}, u32[]{:S(2)}) collective-permute-start(bf16[512,640]{1,0:T(8,128)(2,1)S(1)} %bitcast.12), channel_id=1, source_target_pairs={{0,64},{8,72},{16,80},{24,88},{32,96},{40,104},{48,112},{56,120},{... | collective-permute-start | bytes 1966088 | tf_op jit(solution)/shard_map/ppermute | solution.py:331
  3.4 25.2 %collective-permute-start.1 = (bf16[512,640]{1,0:T(8,128)(2,1)S(1)}, bf16[512,640]{1,0:T(8,128)(2,1)S(1)}, u32[]{:S(2)}, u32[]{:S(2)}) collective-permute-start(bf16[512,640]{1,0:T(8,128)(2,1)S(1)} %bitcast.13), channel_id=1, source_target_pairs={{0,192},{8,200},{16,208},{24,216},{32,224},{40,232},{48,240},{56,2... | collective-permute-start | bytes 1966088 | tf_op jit(solution)/shard_map/ppermute | solution.py:331
  4.2 25.9 %collective-permute-start.16 = (bf16[256,640]{1,0:T(8,128)(2,1)}, bf16[256,640]{1,0:T(8,128)(2,1)}, u32[]{:S(2)}, u32[]{:S(2)}) collective-permute-start(bf16[256,640]{1,0:T(8,128)(2,1)} %q_ref.1), channel_id=1, source_target_pairs={{0,32},{8,40},{16,48},{24,56},{32,0},{40,8},{48,16},{56,24},{64,96... | collective-permute-start | bytes 983048 | tf_op jit(solution)/shard_map/ppermute | solution.py:331
  11.1 19.7 %collective-permute-start.2 = (bf16[512,640]{1,0:T(8,128)(2,1)S(1)}, bf16[512,640]{1,0:T(8,128)(2,1)S(1)}, u32[]{:S(2)}, u32[]{:S(2)}) collective-permute-start(bf16[512,640]{1,0:T(8,128)(2,1)S(1)} %bitcast.14), channel_id=1, source_target_pairs={{0,8},{8,0},{16,24},{24,16},{32,40},{40,32},{48,56},{56,48},{64,72... | collective-permute-start | bytes 1966088 | tf_op jit(solution)/shard_map/ppermute | solution.py:331
  19.1 11.5 %collective-permute-start.5 = (bf16[256,640]{1,0:T(8,128)(2,1)}, bf16[256,640]{1,0:T(8,128)(2,1)}, u32[]{:S(2)}, u32[]{:S(2)}) collective-permute-start(bf16[256,640]{1,0:T(8,128)(2,1)} %slice.12), channel_id=1, source_target_pairs={{0,64},{8,72},{16,80},{24,88},{32,96},{40,104},{48,112},{56,120},{... | collective-permute-start | bytes 983048 | tf_op jit(solution)/shard_map/ppermute | solution.py:331
  21.4 8.7 %collective-permute-start.15 = (s32[1,8]{1,0:T(1,128)S(1)}, s32[1,8]{1,0:T(1,128)S(1)}, u32[]{:S(2)}, u32[]{:S(2)}) collective-permute-start(s32[1,8]{1,0:T(1,128)S(1)} %pad_add_fusion.facts_ref), channel_id=1, source_target_pairs={{0,32},{8,40},{16,48},{24,56},{32,0},{40,8},{48,16},{56,24},{64,96... | collective-permute-start | bytes 104 | tf_op jit(solution)/shard_map/ppermute | solution.py:331
  28.7 8.3 %collective-permute-start.6 = (bf16[256,640]{1,0:T(8,128)(2,1)S(1)}, bf16[256,640]{1,0:T(8,128)(2,1)}, u32[]{:S(2)}, u32[]{:S(2)}) collective-permute-start(bf16[256,640]{1,0:T(8,128)(2,1)S(1)} %slice.13), channel_id=1, source_target_pairs={{0,192},{8,200},{16,208},{24,216},{32,224},{40,232},{48,240},{56,2... | collective-permute-start | bytes 983048 | tf_op jit(solution)/shard_map/ppermute | solution.py:331
  30.1 11.5 %collective-permute-start.3 = (bf16[512,640]{1,0:T(8,128)(2,1)S(1)}, bf16[512,640]{1,0:T(8,128)(2,1)S(1)}, u32[]{:S(2)}, u32[]{:S(2)}) collective-permute-start(bf16[512,640]{1,0:T(8,128)(2,1)S(1)} %collective-permute-done.refs_1_), channel_id=1, source_target_pairs={{0,8},{8,0},{16,24},{24,16},{32,40},{40,32},{48,56},{56,48},{64,72... | collective-permute-start | bytes 1966088 | tf_op jit(solution)/shard_map/ppermute | solution.py:331
  30.1 11.8 %collective-permute-start.4 = (bf16[512,640]{1,0:T(8,128)(2,1)S(1)}, bf16[512,640]{1,0:T(8,128)(2,1)}, u32[]{:S(2)}, u32[]{:S(2)}) collective-permute-start(bf16[512,640]{1,0:T(8,128)(2,1)S(1)} %collective-permute-done.1.refs_2_), channel_id=1, source_target_pairs={{0,8},{8,0},{16,24},{24,16},{32,40},{40,32},{48,56},{56,48},{64,72... | collective-permute-start | bytes 1966088 | tf_op jit(solution)/shard_map/ppermute | solution.py:331
  30.6 6.5 %collective-permute-start.7 = (bf16[256,640]{1,0:T(8,128)(2,1)}, bf16[256,640]{1,0:T(8,128)(2,1)}, u32[]{:S(2)}, u32[]{:S(2)}) collective-permute-start(bf16[256,640]{1,0:T(8,128)(2,1)} %collective-permute-done.5.refs_6_), channel_id=1, source_target_pairs={{0,8},{8,0},{16,24},{24,16},{32,40},{40,32},{48,56},{56,48},{64,72... | collective-permute-start | bytes 983048 | tf_op jit(solution)/shard_map/ppermute | solution.py:331
  30.8 21.4 %collective-permute-start.13 = (bf16[256,640]{1,0:T(8,128)(2,1)}, bf16[256,640]{1,0:T(8,128)(2,1)}, u32[]{:S(2)}, u32[]{:S(2)}) collective-permute-start(bf16[256,640]{1,0:T(8,128)(2,1)} %q_ref.1), channel_id=1, source_target_pairs={{0,48},{8,56},{16,0},{24,8},{32,16},{40,24},{48,32},{56,40},{64,11... | collective-permute-start | bytes 983048 | tf_op jit(solution)/shard_map/ppermute | solution.py:331
  37.0 2.0 %collective-permute-start.8 = (bf16[256,640]{1,0:T(8,128)(2,1)}, bf16[256,640]{1,0:T(8,128)(2,1)}, u32[]{:S(2)}, u32[]{:S(2)}) collective-permute-start(bf16[256,640]{1,0:T(8,128)(2,1)} %collective-permute-done.6.refs_7_), channel_id=1, source_target_pairs={{0,8},{8,0},{16,24},{24,16},{32,40},{40,32},{48,56},{56,48},{64,72... | collective-permute-start | bytes 983048 | tf_op jit(solution)/shard_map/ppermute | solution.py:331
  37.1 26.7 %collective-permute-start.10 = (bf16[256,640]{1,0:T(8,128)(2,1)}, bf16[256,640]{1,0:T(8,128)(2,1)S(1)}, u32[]{:S(2)}, u32[]{:S(2)}) collective-permute-start(bf16[256,640]{1,0:T(8,128)(2,1)} %q_ref.1), channel_id=1, source_target_pairs={{0,16},{8,24},{16,32},{24,40},{32,48},{40,56},{48,0},{56,8},{64,80... | collective-permute-start | bytes 983048 | tf_op jit(solution)/shard_map/ppermute | solution.py:331
  39.0 13.2 %collective-permute-start.12 = (s32[1,8]{1,0:T(1,128)S(1)}, s32[1,8]{1,0:T(1,128)S(1)}, u32[]{:S(2)}, u32[]{:S(2)}) collective-permute-start(s32[1,8]{1,0:T(1,128)S(1)} %pad_add_fusion.facts_ref), channel_id=1, source_target_pairs={{0,48},{8,56},{16,0},{24,8},{32,16},{40,24},{48,32},{56,40},{64,11... | collective-permute-start | bytes 104 | tf_op jit(solution)/shard_map/ppermute | solution.py:331
  41.6 22.3 %collective-permute-start.9 = (s32[1,8]{1,0:T(1,128)S(1)}, s32[1,8]{1,0:T(1,128)S(1)}, u32[]{:S(2)}, u32[]{:S(2)}) collective-permute-start(s32[1,8]{1,0:T(1,128)S(1)} %pad_add_fusion.facts_ref), channel_id=1, source_target_pairs={{0,16},{8,24},{16,32},{24,40},{32,48},{40,56},{48,0},{56,8},{64,80... | collective-permute-start | bytes 104 | tf_op jit(solution)/shard_map/ppermute | solution.py:331
  49.5 30.8 %collective-permute-start.17 = (bf16[272,640]{1,0:T(8,128)(2,1)S(1)}, bf16[272,640]{1,0:T(8,128)(2,1)S(1)}, u32[]{:S(2)}, u32[]{:S(2)}) collective-permute-start(bf16[272,640]{1,0:T(8,128)(2,1)S(1)} %attend.5), channel_id=1, source_target_pairs={{0,32},{8,40},{16,48},{24,56},{32,0},{40,8},{48,16},{56,24},{64,96... | collective-permute-start | bytes 1044488 | tf_op jit(solution)/shard_map/ppermute | solution.py:331
  52.2 36.9 %slice-start = ((s8[6553600]{0:T(1024)(128)(4,1)}), s8[4194304]{0:T(1024)(128)(4,1)S(1)}, s32[]{:S(2)}) async-start(s8[6553600]{0:T(1024)(128)(4,1)} %bitcast.19), calls=%async_computation.2 | async-start | bytes 8388608
  59.9 12.0 %copy-start = (bf16[256,640]{1,0:T(8,128)(2,1)S(1)}, bf16[256,640]{1,0:T(8,128)(2,1)}, u32[]{:S(2)}) copy-start(bf16[256,640]{1,0:T(8,128)(2,1)} %q_ref.1) | copy-start | bytes 983044
  60.0 12.0 %copy-start.1 = (bf16[256,640]{1,0:T(8,128)(2,1)S(1)}, bf16[256,640]{1,0:T(8,128)(2,1)}, u32[]{:S(2)}) copy-start(bf16[256,640]{1,0:T(8,128)(2,1)} %refs_10_.1) | copy-start | bytes 983044
  60.0 12.0 %copy-start.2 = (bf16[256,640]{1,0:T(8,128)(2,1)S(1)}, bf16[256,640]{1,0:T(8,128)(2,1)}, u32[]{:S(2)}) copy-start(bf16[256,640]{1,0:T(8,128)(2,1)} %refs_11_.1) | copy-start | bytes 983044
  60.0 29.1 %slice-start.1 = ((s8[6553600]{0:T(1024)(128)(4,1)}), s8[2359296]{0:T(1024)(128)(4,1)S(1)}, s32[]{:S(2)}) async-start(s8[6553600]{0:T(1024)(128)(4,1)} %bitcast.19), calls=%async_computation.3 | async-start | bytes 4718592
  60.0 20.2 %collective-permute-start.14 = (bf16[272,640]{1,0:T(8,128)(2,1)S(1)}, bf16[272,640]{1,0:T(8,128)(2,1)S(1)}, u32[]{:S(2)}, u32[]{:S(2)}) collective-permute-start(bf16[272,640]{1,0:T(8,128)(2,1)S(1)} %attend.4), channel_id=1, source_target_pairs={{0,16},{8,24},{16,32},{24,40},{32,48},{40,56},{48,0},{56,8},{64,80... | collective-permute-start | bytes 1044488 | tf_op jit(solution)/shard_map/ppermute | solution.py:331
  71.5 17.6 %collective-permute-start.11 = (bf16[272,640]{1,0:T(8,128)(2,1)S(1)}, bf16[272,640]{1,0:T(8,128)(2,1)S(1)}, u32[]{:S(2)}, u32[]{:S(2)}) collective-permute-start(bf16[272,640]{1,0:T(8,128)(2,1)S(1)} %attend.3), channel_id=1, source_target_pairs={{0,48},{8,56},{16,0},{24,8},{32,16},{40,24},{48,32},{56,40},{64,11... | collective-permute-start | bytes 1044488 | tf_op jit(solution)/shard_map/ppermute | solution.py:331
  94.2 4.6 %copy-start.4 = (f32[640]{0:T(1024)S(1)}, f32[640]{0:T(1024)}, u32[]{:S(2)}) copy-start(f32[640]{0:T(1024)} %param.21) | copy-start | bytes 7684
  94.2 42.3 %copy-start.6 = (f32[640]{0:T(1024)S(1)}, f32[640]{0:T(1024)}, u32[]{:S(2)}) copy-start(f32[640]{0:T(1024)} %param.23) | copy-start | bytes 7684
  94.2 36.4 %all-to-all-start = ((bf16[8,256,640]{2,1,0:T(8,128)(2,1)}), bf16[8,256,640]{2,1,0:T(8,128)(2,1)S(1)}, u32[]{:S(2)}, u32[]{:S(2)}) async-start(bf16[8,256,640]{2,1,0:T(8,128)(2,1)} %project.1), calls=%async_computation | async-start | bytes 5242880 | tf_op jit(solution)/shard_map/all_to_all | solution.py:361
  98.8 37.6 %copy-start.5 = (f32[640]{0:T(1024)S(1)}, f32[640]{0:T(1024)}, u32[]{:S(2)}) copy-start(f32[640]{0:T(1024)} %param.22) | copy-start | bytes 7684
  130.5 1.0 copy-start.3
  133.0 9.6 %all-to-all-start.1 = ((f32[8,8,256]{2,1,0:T(8,128)}), f32[8,8,256]{2,1,0:T(8,128)S(1)}, u32[]{:S(2)}, u32[]{:S(2)}) async-start(f32[8,8,256]{2,1,0:T(8,128)} %get-tuple-element.9), calls=%async_computation.1 | async-start | bytes 131072 | tf_op jit(solution)/shard_map/all_to_all | solution.py:363

commit v4 on v3

--- a/solution.py
+++ b/solution.py
@@ -330,7 +330,7 @@
     width = queries.shape[1]
     send = lambda array, dx, dz, dc: lax.ppermute(array, "req", shift(dx, dz, dc))
 
-    ways = (1, -1, 2)
+    ways = (1, 2, -1)
     facts = jnp.concatenate([suffix_lengths, request_group], axis=1)
     their_query = [send(queries, 0, dz, 0) for dz in ways]
     their_facts = [send(facts, 0, dz, 0) for dz in ways]
@@ -339,8 +339,10 @@
     left, right = send(pages, 1, 0, 0), send(pages, -1, 0, 0)
     over_left = send(left[:TOK], 1, 0, 0)
     over_right = send(right[TOK:], -1, 0, 0)
-    across = lambda arrays: arrays + [send(array, 0, 0, 1) for array in arrays]
-    blocks = across([pages, left, right]) + across([over_left, over_right])
+    near = [pages, left, right]
+    blocks = near + [send(array, 0, 0, 1) for array in near] + [over_left, over_right]
+    blocks.append(send(over_left, 0, 0, 1))
+    blocks.append(send(over_right, 0, 0, 1))
 
     me = lax.axis_index("req")
     x, z, c = me // (NZ * NC), (me // NC) % NZ, me % NC
@@ -359,7 +361,7 @@
     num, ml = attend(page_group, facts, queries, blocks, suffix)
     parts = project(num, ml, others, out_weight)
     parts = lax.all_to_all(parts, "tp", 0, 0, tiled=True)
-    combined, sums = combine(parts, residual, attn_gate[None, :])
+    combined, sums = combine(parts, pltpu.with_memory_space_constraint(residual, pltpu.HBM), attn_gate[None, :])
     sums = lax.all_to_all(sums, "tp", 0, 0, tiled=True)
     return finish(combined, sums, mod_shift[None, :], mod_scale[None, :])
 

time: 146 us -> 156 us (1.068)
  waiting for transfers between devices: 56.2 us -> 66.4 us
    ppermute x18, waiting for transfers between devices: 18.2 us -> 27.5 us  [body(): lax.ppermute(array, 'req', shift(dx, dz, dc))]
  transfers between devices with their start and end apart: 20 -> 20, of which waited for: 7 -> 8; matrix products, arithmetic and copies ran while one was open for 1% -> 1% of each run, Pallas kernels for 22% -> 20%
where the time goes in v4:
time: 156 us; the launch traced here: 155 us
  waiting for transfers between devices  66.4 us (43%)
  starting transfers between devices  44.5 us (29%)
  Pallas kernels  39.7 us (25%)
  local copies, waits for them, and re-layouts  2.18 us (1%)
    ppermute x18, starting transfers between devices, body(): lax.ppermute(array, 'req', shift(dx, dz, dc))  36.6 us
    all_to_all x1, waiting for transfers between devices, body(): parts = lax.all_to_all(parts, 'tp', 0, 0, tiled=True)  32.7 us
    pallas_call x4, Pallas kernels, attend(): pl.pallas_call(functools.partial(attend_kernel, own), name='attend_own' i...  31.2 us
    ppermute x18, waiting for transfers between devices, body(): lax.ppermute(array, 'req', shift(dx, dz, dc))  27.5 us
    all_to_all x1, waiting for transfers between devices, body(): sums = lax.all_to_all(sums, 'tp', 0, 0, tiled=True)  6.23 us
    pallas_call x1, Pallas kernels, project(): pl.pallas_call(project_kernel, name='project', out_shape=pltpu.HBM((8, TO...  5.08 us
    all_to_all x1, starting transfers between devices, body(): parts = lax.all_to_all(parts, 'tp', 0, 0, tiled=True)  4.6 us
    all_to_all x1, starting transfers between devices, body(): sums = lax.all_to_all(sums, 'tp', 0, 0, tiled=True)  3.35 us
  transfers between devices with their start and end apart: 20, of which 8 were waited for; matrix products, arithmetic and copies ran while one was open for 1% of the time, Pallas kernels for 20%

profile of v4, /device:TPU:2, one launch (start us, length us, event | category | flops | bytes accessed | tf_op | source)
XLA Modules:
  0.0 154.7 jit_solution(6739520954911141667)
XLA Ops:
  0.6 0.0 copy-start.6
  0.6 1.2 copy.16
  1.8 1.6 %collective-permute-start = (bf16[512,640]{1,0:T(8,128)(2,1)S(1)}, bf16[512,640]{1,0:T(8,128)(2,1)S(1)}, u32[]{:S(2)}, u32[]{:S(2)}) collective-permute-start(bf16[512,640]{1,0:T(8,128)(2,1)S(1)} %bitcast.12), channel_id=1, source_target_pairs={{0,64},{8,72},{16,80},{24,88},{32,96},{40,104},{48,112},{56,120},{... | collective-permute-start | bytes 1966088 | tf_op jit(solution)/shard_map/ppermute | solution.py:331
  3.4 0.8 collective-permute-start.1
  4.2 6.0 %collective-permute-start.16 = (bf16[256,640]{1,0:T(8,128)(2,1)}, bf16[256,640]{1,0:T(8,128)(2,1)}, u32[]{:S(2)}, u32[]{:S(2)}) collective-permute-start(bf16[256,640]{1,0:T(8,128)(2,1)} %q_ref.1), channel_id=1, source_target_pairs={{0,48},{8,56},{16,0},{24,8},{32,16},{40,24},{48,32},{56,40},{64,11... | collective-permute-start | bytes 983048 | tf_op jit(solution)/shard_map/ppermute | solution.py:331
  10.2 0.0 collective-permute-start.2
  10.2 8.1 %collective-permute-done.refs_1_ = bf16[512,640]{1,0:T(8,128)(2,1)S(1)} collective-permute-done((bf16[512,640]{1,0:T(8,128)(2,1)S(1)}, bf16[512,640]{1,0:T(8,128)(2,1)S(1)}, u32[]{:S(2)}, u32[]{:S(2)}) %collective-permute-start) | collective-permute-done | bytes 655392 | tf_op jit(solution)/shard_map/ppermute | solution.py:331
  18.4 0.8 slice.12
  19.1 1.5 collective-permute-start.5
  20.6 0.7 pad_add_fusion.facts_ref
  21.4 6.3 %collective-permute-start.15 = (s32[1,8]{1,0:T(1,128)S(1)}, s32[1,8]{1,0:T(1,128)S(1)}, u32[]{:S(2)}, u32[]{:S(2)}) collective-permute-start(s32[1,8]{1,0:T(1,128)S(1)} %pad_add_fusion.facts_ref), channel_id=1, source_target_pairs={{0,48},{8,56},{16,0},{24,8},{32,16},{40,24},{48,32},{56,40},{64,11... | collective-permute-start | bytes 104 | tf_op jit(solution)/shard_map/ppermute | solution.py:331
  27.7 0.1 stack.35
  27.7 0.0 collective-permute-done.1.refs_2_
  27.8 0.6 collective-permute-start.6
  28.4 0.6 collective-permute-done.15.facts_ref
  28.9 0.0 collective-permute-start.3
  28.9 0.0 collective-permute-done.16.q_ref
  29.0 0.5 collective-permute-start.4
  29.5 0.0 collective-permute-done.5.refs_6_
  29.5 0.1 collective-permute-start.7
  29.6 0.1 iota_add_fusion
  29.6 0.0 collective-permute-done.2.refs_3_
  29.6 5.8 %collective-permute-start.13 = (bf16[256,640]{1,0:T(8,128)(2,1)}, bf16[256,640]{1,0:T(8,128)(2,1)}, u32[]{:S(2)}, u32[]{:S(2)}) collective-permute-start(bf16[256,640]{1,0:T(8,128)(2,1)} %q_ref.1), channel_id=1, source_target_pairs={{0,32},{8,40},{16,48},{24,56},{32,0},{40,8},{48,16},{56,24},{64,96... | collective-permute-start | bytes 983048 | tf_op jit(solution)/shard_map/ppermute | solution.py:331
  35.4 0.7 collective-permute-done.6.refs_7_
  36.1 0.0 collective-permute-start.8
  36.1 0.0 copy-done.6
  36.1 0.1 add.145
  36.2 0.0 collective-permute-done.7.refs_8_
  36.2 1.1 collective-permute-start.10
  37.3 0.2 convert_reduce_fusion.page_group_ref
  37.5 0.6 collective-permute-done.8.refs_9_
  38.1 2.3 %collective-permute-start.12 = (s32[1,8]{1,0:T(1,128)S(1)}, s32[1,8]{1,0:T(1,128)S(1)}, u32[]{:S(2)}, u32[]{:S(2)}) collective-permute-start(s32[1,8]{1,0:T(1,128)S(1)} %pad_add_fusion.facts_ref), channel_id=1, source_target_pairs={{0,32},{8,40},{16,48},{24,56},{32,0},{40,8},{48,16},{56,24},{64,96... | collective-permute-start | bytes 104 | tf_op jit(solution)/shard_map/ppermute | solution.py:331
  40.4 0.0 collective-permute-done.3.refs_4_
  40.4 2.7 %collective-permute-start.9 = (s32[1,8]{1,0:T(1,128)S(1)}, s32[1,8]{1,0:T(1,128)S(1)}, u32[]{:S(2)}, u32[]{:S(2)}) collective-permute-start(s32[1,8]{1,0:T(1,128)S(1)} %pad_add_fusion.facts_ref), channel_id=1, source_target_pairs={{0,16},{8,24},{16,32},{24,40},{32,48},{40,56},{48,0},{56,8},{64,80... | collective-permute-start | bytes 104 | tf_op jit(solution)/shard_map/ppermute | solution.py:331
  43.0 0.0 collective-permute-done.4.refs_5_
  43.0 7.6 %attend.5 = bf16[272,640]{1,0:T(8,128)(2,1)S(1)} custom-call(s32[16]{0:T(128)S(1)} %convert_reduce_fusion.page_group_ref, s32[1,8]{1,0:T(1,128)S(1)} %collective-permute-done.15.facts_ref, bf16[256,640]{1,0:T(8,128)(2,1)} %collective-permute-done.16.q_ref, bf16[512,640]{1,0:T(8,128)(2,1)S(1)} %bitcast.15, bf16[512,640]{1,0:T(8,128)(2,1)S(1)} %collective-permute-done.refs_1_, ...), custom_call_target="tpu_custom_call" | custom-call | flops 1342177280 | bytes 6225920 | tf_op jit(solution)/shard_map/attend/pallas_call | solution.py:176
  50.6 1.8 %collective-permute-start.17 = (bf16[272,640]{1,0:T(8,128)(2,1)S(1)}, bf16[272,640]{1,0:T(8,128)(2,1)S(1)}, u32[]{:S(2)}, u32[]{:S(2)}) collective-permute-start(bf16[272,640]{1,0:T(8,128)(2,1)S(1)} %attend.5), channel_id=1, source_target_pairs={{0,16},{8,24},{16,32},{24,40},{32,48},{40,56},{48,0},{56,8},{64,80... | collective-permute-start | bytes 1044488 | tf_op jit(solution)/shard_map/ppermute | solution.py:331
  52.4 6.2 %collective-permute-done.12.facts_ref = s32[1,8]{1,0:T(1,128)S(1)} collective-permute-done((s32[1,8]{1,0:T(1,128)S(1)}, s32[1,8]{1,0:T(1,128)S(1)}, u32[]{:S(2)}, u32[]{:S(2)}) %collective-permute-start.12) | collective-permute-done | bytes 64 | tf_op jit(solution)/shard_map/ppermute | solution.py:331
  58.6 0.0 collective-permute-done.13.q_ref
  58.7 7.7 %attend.4 = bf16[272,640]{1,0:T(8,128)(2,1)S(1)} custom-call(s32[16]{0:T(128)S(1)} %convert_reduce_fusion.page_group_ref, s32[1,8]{1,0:T(1,128)S(1)} %collective-permute-done.12.facts_ref, bf16[256,640]{1,0:T(8,128)(2,1)} %collective-permute-done.13.q_ref, bf16[512,640]{1,0:T(8,128)(2,1)S(1)} %bitcast.16, bf16[512,640]{1,0:T(8,128)(2,1)S(1)} %collective-permute-done.refs_1_, ...), custom_call_target="tpu_custom_call" | custom-call | flops 1342177280 | bytes 6225920 | tf_op jit(solution)/shard_map/attend/pallas_call | solution.py:176
  66.4 0.0 copy-start
  66.4 0.0 copy-start.1
  66.4 0.0 copy-start.2
  66.4 0.0 slice-start.1
  66.5 5.1 %collective-permute-start.14 = (bf16[272,640]{1,0:T(8,128)(2,1)S(1)}, bf16[272,640]{1,0:T(8,128)(2,1)S(1)}, u32[]{:S(2)}, u32[]{:S(2)}) collective-permute-start(bf16[272,640]{1,0:T(8,128)(2,1)S(1)} %attend.4), channel_id=1, source_target_pairs={{0,32},{8,40},{16,48},{24,56},{32,0},{40,8},{48,16},{56,24},{64,96... | collective-permute-start | bytes 1044488 | tf_op jit(solution)/shard_map/ppermute | solution.py:331
  71.5 0.0 collective-permute-done.9.facts_ref
  71.5 0.0 collective-permute-done.10.q_ref
  71.5 7.6 %attend.3 = bf16[272,640]{1,0:T(8,128)(2,1)S(1)} custom-call(s32[16]{0:T(128)S(1)} %convert_reduce_fusion.page_group_ref, s32[1,8]{1,0:T(1,128)S(1)} %collective-permute-done.9.facts_ref, bf16[256,640]{1,0:T(8,128)(2,1)S(1)} %collective-permute-done.10.q_ref, bf16[512,640]{1,0:T(8,128)(2,1)S(1)} %bitcast.17, ...), custom_call_target="tpu_custom_call" | custom-call | flops 1342177280 | bytes 6225920 | tf_op jit(solution)/shard_map/attend/pallas_call | solution.py:176
  79.2 0.4 collective-permute-start.11
  79.6 0.0 copy-done.1
  79.7 8.3 %attend_own.1 = (f32[256,640]{1,0:T(8,128)S(1)}, f32[16,256]{1,0:T(8,128)S(1)}) custom-call(s32[16]{0:T(128)S(1)} %convert_reduce_fusion.page_group_ref, s32[1,8]{1,0:T(1,128)S(1)} %pad_add_fusion.facts_ref, bf16[256,640]{1,0:T(8,128)(2,1)S(1)} %copy-done, bf16[512,640]{1,0:T(8,128)(2,1)S(1)} %bitcast.18, bf16[512,640]{1,0:T(8,128)(2,1)S(1)} %collective-permute-done.refs_1_, ...), custom_call_target="tpu_custom_call" | custom-call | flops 1509949440 | bytes 6881280 | tf_op jit(solution)/shard_map/attend_own/pallas_call | solution.py:176
  87.9 0.0 collective-permute-done.17.n3
  87.9 11.2 %collective-permute-done.14.n2 = bf16[272,640]{1,0:T(8,128)(2,1)S(1)} collective-permute-done((bf16[272,640]{1,0:T(8,128)(2,1)S(1)}, bf16[272,640]{1,0:T(8,128)(2,1)S(1)}, u32[]{:S(2)}, u32[]{:S(2)}) %collective-permute-start.14) | collective-permute-done | bytes 348192 | tf_op jit(solution)/shard_map/ppermute | solution.py:331
  99.1 0.0 collective-permute-done.11.n1
  99.2 5.1 %project.1 = bf16[8,256,640]{2,1,0:T(8,128)(2,1)} custom-call(f32[256,640]{1,0:T(8,128)S(1)} %get-tuple-element.6.n0, f32[16,256]{1,0:T(8,128)S(1)} %get-tuple-element.7.s0, bf16[272,640]{1,0:T(8,128)(2,1)S(1)} %collective-permute-done.11.n1, bf16[272,640]{1,0:T(8,128)(2,1)S(1)} %collective-permute-done.14.n2, ...), custom_call_target="tpu_custom_call" | custom-call | flops 1677721600 | bytes 10158080 | tf_op jit(solution)/shard_map/project/pallas_call | solution.py:234
  104.2 4.6 %all-to-all-start = ((bf16[8,256,640]{2,1,0:T(8,128)(2,1)}), bf16[8,256,640]{2,1,0:T(8,128)(2,1)S(1)}, u32[]{:S(2)}, u32[]{:S(2)}) async-start(bf16[8,256,640]{2,1,0:T(8,128)(2,1)} %project.1), calls=%async_computation | async-start | bytes 5242880 | tf_op jit(solution)/shard_map/all_to_all | solution.py:363
  108.8 0.0 copy-done.3
  108.9 0.0 copy-start.4
  108.9 0.0 copy-start.5
  108.9 32.7 %all-to-all-done.parts_ref = bf16[8,256,640]{2,1,0:T(8,128)(2,1)S(1)} async-done(((bf16[8,256,640]{2,1,0:T(8,128)(2,1)}), bf16[8,256,640]{2,1,0:T(8,128)(2,1)S(1)}, u32[]{:S(2)}, u32[]{:S(2)}) %all-to-all-start) | async-done | bytes 2621472 | tf_op jit(solution)/shard_map/all_to_all | solution.py:363
  141.6 2.3 %combine.1 = (f32[256,640]{1,0:T(8,128)S(1)}, f32[8,8,256]{2,1,0:T(8,128)}) custom-call(bf16[8,256,640]{2,1,0:T(8,128)(2,1)S(1)} %all-to-all-done.parts_ref, bf16[256,640]{1,0:T(8,128)(2,1)} %residual_ref.1, f32[1,640]{1,0:T(1,128)S(1)} %broadcast_in_dim.11.gate_ref), custom_call_target="tpu_custom_call" | custom-call | tf_op jit(solution)/shard_map/combine/pallas_call | solution.py:270
  143.9 3.4 %all-to-all-start.1 = ((f32[8,8,256]{2,1,0:T(8,128)}), f32[8,8,256]{2,1,0:T(8,128)S(1)}, u32[]{:S(2)}, u32[]{:S(2)}) async-start(f32[8,8,256]{2,1,0:T(8,128)} %get-tuple-element.9), calls=%async_computation.1 | async-start | bytes 131072 | tf_op jit(solution)/shard_map/all_to_all | solution.py:365
  147.3 6.2 %all-to-all-done.1.sums_ref = f32[8,8,256]{2,1,0:T(8,128)S(1)} async-done(((f32[8,8,256]{2,1,0:T(8,128)}), f32[8,8,256]{2,1,0:T(8,128)S(1)}, u32[]{:S(2)}, u32[]{:S(2)}) %all-to-all-start.1) | async-done | bytes 65568 | tf_op jit(solution)/shard_map/all_to_all | solution.py:365
  153.6 1.1 finish.1
  (15 shorter events, 0.1 us)
Async XLA Ops:
  0.6 35.5 %copy-start.6 = (s32[2,32]{1,0:T(2,128)S(1)}, s32[2,32]{1,0:T(2,128)}, u32[]{:S(2)}) copy-start(s32[2,32]{1,0:T(2,128)} %param.16) | copy-start | bytes 772
  1.8 16.6 %collective-permute-start = (bf16[512,640]{1,0:T(8,128)(2,1)S(1)}, bf16[512,640]{1,0:T(8,128)(2,1)S(1)}, u32[]{:S(2)}, u32[]{:S(2)}) collective-permute-start(bf16[512,640]{1,0:T(8,128)(2,1)S(1)} %bitcast.12), channel_id=1, source_target_pairs={{0,64},{8,72},{16,80},{24,88},{32,96},{40,104},{48,112},{56,120},{... | collective-permute-start | bytes 1966088 | tf_op jit(solution)/shard_map/ppermute | solution.py:331
  3.4 24.4 %collective-permute-start.1 = (bf16[512,640]{1,0:T(8,128)(2,1)S(1)}, bf16[512,640]{1,0:T(8,128)(2,1)S(1)}, u32[]{:S(2)}, u32[]{:S(2)}) collective-permute-start(bf16[512,640]{1,0:T(8,128)(2,1)S(1)} %bitcast.13), channel_id=1, source_target_pairs={{0,192},{8,200},{16,208},{24,216},{32,224},{40,232},{48,240},{56,2... | collective-permute-start | bytes 1966088 | tf_op jit(solution)/shard_map/ppermute | solution.py:331
  4.2 24.7 %collective-permute-start.16 = (bf16[256,640]{1,0:T(8,128)(2,1)}, bf16[256,640]{1,0:T(8,128)(2,1)}, u32[]{:S(2)}, u32[]{:S(2)}) collective-permute-start(bf16[256,640]{1,0:T(8,128)(2,1)} %q_ref.1), channel_id=1, source_target_pairs={{0,48},{8,56},{16,0},{24,8},{32,16},{40,24},{48,32},{56,40},{64,11... | collective-permute-start | bytes 983048 | tf_op jit(solution)/shard_map/ppermute | solution.py:331
  10.2 19.4 %collective-permute-start.2 = (bf16[512,640]{1,0:T(8,128)(2,1)S(1)}, bf16[512,640]{1,0:T(8,128)(2,1)S(1)}, u32[]{:S(2)}, u32[]{:S(2)}) collective-permute-start(bf16[512,640]{1,0:T(8,128)(2,1)S(1)} %bitcast.14), channel_id=1, source_target_pairs={{0,8},{8,0},{16,24},{24,16},{32,40},{40,32},{48,56},{56,48},{64,72... | collective-permute-start | bytes 1966088 | tf_op jit(solution)/shard_map/ppermute | solution.py:331
  19.1 10.4 %collective-permute-start.5 = (bf16[256,640]{1,0:T(8,128)(2,1)}, bf16[256,640]{1,0:T(8,128)(2,1)}, u32[]{:S(2)}, u32[]{:S(2)}) collective-permute-start(bf16[256,640]{1,0:T(8,128)(2,1)} %slice.12), channel_id=1, source_target_pairs={{0,64},{8,72},{16,80},{24,88},{32,96},{40,104},{48,112},{56,120},{... | collective-permute-start | bytes 983048 | tf_op jit(solution)/shard_map/ppermute | solution.py:331
  21.4 7.6 %collective-permute-start.15 = (s32[1,8]{1,0:T(1,128)S(1)}, s32[1,8]{1,0:T(1,128)S(1)}, u32[]{:S(2)}, u32[]{:S(2)}) collective-permute-start(s32[1,8]{1,0:T(1,128)S(1)} %pad_add_fusion.facts_ref), channel_id=1, source_target_pairs={{0,48},{8,56},{16,0},{24,8},{32,16},{40,24},{48,32},{56,40},{64,11... | collective-permute-start | bytes 104 | tf_op jit(solution)/shard_map/ppermute | solution.py:331
  27.8 8.3 %collective-permute-start.6 = (bf16[256,640]{1,0:T(8,128)(2,1)S(1)}, bf16[256,640]{1,0:T(8,128)(2,1)}, u32[]{:S(2)}, u32[]{:S(2)}) collective-permute-start(bf16[256,640]{1,0:T(8,128)(2,1)S(1)} %slice.13), channel_id=1, source_target_pairs={{0,192},{8,200},{16,208},{24,216},{32,224},{40,232},{48,240},{56,2... | collective-permute-start | bytes 983048 | tf_op jit(solution)/shard_map/ppermute | solution.py:331
  28.9 11.4 %collective-permute-start.3 = (bf16[512,640]{1,0:T(8,128)(2,1)S(1)}, bf16[512,640]{1,0:T(8,128)(2,1)S(1)}, u32[]{:S(2)}, u32[]{:S(2)}) collective-permute-start(bf16[512,640]{1,0:T(8,128)(2,1)S(1)} %collective-permute-done.refs_1_), channel_id=1, source_target_pairs={{0,8},{8,0},{16,24},{24,16},{32,40},{40,32},{48,56},{56,48},{64,72... | collective-permute-start | bytes 1966088 | tf_op jit(solution)/shard_map/ppermute | solution.py:331
  29.0 14.1 %collective-permute-start.4 = (bf16[512,640]{1,0:T(8,128)(2,1)S(1)}, bf16[512,640]{1,0:T(8,128)(2,1)}, u32[]{:S(2)}, u32[]{:S(2)}) collective-permute-start(bf16[512,640]{1,0:T(8,128)(2,1)S(1)} %collective-permute-done.1.refs_2_), channel_id=1, source_target_pairs={{0,8},{8,0},{16,24},{24,16},{32,40},{40,32},{48,56},{56,48},{64,72... | collective-permute-start | bytes 1966088 | tf_op jit(solution)/shard_map/ppermute | solution.py:331
  29.5 6.7 %collective-permute-start.7 = (bf16[256,640]{1,0:T(8,128)(2,1)}, bf16[256,640]{1,0:T(8,128)(2,1)}, u32[]{:S(2)}, u32[]{:S(2)}) collective-permute-start(bf16[256,640]{1,0:T(8,128)(2,1)} %collective-permute-done.5.refs_6_), channel_id=1, source_target_pairs={{0,8},{8,0},{16,24},{24,16},{32,40},{40,32},{48,56},{56,48},{64,72... | collective-permute-start | bytes 983048 | tf_op jit(solution)/shard_map/ppermute | solution.py:331
  29.6 29.0 %collective-permute-start.13 = (bf16[256,640]{1,0:T(8,128)(2,1)}, bf16[256,640]{1,0:T(8,128)(2,1)}, u32[]{:S(2)}, u32[]{:S(2)}) collective-permute-start(bf16[256,640]{1,0:T(8,128)(2,1)} %q_ref.1), channel_id=1, source_target_pairs={{0,32},{8,40},{16,48},{24,56},{32,0},{40,8},{48,16},{56,24},{64,96... | collective-permute-start | bytes 983048 | tf_op jit(solution)/shard_map/ppermute | solution.py:331
  36.1 2.0 %collective-permute-start.8 = (bf16[256,640]{1,0:T(8,128)(2,1)}, bf16[256,640]{1,0:T(8,128)(2,1)}, u32[]{:S(2)}, u32[]{:S(2)}) collective-permute-start(bf16[256,640]{1,0:T(8,128)(2,1)} %collective-permute-done.6.refs_7_), channel_id=1, source_target_pairs={{0,8},{8,0},{16,24},{24,16},{32,40},{40,32},{48,56},{56,48},{64,72... | collective-permute-start | bytes 983048 | tf_op jit(solution)/shard_map/ppermute | solution.py:331
  36.2 35.4 %collective-permute-start.10 = (bf16[256,640]{1,0:T(8,128)(2,1)}, bf16[256,640]{1,0:T(8,128)(2,1)S(1)}, u32[]{:S(2)}, u32[]{:S(2)}) collective-permute-start(bf16[256,640]{1,0:T(8,128)(2,1)} %q_ref.1), channel_id=1, source_target_pairs={{0,16},{8,24},{16,32},{24,40},{32,48},{40,56},{48,0},{56,8},{64,80... | collective-permute-start | bytes 983048 | tf_op jit(solution)/shard_map/ppermute | solution.py:331
  38.1 20.6 %collective-permute-start.12 = (s32[1,8]{1,0:T(1,128)S(1)}, s32[1,8]{1,0:T(1,128)S(1)}, u32[]{:S(2)}, u32[]{:S(2)}) collective-permute-start(s32[1,8]{1,0:T(1,128)S(1)} %pad_add_fusion.facts_ref), channel_id=1, source_target_pairs={{0,32},{8,40},{16,48},{24,56},{32,0},{40,8},{48,16},{56,24},{64,96... | collective-permute-start | bytes 104 | tf_op jit(solution)/shard_map/ppermute | solution.py:331
  40.4 31.2 %collective-permute-start.9 = (s32[1,8]{1,0:T(1,128)S(1)}, s32[1,8]{1,0:T(1,128)S(1)}, u32[]{:S(2)}, u32[]{:S(2)}) collective-permute-start(s32[1,8]{1,0:T(1,128)S(1)} %pad_add_fusion.facts_ref), channel_id=1, source_target_pairs={{0,16},{8,24},{16,32},{24,40},{32,48},{40,56},{48,0},{56,8},{64,80... | collective-permute-start | bytes 104 | tf_op jit(solution)/shard_map/ppermute | solution.py:331
  50.6 37.3 %collective-permute-start.17 = (bf16[272,640]{1,0:T(8,128)(2,1)S(1)}, bf16[272,640]{1,0:T(8,128)(2,1)S(1)}, u32[]{:S(2)}, u32[]{:S(2)}) collective-permute-start(bf16[272,640]{1,0:T(8,128)(2,1)S(1)} %attend.5), channel_id=1, source_target_pairs={{0,16},{8,24},{16,32},{24,40},{32,48},{40,56},{48,0},{56,8},{64,80... | collective-permute-start | bytes 1044488 | tf_op jit(solution)/shard_map/ppermute | solution.py:331
  58.6 40.5 %slice-start = ((s8[6553600]{0:T(1024)(128)(4,1)}), s8[4194304]{0:T(1024)(128)(4,1)S(1)}, s32[]{:S(2)}) async-start(s8[6553600]{0:T(1024)(128)(4,1)} %bitcast.19), calls=%async_computation.2 | async-start | bytes 8388608
  66.4 13.2 %copy-start = (bf16[256,640]{1,0:T(8,128)(2,1)S(1)}, bf16[256,640]{1,0:T(8,128)(2,1)}, u32[]{:S(2)}) copy-start(bf16[256,640]{1,0:T(8,128)(2,1)} %q_ref.1) | copy-start | bytes 983044
  66.4 13.2 %copy-start.1 = (bf16[256,640]{1,0:T(8,128)(2,1)S(1)}, bf16[256,640]{1,0:T(8,128)(2,1)}, u32[]{:S(2)}) copy-start(bf16[256,640]{1,0:T(8,128)(2,1)} %refs_10_.1) | copy-start | bytes 983044
  66.4 13.2 %copy-start.2 = (bf16[256,640]{1,0:T(8,128)(2,1)S(1)}, bf16[256,640]{1,0:T(8,128)(2,1)}, u32[]{:S(2)}) copy-start(bf16[256,640]{1,0:T(8,128)(2,1)} %refs_11_.1) | copy-start | bytes 983044
  66.4 32.7 %slice-start.1 = ((s8[6553600]{0:T(1024)(128)(4,1)}), s8[2359296]{0:T(1024)(128)(4,1)S(1)}, s32[]{:S(2)}) async-start(s8[6553600]{0:T(1024)(128)(4,1)} %bitcast.19), calls=%async_computation.3 | async-start | bytes 4718592
  66.5 32.7 %collective-permute-start.14 = (bf16[272,640]{1,0:T(8,128)(2,1)S(1)}, bf16[272,640]{1,0:T(8,128)(2,1)S(1)}, u32[]{:S(2)}, u32[]{:S(2)}) collective-permute-start(bf16[272,640]{1,0:T(8,128)(2,1)S(1)} %attend.4), channel_id=1, source_target_pairs={{0,32},{8,40},{16,48},{24,56},{32,0},{40,8},{48,16},{56,24},{64,96... | collective-permute-start | bytes 1044488 | tf_op jit(solution)/shard_map/ppermute | solution.py:331
  79.2 19.9 %collective-permute-start.11 = (bf16[272,640]{1,0:T(8,128)(2,1)S(1)}, bf16[272,640]{1,0:T(8,128)(2,1)S(1)}, u32[]{:S(2)}, u32[]{:S(2)}) collective-permute-start(bf16[272,640]{1,0:T(8,128)(2,1)S(1)} %attend.3), channel_id=1, source_target_pairs={{0,48},{8,56},{16,0},{24,8},{32,16},{40,24},{48,32},{56,40},{64,11... | collective-permute-start | bytes 1044488 | tf_op jit(solution)/shard_map/ppermute | solution.py:331
  104.2 4.6 %copy-start.3 = (f32[640]{0:T(1024)S(1)}, f32[640]{0:T(1024)}, u32[]{:S(2)}) copy-start(f32[640]{0:T(1024)} %param.21) | copy-start | bytes 7684
  104.2 37.4 %all-to-all-start = ((bf16[8,256,640]{2,1,0:T(8,128)(2,1)}), bf16[8,256,640]{2,1,0:T(8,128)(2,1)S(1)}, u32[]{:S(2)}, u32[]{:S(2)}) async-start(bf16[8,256,640]{2,1,0:T(8,128)(2,1)} %project.1), calls=%async_computation | async-start | bytes 5242880 | tf_op jit(solution)/shard_map/all_to_all | solution.py:363
  108.9 38.5 %copy-start.4 = (f32[640]{0:T(1024)S(1)}, f32[640]{0:T(1024)}, u32[]{:S(2)}) copy-start(f32[640]{0:T(1024)} %param.22) | copy-start | bytes 7684
  108.9 38.5 %copy-start.5 = (f32[640]{0:T(1024)S(1)}, f32[640]{0:T(1024)}, u32[]{:S(2)}) copy-start(f32[640]{0:T(1024)} %param.23) | copy-start | bytes 7684
  143.9 9.6 %all-to-all-start.1 = ((f32[8,8,256]{2,1,0:T(8,128)}), f32[8,8,256]{2,1,0:T(8,128)S(1)}, u32[]{:S(2)}, u32[]{:S(2)}) async-start(f32[8,8,256]{2,1,0:T(8,128)} %get-tuple-element.9), calls=%async_computation.1 | async-start | bytes 131072 | tf_op jit(solution)/shard_map/all_to_all | solution.py:365

commit v5 on v3

--- a/solution.py
+++ b/solution.py
@@ -100,7 +100,7 @@
 
 
 def attend_kernel(own, page_group_ref, facts_ref, q_ref, *refs):
-    kv_refs, refs = refs[:10], refs[10:]
+    kv_refs, refs = refs[:16], refs[16:]
     suffix, refs = (refs[:2], refs[2:]) if own else ((), refs)
     if own:
         num_ref, ml_ref, feat, kfeat, scores, top, ml = refs
@@ -116,11 +116,10 @@
 
     def rows(start):
         pick = slice(start, start + 128)
-        later = slice(start + 256, start + 384)
-        out = [jnp.concatenate([r[pick, :], r[later, :]], axis=0) for r in kv_refs[:6]]
-        for a, b in (kv_refs[6:8], kv_refs[8:10]):
-            out.append(jnp.concatenate([a[pick, :], b[pick, :]], axis=0))
-        return out
+        return [
+            jnp.concatenate([a[pick, :], b[pick, :]], axis=0)
+            for a, b in zip(kv_refs[0::2], kv_refs[1::2])
+        ]
 
     @pl.when(page_group_ref[0] >= 0)
     def _():
@@ -335,12 +334,17 @@
     their_query = [send(queries, 0, dz, 0) for dz in ways]
     their_facts = [send(facts, 0, dz, 0) for dz in ways]
 
-    pages = page_cache.transpose(0, 2, 1, 3).reshape(2 * TOK, width)
-    left, right = send(pages, 1, 0, 0), send(pages, -1, 0, 0)
-    over_left = send(left[:TOK], 1, 0, 0)
-    over_right = send(right[TOK:], -1, 0, 0)
-    across = lambda arrays: arrays + [send(array, 0, 0, 1) for array in arrays]
-    blocks = across([pages, left, right]) + across([over_left, over_right])
+    one, two = [
+        page.transpose(1, 0, 2).reshape(TOK, width) for page in (page_cache[0], page_cache[1])
+    ]
+    left_one = send(one, 1, 0, 0)
+    right_two = send(two, -1, 0, 0)
+    left_two = send(two, 1, 0, 0)
+    right_one = send(one, -1, 0, 0)
+    over = [send(left_one, 1, 0, 0), send(right_two, -1, 0, 0)]
+    near = [one, two, left_one, left_two, right_one, right_two]
+    blocks = near + [send(page, 0, 0, 1) for page in near]
+    blocks = blocks + over + [send(page, 0, 0, 1) for page in over]
 
     me = lax.axis_index("req")
     x, z, c = me // (NZ * NC), (me // NC) % NZ, me % NC
@@ -359,7 +363,7 @@
     num, ml = attend(page_group, facts, queries, blocks, suffix)
     parts = project(num, ml, others, out_weight)
     parts = lax.all_to_all(parts, "tp", 0, 0, tiled=True)
-    combined, sums = combine(parts, residual, attn_gate[None, :])
+    combined, sums = combine(parts, pltpu.with_memory_space_constraint(residual, pltpu.HBM), attn_gate[None, :])
     sums = lax.all_to_all(sums, "tp", 0, 0, tiled=True)
     return finish(combined, sums, mod_shift[None, :], mod_scale[None, :])
 

time: 146 us -> 152 us (1.041)
  starting transfers between devices: 43.7 us -> 50.3 us
    ppermute x18 -> x23, starting transfers between devices: 35.7 us -> 42.3 us  [body(): lax.ppermute(array, 'req', shift(dx, dz, dc))]
    ppermute x18 -> x23, waiting for transfers between devices: 18.2 us -> 16.5 us  [body(): lax.ppermute(array, 'req', shift(dx, dz, dc))]
  transfers between devices with their start and end apart: 20 -> 25, of which waited for: 7 -> 7; matrix products, arithmetic and copies ran while one was open for 1% -> 0% of each run, Pallas kernels for 22% -> 21%
where the time goes in v5:
time: 152 us; the launch traced here: 150 us
  waiting for transfers between devices  55.3 us (36%)
  starting transfers between devices  50.3 us (33%)
  Pallas kernels  40.1 us (26%)
  local copies, waits for them, and re-layouts  3.54 us (2%)
    ppermute x23, starting transfers between devices, body(): lax.ppermute(array, 'req', shift(dx, dz, dc))  42.3 us
    all_to_all x1, waiting for transfers between devices, body(): parts = lax.all_to_all(parts, 'tp', 0, 0, tiled=True)  32.5 us
    pallas_call x4, Pallas kernels, attend(): pl.pallas_call(functools.partial(attend_kernel, own), name='attend_own' i...  31.6 us
    ppermute x23, waiting for transfers between devices, body(): lax.ppermute(array, 'req', shift(dx, dz, dc))  16.5 us
    all_to_all x1, waiting for transfers between devices, body(): sums = lax.all_to_all(sums, 'tp', 0, 0, tiled=True)  6.23 us
    pallas_call x1, Pallas kernels, project(): pl.pallas_call(project_kernel, name='project', out_shape=pltpu.HBM((8, TO...  5.08 us
    all_to_all x1, starting transfers between devices, body(): parts = lax.all_to_all(parts, 'tp', 0, 0, tiled=True)  4.6 us
    all_to_all x1, starting transfers between devices, body(): sums = lax.all_to_all(sums, 'tp', 0, 0, tiled=True)  3.35 us
  transfers between devices with their start and end apart: 25, of which 7 were waited for; matrix products, arithmetic and copies ran while one was open for 0% of the time, Pallas kernels for 21%

profile of v5, /device:TPU:2, one launch (start us, length us, event | category | flops | bytes accessed | tf_op | source)
XLA Modules:
  0.0 150.4 jit_solution(4050183759715457050)
XLA Ops:
  0.7 1.5 %slice_bitcast_fusion = (bf16[2,128,640]{2,0,1:T(2,128)(2,1)S(1)}, bf16[2,128,640]{2,0,1:T(2,128)(2,1)S(1)}) fusion(bf16[2,128,2,640]{3,2,1,0:T(2,128)(2,1)} %param.15), kind=kLoop, calls=%fused_computation | loop fusion | bytes 1310720 | tf_op jit(solution)/shard_map/transpose | solution.py:338
  2.2 1.6 %collective-permute-start = (bf16[256,640]{1,0:T(8,128)(2,1)S(1)}, bf16[256,640]{1,0:T(8,128)(2,1)S(1)}, u32[]{:S(2)}, u32[]{:S(2)}) collective-permute-start(bf16[256,640]{1,0:T(8,128)(2,1)S(1)} %bitcast.20), channel_id=1, source_target_pairs={{0,64},{8,72},{16,80},{24,88},{32,96},{40,104},{48,112},{56,120},{... | collective-permute-start | bytes 983048 | tf_op jit(solution)/shard_map/ppermute | solution.py:330
  3.9 0.8 collective-permute-start.3
  4.7 1.3 collective-permute-start.1
  6.0 2.0 %collective-permute-start.2 = (bf16[256,640]{1,0:T(8,128)(2,1)S(1)}, bf16[256,640]{1,0:T(8,128)(2,1)S(1)}, u32[]{:S(2)}, u32[]{:S(2)}) collective-permute-start(bf16[256,640]{1,0:T(8,128)(2,1)S(1)} %bitcast.21), channel_id=1, source_target_pairs={{0,192},{8,200},{16,208},{24,216},{32,224},{40,232},{48,240},{56,2... | collective-permute-start | bytes 983048 | tf_op jit(solution)/shard_map/ppermute | solution.py:330
  7.9 0.1 pad_add_fusion.facts_ref
  8.0 5.8 %collective-permute-start.20 = (s32[1,8]{1,0:T(1,128)S(1)}, s32[1,8]{1,0:T(1,128)S(1)}, u32[]{:S(2)}, u32[]{:S(2)}) collective-permute-start(s32[1,8]{1,0:T(1,128)S(1)} %pad_add_fusion.facts_ref), channel_id=1, source_target_pairs={{0,32},{8,40},{16,48},{24,56},{32,0},{40,8},{48,16},{56,24},{64,96... | collective-permute-start | bytes 104 | tf_op jit(solution)/shard_map/ppermute | solution.py:330
  13.8 1.7 %collective-permute-done.20.facts_ref = s32[1,8]{1,0:T(1,128)S(1)} collective-permute-done((s32[1,8]{1,0:T(1,128)S(1)}, s32[1,8]{1,0:T(1,128)S(1)}, u32[]{:S(2)}, u32[]{:S(2)}) %collective-permute-start.20) | collective-permute-done | bytes 64 | tf_op jit(solution)/shard_map/ppermute | solution.py:330
  15.5 0.0 collective-permute-done.refs_2_
  15.5 0.5 collective-permute-start.5
  16.0 0.0 collective-permute-done.3.refs_5_
  16.0 5.8 %collective-permute-start.21 = (bf16[256,640]{1,0:T(8,128)(2,1)}, bf16[256,640]{1,0:T(8,128)(2,1)}, u32[]{:S(2)}, u32[]{:S(2)}) collective-permute-start(bf16[256,640]{1,0:T(8,128)(2,1)} %q_ref.1), channel_id=1, source_target_pairs={{0,32},{8,40},{16,48},{24,56},{32,0},{40,8},{48,16},{56,24},{64,96... | collective-permute-start | bytes 983048 | tf_op jit(solution)/shard_map/ppermute | solution.py:330
  21.8 0.1 stack.35
  21.9 1.6 %collective-permute-start.10 = (bf16[256,640]{1,0:T(8,128)(2,1)S(1)}, bf16[256,640]{1,0:T(8,128)(2,1)S(1)}, u32[]{:S(2)}, u32[]{:S(2)}) collective-permute-start(bf16[256,640]{1,0:T(8,128)(2,1)S(1)} %collective-permute-done.refs_2_), channel_id=1, source_target_pairs={{0,64},{8,72},{16,80},{24,88},{32,96},{40,104},{48,112},{56,120},{... | collective-permute-start | bytes 983048 | tf_op jit(solution)/shard_map/ppermute | solution.py:330
  23.4 0.0 collective-permute-done.4.refs_6_
  23.5 1.7 %collective-permute-start.11 = (bf16[256,640]{1,0:T(8,128)(2,1)S(1)}, bf16[256,640]{1,0:T(8,128)(2,1)}, u32[]{:S(2)}, u32[]{:S(2)}) collective-permute-start(bf16[256,640]{1,0:T(8,128)(2,1)S(1)} %collective-permute-done.3.refs_5_), channel_id=1, source_target_pairs={{0,192},{8,200},{16,208},{24,216},{32,224},{40,232},{48,240},{56,2... | collective-permute-start | bytes 983048 | tf_op jit(solution)/shard_map/ppermute | solution.py:330
  25.1 0.0 collective-permute-done.5.refs_7_
  25.1 0.1 collective-permute-start.9
  25.3 5.9 %collective-permute-done.21.q_ref = bf16[256,640]{1,0:T(8,128)(2,1)} collective-permute-done((bf16[256,640]{1,0:T(8,128)(2,1)}, bf16[256,640]{1,0:T(8,128)(2,1)}, u32[]{:S(2)}, u32[]{:S(2)}) %collective-permute-start.21) | collective-permute-done | bytes 327712 | tf_op jit(solution)/shard_map/ppermute | solution.py:330
  31.2 0.1 iota_add_fusion
  31.3 1.3 collective-permute-done.10.refs_12_
  32.6 9.2 %collective-permute-start.18 = (bf16[256,640]{1,0:T(8,128)(2,1)}, bf16[256,640]{1,0:T(8,128)(2,1)}, u32[]{:S(2)}, u32[]{:S(2)}) collective-permute-start(bf16[256,640]{1,0:T(8,128)(2,1)} %q_ref.1), channel_id=1, source_target_pairs={{0,48},{8,56},{16,0},{24,8},{32,16},{40,24},{48,32},{56,40},{64,11... | collective-permute-start | bytes 983048 | tf_op jit(solution)/shard_map/ppermute | solution.py:330
  41.8 0.0 collective-permute-done.11.refs_13_
  41.8 0.2 collective-permute-start.8
  42.0 0.0 collective-permute-done.6.refs_8_
  42.1 0.3 collective-permute-start.12
  42.3 0.0 collective-permute-done.9.refs_11_
  42.4 0.7 copy-done
  43.1 0.2 collective-permute-start.13
  43.3 0.1 add.145
  43.4 0.3 collective-permute-start.15
  43.7 0.2 convert_reduce_fusion.page_group_ref
  43.8 4.2 %collective-permute-start.17 = (s32[1,8]{1,0:T(1,128)S(1)}, s32[1,8]{1,0:T(1,128)S(1)}, u32[]{:S(2)}, u32[]{:S(2)}) collective-permute-start(s32[1,8]{1,0:T(1,128)S(1)} %pad_add_fusion.facts_ref), channel_id=1, source_target_pairs={{0,48},{8,56},{16,0},{24,8},{32,16},{40,24},{48,32},{56,40},{64,11... | collective-permute-start | bytes 104 | tf_op jit(solution)/shard_map/ppermute | solution.py:330
  48.0 0.0 collective-permute-done.12.refs_14_
  48.0 0.0 collective-permute-start.14
  48.0 0.0 collective-permute-done.13.refs_15_
  48.0 0.0 copy-start.1
  48.1 1.0 copy-done.1
  49.0 7.7 %attend.5 = bf16[272,640]{1,0:T(8,128)(2,1)S(1)} custom-call(s32[16]{0:T(128)S(1)} %convert_reduce_fusion.page_group_ref, s32[1,8]{1,0:T(1,128)S(1)} %collective-permute-done.20.facts_ref, bf16[256,640]{1,0:T(8,128)(2,1)} %collective-permute-done.21.q_ref, bf16[256,640]{1,0:T(8,128)(2,1)S(1)} %bitcast.23, bf16[256,640]{1,0:T(8,128)(2,1)S(1)} %bitcast.30, ...), custom_call_target="tpu_custom_call" | custom-call | flops 1342177280 | bytes 6225920 | tf_op jit(solution)/shard_map/attend/pallas_call | solution.py:175
  56.7 2.5 %collective-permute-start.22 = (bf16[272,640]{1,0:T(8,128)(2,1)S(1)}, bf16[272,640]{1,0:T(8,128)(2,1)S(1)}, u32[]{:S(2)}, u32[]{:S(2)}) collective-permute-start(bf16[272,640]{1,0:T(8,128)(2,1)S(1)} %attend.5), channel_id=1, source_target_pairs={{0,32},{8,40},{16,48},{24,56},{32,0},{40,8},{48,16},{56,24},{64,96... | collective-permute-start | bytes 1044488 | tf_op jit(solution)/shard_map/ppermute | solution.py:330
  59.3 0.0 collective-permute-done.17.facts_ref
  59.3 0.0 collective-permute-done.18.q_ref
  59.3 7.9 %attend.4 = bf16[272,640]{1,0:T(8,128)(2,1)S(1)} custom-call(s32[16]{0:T(128)S(1)} %convert_reduce_fusion.page_group_ref, s32[1,8]{1,0:T(1,128)S(1)} %collective-permute-done.17.facts_ref, bf16[256,640]{1,0:T(8,128)(2,1)} %collective-permute-done.18.q_ref, bf16[256,640]{1,0:T(8,128)(2,1)S(1)} %bitcast.24, bf16[256,640]{1,0:T(8,128)(2,1)S(1)} %bitcast.31, ...), custom_call_target="tpu_custom_call" | custom-call | flops 1342177280 | bytes 6225920 | tf_op jit(solution)/shard_map/attend/pallas_call | solution.py:175
  67.2 0.0 copy-start.2
  67.2 0.0 copy-start.3
  67.2 0.0 copy-start.4
  67.2 0.0 slice-start.1
  67.2 4.1 %collective-permute-start.19 = (bf16[272,640]{1,0:T(8,128)(2,1)S(1)}, bf16[272,640]{1,0:T(8,128)(2,1)S(1)}, u32[]{:S(2)}, u32[]{:S(2)}) collective-permute-start(bf16[272,640]{1,0:T(8,128)(2,1)S(1)} %attend.4), channel_id=1, source_target_pairs={{0,16},{8,24},{16,32},{24,40},{32,48},{40,56},{48,0},{56,8},{64,80... | collective-permute-start | bytes 1044488 | tf_op jit(solution)/shard_map/ppermute | solution.py:330
  71.3 0.0 collective-permute-done.14.facts_ref
  71.3 0.0 collective-permute-done.15.q_ref
  71.3 7.7 %attend.3 = bf16[272,640]{1,0:T(8,128)(2,1)S(1)} custom-call(s32[16]{0:T(128)S(1)} %convert_reduce_fusion.page_group_ref, s32[1,8]{1,0:T(1,128)S(1)} %collective-permute-done.14.facts_ref, bf16[256,640]{1,0:T(8,128)(2,1)S(1)} %collective-permute-done.15.q_ref, bf16[256,640]{1,0:T(8,128)(2,1)S(1)} %bitcast.25, bf16[256,640]{1,0:T(8,128)(2,1)S(1)} %bitcast.32, ...), custom_call_target="tpu_custom_call" | custom-call | flops 1342177280 | bytes 6225920 | tf_op jit(solution)/shard_map/attend/pallas_call | solution.py:175
  79.1 0.2 collective-permute-start.16
  79.3 8.3 %attend_own.1 = (f32[256,640]{1,0:T(8,128)S(1)}, f32[16,256]{1,0:T(8,128)S(1)}) custom-call(s32[16]{0:T(128)S(1)} %convert_reduce_fusion.page_group_ref, s32[1,8]{1,0:T(1,128)S(1)} %pad_add_fusion.facts_ref, bf16[256,640]{1,0:T(8,128)(2,1)} %q_ref.1, bf16[256,640]{1,0:T(8,128)(2,1)S(1)} %bitcast.26, bf16[256,640]{1,0:T(8,128)(2,1)S(1)} %bitcast.33, ...), custom_call_target="tpu_custom_call" | custom-call | flops 1509949440 | bytes 6881280 | tf_op jit(solution)/shard_map/attend_own/pallas_call | solution.py:175
  87.6 5.0 %collective-permute-done.19.n2 = bf16[272,640]{1,0:T(8,128)(2,1)S(1)} collective-permute-done((bf16[272,640]{1,0:T(8,128)(2,1)S(1)}, bf16[272,640]{1,0:T(8,128)(2,1)S(1)}, u32[]{:S(2)}, u32[]{:S(2)}) %collective-permute-start.19) | collective-permute-done | bytes 348192 | tf_op jit(solution)/shard_map/ppermute | solution.py:330
  92.6 2.4 %collective-permute-done.16.n1 = bf16[272,640]{1,0:T(8,128)(2,1)S(1)} collective-permute-done((bf16[272,640]{1,0:T(8,128)(2,1)S(1)}, bf16[272,640]{1,0:T(8,128)(2,1)S(1)}, u32[]{:S(2)}, u32[]{:S(2)}) %collective-permute-start.16) | collective-permute-done | bytes 348192 | tf_op jit(solution)/shard_map/ppermute | solution.py:330
  95.1 5.1 %project.1 = bf16[8,256,640]{2,1,0:T(8,128)(2,1)} custom-call(f32[256,640]{1,0:T(8,128)S(1)} %get-tuple-element.6.n0, f32[16,256]{1,0:T(8,128)S(1)} %get-tuple-element.7.s0, bf16[272,640]{1,0:T(8,128)(2,1)S(1)} %collective-permute-done.16.n1, bf16[272,640]{1,0:T(8,128)(2,1)S(1)} %collective-permute-done.19.n2, ...), custom_call_target="tpu_custom_call" | custom-call | flops 1677721600 | bytes 10158080 | tf_op jit(solution)/shard_map/project/pallas_call | solution.py:233
  100.2 4.6 %all-to-all-start = ((bf16[8,256,640]{2,1,0:T(8,128)(2,1)}), bf16[8,256,640]{2,1,0:T(8,128)(2,1)S(1)}, u32[]{:S(2)}, u32[]{:S(2)}) async-start(bf16[8,256,640]{2,1,0:T(8,128)(2,1)} %project.1), calls=%async_computation | async-start | bytes 5242880 | tf_op jit(solution)/shard_map/all_to_all | solution.py:365
  104.8 0.0 copy-start.6
  104.8 0.0 copy-start.7
  104.8 32.5 %all-to-all-done.parts_ref = bf16[8,256,640]{2,1,0:T(8,128)(2,1)S(1)} async-done(((bf16[8,256,640]{2,1,0:T(8,128)(2,1)}), bf16[8,256,640]{2,1,0:T(8,128)(2,1)S(1)}, u32[]{:S(2)}, u32[]{:S(2)}) %all-to-all-start) | async-done | bytes 2621472 | tf_op jit(solution)/shard_map/all_to_all | solution.py:365
  137.4 2.3 %combine.1 = (f32[256,640]{1,0:T(8,128)S(1)}, f32[8,8,256]{2,1,0:T(8,128)}) custom-call(bf16[8,256,640]{2,1,0:T(8,128)(2,1)S(1)} %all-to-all-done.parts_ref, bf16[256,640]{1,0:T(8,128)(2,1)} %residual_ref.1, f32[1,640]{1,0:T(1,128)S(1)} %broadcast_in_dim.11.gate_ref), custom_call_target="tpu_custom_call" | custom-call | tf_op jit(solution)/shard_map/combine/pallas_call | solution.py:269
  139.7 3.4 %all-to-all-start.1 = ((f32[8,8,256]{2,1,0:T(8,128)}), f32[8,8,256]{2,1,0:T(8,128)S(1)}, u32[]{:S(2)}, u32[]{:S(2)}) async-start(f32[8,8,256]{2,1,0:T(8,128)} %get-tuple-element.9), calls=%async_computation.1 | async-start | bytes 131072 | tf_op jit(solution)/shard_map/all_to_all | solution.py:367
  143.1 6.2 %all-to-all-done.1.sums_ref = f32[8,8,256]{2,1,0:T(8,128)S(1)} async-done(((f32[8,8,256]{2,1,0:T(8,128)}), f32[8,8,256]{2,1,0:T(8,128)S(1)}, u32[]{:S(2)}, u32[]{:S(2)}) %all-to-all-start.1) | async-done | bytes 65568 | tf_op jit(solution)/shard_map/all_to_all | solution.py:367
  149.3 1.1 finish.1
  (33 shorter events, 0.1 us)
Async XLA Ops:
  0.6 7.3 %copy-start.10 = (s32[1,4]{1,0:T(1,128)S(1)}, s32[1,4]{1,0:T(1,128)}, u32[]{:S(2)}) copy-start(s32[1,4]{1,0:T(1,128)} %param.17) | copy-start | bytes 52
  0.6 7.3 %copy-start.9 = (s32[1,4]{1,0:T(1,128)S(1)}, s32[1,4]{1,0:T(1,128)}, u32[]{:S(2)}) copy-start(s32[1,4]{1,0:T(1,128)} %param.18) | copy-start | bytes 52
  0.7 42.6 %copy-start.8 = (s32[2,32]{1,0:T(2,128)S(1)}, s32[2,32]{1,0:T(2,128)}, u32[]{:S(2)}) copy-start(s32[2,32]{1,0:T(2,128)} %param.16) | copy-start | bytes 772
  2.2 13.3 %collective-permute-start = (bf16[256,640]{1,0:T(8,128)(2,1)S(1)}, bf16[256,640]{1,0:T(8,128)(2,1)S(1)}, u32[]{:S(2)}, u32[]{:S(2)}) collective-permute-start(bf16[256,640]{1,0:T(8,128)(2,1)S(1)} %bitcast.20), channel_id=1, source_target_pairs={{0,64},{8,72},{16,80},{24,88},{32,96},{40,104},{48,112},{56,120},{... | collective-permute-start | bytes 983048 | tf_op jit(solution)/shard_map/ppermute | solution.py:330
  3.9 12.2 %collective-permute-start.3 = (bf16[256,640]{1,0:T(8,128)(2,1)S(1)}, bf16[256,640]{1,0:T(8,128)(2,1)S(1)}, u32[]{:S(2)}, u32[]{:S(2)}) collective-permute-start(bf16[256,640]{1,0:T(8,128)(2,1)S(1)} %bitcast.27), channel_id=1, source_target_pairs={{0,192},{8,200},{16,208},{24,216},{32,224},{40,232},{48,240},{56,2... | collective-permute-start | bytes 983048 | tf_op jit(solution)/shard_map/ppermute | solution.py:330
  4.7 17.2 %collective-permute-start.1 = (bf16[256,640]{1,0:T(8,128)(2,1)S(1)}, bf16[256,640]{1,0:T(8,128)(2,1)S(1)}, u32[]{:S(2)}, u32[]{:S(2)}) collective-permute-start(bf16[256,640]{1,0:T(8,128)(2,1)S(1)} %bitcast.28), channel_id=1, source_target_pairs={{0,64},{8,72},{16,80},{24,88},{32,96},{40,104},{48,112},{56,120},{... | collective-permute-start | bytes 983048 | tf_op jit(solution)/shard_map/ppermute | solution.py:330
  6.0 17.5 %collective-permute-start.2 = (bf16[256,640]{1,0:T(8,128)(2,1)S(1)}, bf16[256,640]{1,0:T(8,128)(2,1)S(1)}, u32[]{:S(2)}, u32[]{:S(2)}) collective-permute-start(bf16[256,640]{1,0:T(8,128)(2,1)S(1)} %bitcast.21), channel_id=1, source_target_pairs={{0,192},{8,200},{16,208},{24,216},{32,224},{40,232},{48,240},{56,2... | collective-permute-start | bytes 983048 | tf_op jit(solution)/shard_map/ppermute | solution.py:330
  8.0 7.5 %collective-permute-start.20 = (s32[1,8]{1,0:T(1,128)S(1)}, s32[1,8]{1,0:T(1,128)S(1)}, u32[]{:S(2)}, u32[]{:S(2)}) collective-permute-start(s32[1,8]{1,0:T(1,128)S(1)} %pad_add_fusion.facts_ref), channel_id=1, source_target_pairs={{0,32},{8,40},{16,48},{24,56},{32,0},{40,8},{48,16},{56,24},{64,96... | collective-permute-start | bytes 104 | tf_op jit(solution)/shard_map/ppermute | solution.py:330
  15.5 7.9 %collective-permute-start.4 = (bf16[256,640]{1,0:T(8,128)(2,1)S(1)}, bf16[256,640]{1,0:T(8,128)(2,1)S(1)}, u32[]{:S(2)}, u32[]{:S(2)}) collective-permute-start(bf16[256,640]{1,0:T(8,128)(2,1)S(1)} %bitcast.22), channel_id=1, source_target_pairs={{0,8},{8,0},{16,24},{24,16},{32,40},{40,32},{48,56},{56,48},{64,72... | collective-permute-start | bytes 983048 | tf_op jit(solution)/shard_map/ppermute | solution.py:330
  15.5 9.6 %collective-permute-start.5 = (bf16[256,640]{1,0:T(8,128)(2,1)S(1)}, bf16[256,640]{1,0:T(8,128)(2,1)S(1)}, u32[]{:S(2)}, u32[]{:S(2)}) collective-permute-start(bf16[256,640]{1,0:T(8,128)(2,1)S(1)} %bitcast.29), channel_id=1, source_target_pairs={{0,8},{8,0},{16,24},{24,16},{32,40},{40,32},{48,56},{56,48},{64,72... | collective-permute-start | bytes 983048 | tf_op jit(solution)/shard_map/ppermute | solution.py:330
  16.0 15.2 %collective-permute-start.21 = (bf16[256,640]{1,0:T(8,128)(2,1)}, bf16[256,640]{1,0:T(8,128)(2,1)}, u32[]{:S(2)}, u32[]{:S(2)}) collective-permute-start(bf16[256,640]{1,0:T(8,128)(2,1)} %q_ref.1), channel_id=1, source_target_pairs={{0,32},{8,40},{16,48},{24,56},{32,0},{40,8},{48,16},{56,24},{64,96... | collective-permute-start | bytes 983048 | tf_op jit(solution)/shard_map/ppermute | solution.py:330
  21.9 10.7 %collective-permute-start.10 = (bf16[256,640]{1,0:T(8,128)(2,1)S(1)}, bf16[256,640]{1,0:T(8,128)(2,1)S(1)}, u32[]{:S(2)}, u32[]{:S(2)}) collective-permute-start(bf16[256,640]{1,0:T(8,128)(2,1)S(1)} %collective-permute-done.refs_2_), channel_id=1, source_target_pairs={{0,64},{8,72},{16,80},{24,88},{32,96},{40,104},{48,112},{56,120},{... | collective-permute-start | bytes 983048 | tf_op jit(solution)/shard_map/ppermute | solution.py:330
  23.4 18.6 %collective-permute-start.6 = (bf16[256,640]{1,0:T(8,128)(2,1)S(1)}, bf16[256,640]{1,0:T(8,128)(2,1)S(1)}, u32[]{:S(2)}, u32[]{:S(2)}) collective-permute-start(bf16[256,640]{1,0:T(8,128)(2,1)S(1)} %collective-permute-done.refs_2_), channel_id=1, source_target_pairs={{0,8},{8,0},{16,24},{24,16},{32,40},{40,32},{48,56},{56,48},{64,72... | collective-permute-start | bytes 983048 | tf_op jit(solution)/shard_map/ppermute | solution.py:330
  23.5 18.4 %collective-permute-start.11 = (bf16[256,640]{1,0:T(8,128)(2,1)S(1)}, bf16[256,640]{1,0:T(8,128)(2,1)}, u32[]{:S(2)}, u32[]{:S(2)}) collective-permute-start(bf16[256,640]{1,0:T(8,128)(2,1)S(1)} %collective-permute-done.3.refs_5_), channel_id=1, source_target_pairs={{0,192},{8,200},{16,208},{24,216},{32,224},{40,232},{48,240},{56,2... | collective-permute-start | bytes 983048 | tf_op jit(solution)/shard_map/ppermute | solution.py:330
  25.1 17.2 %collective-permute-start.9 = (bf16[256,640]{1,0:T(8,128)(2,1)S(1)}, bf16[256,640]{1,0:T(8,128)(2,1)S(1)}, u32[]{:S(2)}, u32[]{:S(2)}) collective-permute-start(bf16[256,640]{1,0:T(8,128)(2,1)S(1)} %collective-permute-done.3.refs_5_), channel_id=1, source_target_pairs={{0,8},{8,0},{16,24},{24,16},{32,40},{40,32},{48,56},{56,48},{64,72... | collective-permute-start | bytes 983048 | tf_op jit(solution)/shard_map/ppermute | solution.py:330
  31.2 12.2 %collective-permute-start.7 = (bf16[256,640]{1,0:T(8,128)(2,1)S(1)}, bf16[256,640]{1,0:T(8,128)(2,1)}, u32[]{:S(2)}, u32[]{:S(2)}) collective-permute-start(bf16[256,640]{1,0:T(8,128)(2,1)S(1)} %collective-permute-done.1.refs_3_), channel_id=1, source_target_pairs={{0,8},{8,0},{16,24},{24,16},{32,40},{40,32},{48,56},{56,48},{64,72... | collective-permute-start | bytes 983048 | tf_op jit(solution)/shard_map/ppermute | solution.py:330
  32.6 26.7 %collective-permute-start.18 = (bf16[256,640]{1,0:T(8,128)(2,1)}, bf16[256,640]{1,0:T(8,128)(2,1)}, u32[]{:S(2)}, u32[]{:S(2)}) collective-permute-start(bf16[256,640]{1,0:T(8,128)(2,1)} %q_ref.1), channel_id=1, source_target_pairs={{0,48},{8,56},{16,0},{24,8},{32,16},{40,24},{48,32},{56,40},{64,11... | collective-permute-start | bytes 983048 | tf_op jit(solution)/shard_map/ppermute | solution.py:330
  41.8 2.0 %collective-permute-start.8 = (bf16[256,640]{1,0:T(8,128)(2,1)S(1)}, bf16[256,640]{1,0:T(8,128)(2,1)}, u32[]{:S(2)}, u32[]{:S(2)}) collective-permute-start(bf16[256,640]{1,0:T(8,128)(2,1)S(1)} %collective-permute-done.2.refs_4_), channel_id=1, source_target_pairs={{0,8},{8,0},{16,24},{24,16},{32,40},{40,32},{48,56},{56,48},{64,72... | collective-permute-start | bytes 983048 | tf_op jit(solution)/shard_map/ppermute | solution.py:330
  42.1 6.0 %collective-permute-start.12 = (bf16[256,640]{1,0:T(8,128)(2,1)S(1)}, bf16[256,640]{1,0:T(8,128)(2,1)}, u32[]{:S(2)}, u32[]{:S(2)}) collective-permute-start(bf16[256,640]{1,0:T(8,128)(2,1)S(1)} %collective-permute-done.10.refs_12_), channel_id=1, source_target_pairs={{0,8},{8,0},{16,24},{24,16},{32,40},{40,32},{48,56},{56,48},{64,72... | collective-permute-start | bytes 983048 | tf_op jit(solution)/shard_map/ppermute | solution.py:330
  42.4 0.7 copy-start
  43.1 5.0 %collective-permute-start.13 = (bf16[256,640]{1,0:T(8,128)(2,1)}, bf16[256,640]{1,0:T(8,128)(2,1)}, u32[]{:S(2)}, u32[]{:S(2)}) collective-permute-start(bf16[256,640]{1,0:T(8,128)(2,1)} %collective-permute-done.11.refs_13_), channel_id=1, source_target_pairs={{0,8},{8,0},{16,24},{24,16},{32,40},{40,32},{48,56},{56,48},{64,72... | collective-permute-start | bytes 983048 | tf_op jit(solution)/shard_map/ppermute | solution.py:330
  43.4 28.0 %collective-permute-start.15 = (bf16[256,640]{1,0:T(8,128)(2,1)}, bf16[256,640]{1,0:T(8,128)(2,1)S(1)}, u32[]{:S(2)}, u32[]{:S(2)}) collective-permute-start(bf16[256,640]{1,0:T(8,128)(2,1)} %q_ref.1), channel_id=1, source_target_pairs={{0,16},{8,24},{16,32},{24,40},{32,48},{40,56},{48,0},{56,8},{64,80... | collective-permute-start | bytes 983048 | tf_op jit(solution)/shard_map/ppermute | solution.py:330
  43.8 15.4 %collective-permute-start.17 = (s32[1,8]{1,0:T(1,128)S(1)}, s32[1,8]{1,0:T(1,128)S(1)}, u32[]{:S(2)}, u32[]{:S(2)}) collective-permute-start(s32[1,8]{1,0:T(1,128)S(1)} %pad_add_fusion.facts_ref), channel_id=1, source_target_pairs={{0,48},{8,56},{16,0},{24,8},{32,16},{40,24},{48,32},{56,40},{64,11... | collective-permute-start | bytes 104 | tf_op jit(solution)/shard_map/ppermute | solution.py:330
  48.0 23.3 %collective-permute-start.14 = (s32[1,8]{1,0:T(1,128)S(1)}, s32[1,8]{1,0:T(1,128)S(1)}, u32[]{:S(2)}, u32[]{:S(2)}) collective-permute-start(s32[1,8]{1,0:T(1,128)S(1)} %pad_add_fusion.facts_ref), channel_id=1, source_target_pairs={{0,16},{8,24},{16,32},{24,40},{32,48},{40,56},{48,0},{56,8},{64,80... | collective-permute-start | bytes 104 | tf_op jit(solution)/shard_map/ppermute | solution.py:330
  48.0 1.0 copy-start.1
  56.7 30.8 %collective-permute-start.22 = (bf16[272,640]{1,0:T(8,128)(2,1)S(1)}, bf16[272,640]{1,0:T(8,128)(2,1)S(1)}, u32[]{:S(2)}, u32[]{:S(2)}) collective-permute-start(bf16[272,640]{1,0:T(8,128)(2,1)S(1)} %attend.5), channel_id=1, source_target_pairs={{0,32},{8,40},{16,48},{24,56},{32,0},{40,8},{48,16},{56,24},{64,96... | collective-permute-start | bytes 1044488 | tf_op jit(solution)/shard_map/ppermute | solution.py:330
  59.3 35.8 %slice-start = ((s8[6553600]{0:T(1024)(128)(4,1)}), s8[4194304]{0:T(1024)(128)(4,1)S(1)}, s32[]{:S(2)}) async-start(s8[6553600]{0:T(1024)(128)(4,1)} %bitcast.34), calls=%async_computation.2 | async-start | bytes 8388608
  67.2 12.1 %copy-start.2 = (bf16[256,640]{1,0:T(8,128)(2,1)S(1)}, bf16[256,640]{1,0:T(8,128)(2,1)}, u32[]{:S(2)}) copy-start(bf16[256,640]{1,0:T(8,128)(2,1)} %copy-done) | copy-start | bytes 983044
  67.2 12.1 %copy-start.3 = (bf16[256,640]{1,0:T(8,128)(2,1)S(1)}, bf16[256,640]{1,0:T(8,128)(2,1)}, u32[]{:S(2)}) copy-start(bf16[256,640]{1,0:T(8,128)(2,1)} %refs_16_.1) | copy-start | bytes 983044
  67.2 12.1 %copy-start.4 = (bf16[256,640]{1,0:T(8,128)(2,1)S(1)}, bf16[256,640]{1,0:T(8,128)(2,1)}, u32[]{:S(2)}) copy-start(bf16[256,640]{1,0:T(8,128)(2,1)} %refs_17_.1) | copy-start | bytes 983044
  67.2 27.9 %slice-start.1 = ((s8[6553600]{0:T(1024)(128)(4,1)}), s8[2359296]{0:T(1024)(128)(4,1)S(1)}, s32[]{:S(2)}) async-start(s8[6553600]{0:T(1024)(128)(4,1)} %bitcast.34), calls=%async_computation.3 | async-start | bytes 4718592
  67.2 25.4 %collective-permute-start.19 = (bf16[272,640]{1,0:T(8,128)(2,1)S(1)}, bf16[272,640]{1,0:T(8,128)(2,1)S(1)}, u32[]{:S(2)}, u32[]{:S(2)}) collective-permute-start(bf16[272,640]{1,0:T(8,128)(2,1)S(1)} %attend.4), channel_id=1, source_target_pairs={{0,16},{8,24},{16,32},{24,40},{32,48},{40,56},{48,0},{56,8},{64,80... | collective-permute-start | bytes 1044488 | tf_op jit(solution)/shard_map/ppermute | solution.py:330
  79.1 16.0 %collective-permute-start.16 = (bf16[272,640]{1,0:T(8,128)(2,1)S(1)}, bf16[272,640]{1,0:T(8,128)(2,1)S(1)}, u32[]{:S(2)}, u32[]{:S(2)}) collective-permute-start(bf16[272,640]{1,0:T(8,128)(2,1)S(1)} %attend.3), channel_id=1, source_target_pairs={{0,48},{8,56},{16,0},{24,8},{32,16},{40,24},{48,32},{56,40},{64,11... | collective-permute-start | bytes 1044488 | tf_op jit(solution)/shard_map/ppermute | solution.py:330
  100.2 4.6 %copy-start.5 = (f32[640]{0:T(1024)S(1)}, f32[640]{0:T(1024)}, u32[]{:S(2)}) copy-start(f32[640]{0:T(1024)} %param.21) | copy-start | bytes 7684
  100.2 37.2 %all-to-all-start = ((bf16[8,256,640]{2,1,0:T(8,128)(2,1)}), bf16[8,256,640]{2,1,0:T(8,128)(2,1)S(1)}, u32[]{:S(2)}, u32[]{:S(2)}) async-start(bf16[8,256,640]{2,1,0:T(8,128)(2,1)} %project.1), calls=%async_computation | async-start | bytes 5242880 | tf_op jit(solution)/shard_map/all_to_all | solution.py:365
  104.8 38.3 %copy-start.6 = (f32[640]{0:T(1024)S(1)}, f32[640]{0:T(1024)}, u32[]{:S(2)}) copy-start(f32[640]{0:T(1024)} %param.22) | copy-start | bytes 7684
  104.8 38.3 %copy-start.7 = (f32[640]{0:T(1024)S(1)}, f32[640]{0:T(1024)}, u32[]{:S(2)}) copy-start(f32[640]{0:T(1024)} %param.23) | copy-start | bytes 7684
  139.7 9.6 %all-to-all-start.1 = ((f32[8,8,256]{2,1,0:T(8,128)}), f32[8,8,256]{2,1,0:T(8,128)S(1)}, u32[]{:S(2)}, u32[]{:S(2)}) async-start(f32[8,8,256]{2,1,0:T(8,128)} %get-tuple-element.9), calls=%async_computation.1 | async-start | bytes 131072 | tf_op jit(solution)/shard_map/all_to_all | solution.py:367
